TPU v7x, 32 devices: a whole 2x2x4 slice. The times are simulated.
32 devices in a mesh: dp: 16 (over z, x, core), tp: 2 (over y).
Axes of the slice: x: 2, y: 2, z: 4, core: 2. Of those that a mesh axis runs over, the one named last changes fastest.
Arguments:
- hidden_in: bfloat16 [28672, 1024], P('dp', 'tp'), may hold values from -6 to 6
- encoder_states: bfloat16 [64, 1500, 1024], P('dp'), may hold values from -6 to 6
- positions: int32 [64, 448], P('dp'), may hold values from 0 to 447, each once within a row
- self_qkv: bfloat16 [1024, 3, 1024], P('dp', None, 'tp'), may hold values from -0.1875 to 0.1875
- self_out: bfloat16 [1024, 1024], P('tp', 'dp'), may hold values from -1 to 1
- cross_query: bfloat16 [1024, 1024], P('dp', 'tp'), may hold values from -0.1875 to 0.1875
- cross_kv: bfloat16 [1024, 2, 1024], P('dp', None, 'tp'), may hold values from -0.1875 to 0.1875
- cross_out: bfloat16 [1024, 1024], P('tp', 'dp'), may hold values from -1.5 to 1.5
- up_weight: bfloat16 [1024, 4096], P('dp', 'tp'), may hold values from -0.1875 to 0.1875
- down_weight: bfloat16 [4096, 1024], P('tp', 'dp'), may hold values from -0.09375 to 0.09375
- norm_gains: float32 [3, 1024], P(None, 'tp'), may hold values from 0.5 to 1.5
- bias_rows: float32 [10, 1024], P(None, 'tp'), may hold values from -1.25 to 1.25
- up_bias: float32 [4096], P('tp'), may hold values from -1.25 to 1.25
- out_grad: bfloat16 [28672, 1024], P('dp', 'tp'), may hold values from -6 to 6
Outputs:
- output: bfloat16 [28672, 1024], P('dp', 'tp')
- hidden_grad: float32 [28672, 1024], P('dp', 'tp')
- encoder_grad: float32 [64, 1500, 1024], P('dp', None, 'tp')
- grad_self_qkv: float32 [1024, 3, 1024], P('dp', None, 'tp')
- grad_self_out: float32 [1024, 1024], P('tp', 'dp')
- grad_cross_query: float32 [1024, 1024], P('dp', 'tp')
- grad_cross_kv: float32 [1024, 2, 1024], P('dp', None, 'tp')
- grad_cross_out: float32 [1024, 1024], P('tp', 'dp')
- grad_up_weight: float32 [1024, 4096], P('dp', 'tp')
- grad_down_weight: float32 [4096, 1024], P('tp', 'dp')
- grad_norm_gains: float32 [3, 1024], P(None, 'tp')
- grad_bias_rows: float32 [10, 1024], P(None, 'tp')
- grad_up_bias: float32 [4096], P('tp')
Inputs may be any that keep to these rules, and one draw needn't show every extreme that they name: `positions`: each row lists every position 0 to 447 once.
All inputs are finite; a program needn't handle non-finite values.
Results may differ from a plain program's by a relative error of at most 0.02.
Values may be sent and summed in bfloat16 or wider, within the bound.
No kernel may reach another device: no remote copies, remote signals or barrier semaphores. Data moves between devices by JAX's collectives and lax.ppermute only.
A program may use at most 512 MiB of HBM per device.

v0:
```python
import math

import jax
import jax.numpy as jnp
from jax import lax
from jax.sharding import PartitionSpec as P

D = 1024
LEN = 448
SEQ_MB = 1
MICRO = 4
HEAD_DIM = 64


EPSILON = 1e-05
NEGATIVE = -1e30


def to_heads(matrix, groups):
    return matrix.reshape(groups, -1, matrix.shape[-1] // HEAD_DIM, HEAD_DIM)


def norm_forward(values, gain, shift):
    row_sum, square_sum = lax.psum(
        (jnp.sum(values, axis=1), jnp.sum(values * values, axis=1)), "tp"
    )
    width = values.shape[1] * lax.axis_size("tp")
    row_mean = row_sum / width
    inverse = lax.rsqrt(square_sum / width - row_mean * row_mean + EPSILON)
    unit = (values - row_mean[:, None]) * inverse[:, None]
    normed = (unit * gain + shift).astype(jnp.bfloat16)
    return (lax.all_gather(normed, "tp", axis=1, tiled=True), unit, inverse)


def norm_backward(incoming, unit, inverse, gain):
    scaled = incoming * gain
    first_sum, second_sum = lax.psum(
        (jnp.sum(scaled, axis=1), jnp.sum(scaled * unit, axis=1)), "tp"
    )
    width = incoming.shape[1] * lax.axis_size("tp")
    outgoing = inverse[:, None] * (
        scaled - first_sum[:, None] / width - unit * (second_sum[:, None] / width)
    )
    return (outgoing, jnp.sum(incoming * unit, axis=0), jnp.sum(incoming, axis=0))


def branch_total(partial_value):
    return lax.psum_scatter(partial_value, "tp", scatter_dimension=1, tiled=True)


def spread_grad(incoming):
    return lax.all_gather(incoming.astype(jnp.bfloat16), "tp", axis=1, tiled=True)


def spread_heads(columns):
    return lax.all_gather(columns, "tp", axis=1, tiled=True)


def input_total(partial_value):
    return lax.psum_scatter(partial_value, "tp", scatter_dimension=1, tiled=True)


def scores_of(query, key_rows, visible):
    scores = jnp.einsum(
        "sqhe,skhe->shqk", query, key_rows, preferred_element_type=jnp.float32
    ) * HEAD_DIM ** (-0.5)
    if visible is None:
        return scores
    return jnp.where(visible[:, None], scores, NEGATIVE)


def attend_forward(query, key_rows, value_rows, visible):
    scores = scores_of(query, key_rows, visible)
    row_max = jnp.max(scores, axis=-1, keepdims=True)
    weights = jnp.exp(scores - row_max)
    row_total = jnp.sum(weights, axis=-1, keepdims=True)
    probs = (weights / row_total).astype(jnp.bfloat16)
    mixed = jnp.einsum("shqk,skhe->sqhe", probs, value_rows, preferred_element_type=jnp.float32)
    return (mixed.astype(jnp.bfloat16), row_max + jnp.log(row_total))


def attend_backward(query, key_rows, value_rows, visible, log_total, grad_mixed):
    weights = jnp.exp(scores_of(query, key_rows, visible) - log_total)
    grad_weights = jnp.einsum(
        "sqhe,skhe->shqk", grad_mixed, value_rows, preferred_element_type=jnp.float32
    )
    inner = jnp.sum(weights * grad_weights, axis=-1, keepdims=True)
    grad_scores = (weights * (grad_weights - inner)).astype(jnp.bfloat16)
    factor = HEAD_DIM ** (-0.5)
    grad_query = (
        jnp.einsum("shqk,skhe->sqhe", grad_scores, key_rows, preferred_element_type=jnp.float32)
        * factor
    )
    grad_key = (
        jnp.einsum("shqk,sqhe->skhe", grad_scores, query, preferred_element_type=jnp.float32)
        * factor
    )
    grad_value = jnp.einsum(
        "shqk,sqhe->skhe",
        weights.astype(jnp.bfloat16),
        grad_mixed,
        preferred_element_type=jnp.float32,
    )
    return (
        grad_query.astype(jnp.bfloat16),
        grad_key.astype(jnp.bfloat16),
        grad_value.astype(jnp.bfloat16),
    )


def column_sum(matrix):
    return jnp.sum(matrix, axis=0, dtype=jnp.float32)


def per_device(
    hidden_in,
    encoder_states,
    positions,
    self_qkv,
    self_out,
    cross_query,
    cross_kv,
    cross_out,
    up_weight,
    down_weight,
    norm_gains,
    bias_rows,
    up_bias,
    out_grad,
):
    local_width = hidden_in.shape[1]
    local_units = up_weight.shape[1]
    group_rows = SEQ_MB * LEN
    zeros_f = jnp.float32
    grad_qkv = jnp.zeros((D, 3, local_width), zeros_f)
    grad_out = jnp.zeros((local_width, D), zeros_f)
    grad_cq = jnp.zeros((D, local_width), zeros_f)
    grad_ckv = jnp.zeros((D, 2, local_width), zeros_f)
    grad_co = jnp.zeros((local_width, D), zeros_f)
    grad_up = jnp.zeros((D, local_units), zeros_f)
    grad_down = jnp.zeros((local_units, D), zeros_f)
    gain_terms = jnp.zeros((3, local_width), zeros_f)
    bias_terms = jnp.zeros((10, local_width), zeros_f)
    upbias_terms = jnp.zeros((local_units,), zeros_f)
    outputs = []
    hidden_grads = []
    encoder_grads = []
    for batch_index in range(MICRO):
        weights_now = (
            lax.all_gather(self_qkv, "dp", axis=0, tiled=True),
            lax.all_gather(self_out, "dp", axis=1, tiled=True),
            lax.all_gather(cross_query, "dp", axis=0, tiled=True),
            lax.all_gather(cross_kv, "dp", axis=0, tiled=True),
            lax.all_gather(cross_out, "dp", axis=1, tiled=True),
            lax.all_gather(up_weight, "dp", axis=0, tiled=True),
            lax.all_gather(down_weight, "dp", axis=1, tiled=True),
        )
        qkv_full, out_full, cq_full, ckv_full, co_full, up_full, down_full = weights_now
        self_columns, cross_columns, query_transposed = (
            lax.all_to_all(out_full, "tp", split_axis=1, concat_axis=0, tiled=True),
            lax.all_to_all(co_full, "tp", split_axis=1, concat_axis=0, tiled=True),
            lax.all_to_all(cq_full.T, "tp", split_axis=1, concat_axis=0, tiled=True),
        )
        lower = batch_index * group_rows
        first_seq = batch_index * SEQ_MB
        resid = hidden_in[lower : lower + group_rows].astype(jnp.float32)
        frames = encoder_states[first_seq : first_seq + SEQ_MB]
        order = positions[first_seq : first_seq + SEQ_MB]
        visible = order[:, None, :] <= order[:, :, None]
        normed_a, unit_a, inverse_a = norm_forward(resid, norm_gains[0], bias_rows[0])
        triple = jnp.einsum("td,dcf->tcf", normed_a, qkv_full, preferred_element_type=jnp.float32)
        query = to_heads((triple[:, 0] + bias_rows[3]).astype(jnp.bfloat16), SEQ_MB)
        keys = to_heads(triple[:, 1].astype(jnp.bfloat16), SEQ_MB)
        values = to_heads((triple[:, 2] + bias_rows[4]).astype(jnp.bfloat16), SEQ_MB)
        mixed, log_self = attend_forward(query, keys, values, visible)
        mixed_rows = mixed.reshape(group_rows, local_width)
        self_share = jnp.dot(
            spread_heads(mixed_rows), self_columns, preferred_element_type=jnp.float32
        )
        first = resid + self_share + bias_rows[5]
        normed_c, unit_c, inverse_c = norm_forward(first, norm_gains[1], bias_rows[1])
        cross_q = to_heads(
            (jnp.dot(normed_c, cq_full, preferred_element_type=jnp.float32) + bias_rows[6]).astype(
                jnp.bfloat16
            ),
            SEQ_MB,
        )
        paired = jnp.einsum("sfd,dcg->sfcg", frames, ckv_full, preferred_element_type=jnp.float32)
        cross_k = to_heads(paired[:, :, 0].astype(jnp.bfloat16), SEQ_MB)
        cross_v = to_heads((paired[:, :, 1] + bias_rows[7]).astype(jnp.bfloat16), SEQ_MB)
        cross_mixed, log_cross = attend_forward(cross_q, cross_k, cross_v, None)
        cross_rows = cross_mixed.reshape(group_rows, local_width)
        cross_share = jnp.dot(
            spread_heads(cross_rows), cross_columns, preferred_element_type=jnp.float32
        )
        second = first + cross_share + bias_rows[8]
        normed_m, unit_m, inverse_m = norm_forward(second, norm_gains[2], bias_rows[2])
        before = jnp.dot(normed_m, up_full, preferred_element_type=jnp.float32) + up_bias
        activated = jax.nn.gelu(before, approximate=False).astype(jnp.bfloat16)
        final = (
            second
            + branch_total(jnp.dot(activated, down_full, preferred_element_type=jnp.float32))
            + bias_rows[9]
        )
        outputs.append(final.astype(jnp.bfloat16))
        weights_back = (
            lax.all_gather(self_qkv, "dp", axis=0, tiled=True),
            lax.all_gather(self_out, "dp", axis=1, tiled=True),
            lax.all_gather(cross_query, "dp", axis=0, tiled=True),
            lax.all_gather(cross_kv, "dp", axis=0, tiled=True),
            lax.all_gather(cross_out, "dp", axis=1, tiled=True),
            lax.all_gather(up_weight, "dp", axis=0, tiled=True),
            lax.all_gather(down_weight, "dp", axis=1, tiled=True),
        )
        qkv_back, out_back, cq_back, ckv_back, co_back, up_back, down_back = weights_back
        grad_final = out_grad[lower : lower + group_rows]
        grad_final_full = spread_grad(grad_final)
        grad_down = grad_down + jnp.einsum(
            "tf,td->fd", activated, grad_final_full, preferred_element_type=jnp.float32
        )
        grad_act = jnp.einsum(
            "td,fd->tf", grad_final_full, down_back, preferred_element_type=jnp.float32
        )
        normal_cdf = 0.5 * (1.0 + lax.erf(before / math.sqrt(2.0)))
        density = jnp.exp(-0.5 * before * before) / math.sqrt(2.0 * math.pi)
        grad_before = (grad_act * (normal_cdf + before * density)).astype(jnp.bfloat16)
        grad_up = grad_up + jnp.einsum(
            "td,tf->df", normed_m, grad_before, preferred_element_type=jnp.float32
        )
        grad_norm_m = input_total(
            jnp.einsum("tf,df->td", grad_before, up_back, preferred_element_type=jnp.float32)
        )
        back_m, gain_m, shift_m = norm_backward(grad_norm_m, unit_m, inverse_m, norm_gains[2])
        grad_second = grad_final.astype(jnp.float32) + back_m
        grad_cross_full = spread_grad(grad_second)
        grad_co = grad_co + jnp.einsum(
            "tg,td->gd", cross_rows, grad_cross_full, preferred_element_type=jnp.float32
        )
        grad_cross_mixed = to_heads(
            jnp.einsum(
                "td,gd->tg", grad_cross_full, co_back, preferred_element_type=jnp.float32
            ).astype(jnp.bfloat16),
            SEQ_MB,
        )
        grad_cq_heads, grad_ck_heads, grad_cv_heads = attend_backward(
            cross_q, cross_k, cross_v, None, log_cross, grad_cross_mixed
        )
        grad_cq_rows = grad_cq_heads.reshape(group_rows, local_width)
        grad_kv = jnp.stack(
            [
                grad_ck_heads.reshape(SEQ_MB, -1, local_width),
                grad_cv_heads.reshape(SEQ_MB, -1, local_width),
            ],
            axis=2,
        )
        grad_cq = grad_cq + jnp.einsum(
            "td,tg->dg", normed_c, grad_cq_rows, preferred_element_type=jnp.float32
        )
        grad_ckv = grad_ckv + jnp.einsum(
            "sfd,sfcg->dcg", frames, grad_kv, preferred_element_type=jnp.float32
        )
        frame_partial = jnp.einsum(
            "sfcg,dcg->sfd", grad_kv, ckv_back, preferred_element_type=jnp.float32
        )
        encoder_grads.append(
            lax.psum_scatter(
                frame_partial.astype(jnp.bfloat16), "tp", scatter_dimension=2, tiled=True
            ).astype(jnp.float32)
        )
        grad_norm_c = jnp.dot(
            spread_heads(grad_cq_rows), query_transposed, preferred_element_type=jnp.float32
        )
        back_c, gain_c, shift_c = norm_backward(grad_norm_c, unit_c, inverse_c, norm_gains[1])
        grad_first = grad_second + back_c
        grad_self_full = spread_grad(grad_first)
        grad_out = grad_out + jnp.einsum(
            "tg,td->gd", mixed_rows, grad_self_full, preferred_element_type=jnp.float32
        )
        grad_mixed = to_heads(
            jnp.einsum(
                "td,gd->tg", grad_self_full, out_back, preferred_element_type=jnp.float32
            ).astype(jnp.bfloat16),
            SEQ_MB,
        )
        grad_q_heads, grad_k_heads, grad_v_heads = attend_backward(
            query, keys, values, visible, log_self, grad_mixed
        )
        grad_triple = jnp.stack(
            [
                grad_q_heads.reshape(group_rows, local_width),
                grad_k_heads.reshape(group_rows, local_width),
                grad_v_heads.reshape(group_rows, local_width),
            ],
            axis=1,
        )
        grad_qkv = grad_qkv + jnp.einsum(
            "td,tcg->dcg", normed_a, grad_triple, preferred_element_type=jnp.float32
        )
        grad_norm_a = input_total(
            jnp.einsum("tcg,dcg->td", grad_triple, qkv_back, preferred_element_type=jnp.float32)
        )
        back_a, gain_a, shift_a = norm_backward(grad_norm_a, unit_a, inverse_a, norm_gains[0])
        hidden_grads.append(grad_first + back_a)
        gain_terms = gain_terms + jnp.stack([gain_a, gain_c, gain_m])
        bias_terms = bias_terms + jnp.stack(
            [
                shift_a,
                shift_c,
                shift_m,
                column_sum(grad_triple[:, 0]),
                column_sum(grad_triple[:, 2]),
                column_sum(grad_first.astype(jnp.bfloat16)),
                column_sum(grad_cq_rows),
                column_sum(grad_kv[:, :, 1].reshape(-1, local_width)),
                column_sum(grad_second.astype(jnp.bfloat16)),
                column_sum(grad_final),
            ]
        )
        upbias_terms = upbias_terms + column_sum(grad_before)
    weight_totals = (
        lax.psum_scatter(
            grad_qkv.astype(jnp.bfloat16), "dp", scatter_dimension=0, tiled=True
        ).astype(jnp.float32),
        lax.psum_scatter(
            grad_out.astype(jnp.bfloat16), "dp", scatter_dimension=1, tiled=True
        ).astype(jnp.float32),
        lax.psum_scatter(
            grad_cq.astype(jnp.bfloat16), "dp", scatter_dimension=0, tiled=True
        ).astype(jnp.float32),
        lax.psum_scatter(
            grad_ckv.astype(jnp.bfloat16), "dp", scatter_dimension=0, tiled=True
        ).astype(jnp.float32),
        lax.psum_scatter(
            grad_co.astype(jnp.bfloat16), "dp", scatter_dimension=1, tiled=True
        ).astype(jnp.float32),
        lax.psum_scatter(
            grad_up.astype(jnp.bfloat16), "dp", scatter_dimension=0, tiled=True
        ).astype(jnp.float32),
        lax.psum_scatter(
            grad_down.astype(jnp.bfloat16), "dp", scatter_dimension=1, tiled=True
        ).astype(jnp.float32),
    )
    vector_totals = lax.psum((gain_terms, bias_terms, upbias_terms), "dp")
    return (
        jnp.concatenate(outputs, axis=0),
        jnp.concatenate(hidden_grads, axis=0),
        jnp.concatenate(encoder_grads, axis=0),
        weight_totals[0],
        weight_totals[1],
        weight_totals[2],
        weight_totals[3],
        weight_totals[4],
        weight_totals[5],
        weight_totals[6],
        vector_totals[0],
        vector_totals[1],
        vector_totals[2],
    )


def solution(mesh):
    in_specs = (
        P("dp", "tp"),
        P("dp", None, None),
        P("dp", None),
        P("dp", None, "tp"),
        P("tp", "dp"),
        P("dp", "tp"),
        P("dp", None, "tp"),
        P("tp", "dp"),
        P("dp", "tp"),
        P("tp", "dp"),
        P(None, "tp"),
        P(None, "tp"),
        P("tp"),
        P("dp", "tp"),
    )
    out_specs = (
        P("dp", "tp"),
        P("dp", "tp"),
        P("dp", None, "tp"),
        P("dp", None, "tp"),
        P("tp", "dp"),
        P("dp", "tp"),
        P("dp", None, "tp"),
        P("tp", "dp"),
        P("dp", "tp"),
        P("tp", "dp"),
        P(None, "tp"),
        P(None, "tp"),
        P("tp"),
    )
    return jax.shard_map(
        per_device, mesh=mesh, in_specs=in_specs, out_specs=out_specs, check_vma=False
    )
```

profile of v0, /device:TPU:0, one launch (start us, length us, event | category | flops | bytes accessed | tf_op | source)
XLA Modules:
  0.0 2208.9 jit_solution(7442638584875605141)
XLA Ops:
  16.0 38.2 %fusion.282 = (bf16[1,1500,1024]{2,0,1:T(2,128)(2,1)}, bf16[1,1500,1024]{2,0,1:T(2,128)(2,1)}, bf16[1,1500,1024]{2,0,1:T(2,128)(2,1)}, bf16[1,1500,1024]{2,0,1:T(2,128)(2,1)}) fusion(bf16[4,1500,1024]{2,0,1:T(4,128)(2,1)} %param.15), kind=kLoop, calls=%fused_computation.611 | loop fusion | bytes 24576000 | tf_op jit(solution)/shard_map/slice | solution.py:167
  64.0 22.7 %all_gather.186 = bf16[448,1024]{1,0:T(8,128)(2,1)} all-gather(bf16[448,512]{1,0:T(8,128)(2,1)S(1)} %fusion.200), channel_id=1, replica_groups=mesh['dp'=16,'tp'=2] {'tp'}, dimensions={1}, use_global_device_ids=true | all-gather | bytes 1376256 | tf_op jit(solution)/shard_map/all_gather | solution.py:32
  95.2 23.3 %all_gather.205 = bf16[448,1024]{1,0:T(8,128)(2,1)} all-gather(bf16[448,512]{1,0:T(8,128)(2,1)S(1)} %get-tuple-element.252), channel_id=1, replica_groups=mesh['dp'=16,'tp'=2] {'tp'}, dimensions={1}, use_global_device_ids=true | all-gather | bytes 1376256 | tf_op jit(solution)/shard_map/all_gather | solution.py:52
  123.1 9.8 all-gather.12.cloned.1.call-done
  148.3 30.7 %all-gather.8.cloned.1.call-done = bf16[1024,3,512]{2,0,1:T(8,128)(2,1)} async-done(((bf16[64,3,512]{2,0,1:T(8,128)(2,1)}), bf16[1024,3,512]{2,0,1:T(8,128)(2,1)}) %all-gather.8.cloned.1.call-update) | async-done | bytes 3145744 | tf_op jit(solution)/shard_map/all_gather | solution.py:150
  199.4 14.7 all_gather.187
  222.2 11.6 all_gather.188
  248.9 9.6 fusion.175
  258.5 12.0 all_gather.189
  286.0 13.0 fusion.37
  299.0 21.7 all-gather.20.cloned.1.call-done
  337.9 30.4 %all_to_all.42 = bf16[512,2,512]{0,2,1:T(8,128)(2,1)} all-to-all(bf16[512,2,512]{0,2,1:T(8,128)(2,1)} %bitcast.692), channel_id=1, replica_groups=mesh['dp'=16,'tp'=2] {'tp'}, dimensions={1} | all-to-all | bytes 2097152 | tf_op jit(solution)/shard_map/all_to_all | solution.py:162
  370.7 31.2 %reduce-scatter.25.cloned.1.call-done = f32[448,512]{1,0:T(8,128)} async-done(((f32[448,1024]{1,0:T(8,128)}), f32[448,512]{1,0:T(8,128)}) %reduce-scatter.25.cloned.1.call-update) | async-done | bytes 917520 | tf_op jit(solution)/shard_map/reduce_scatter | solution.py:48
  413.3 12.0 all_gather.206
  428.9 15.1 multiply_reduce_fusion.2
  444.0 14.7 multiply_convert_fusion.2
  463.8 12.2 all_gather.207
  485.6 9.7 all_gather.208
  525.5 11.3 all_gather.213
  592.6 13.9 all_gather.196
  610.4 13.1 all_gather.191
  668.7 14.2 all_gather.176
  690.6 14.9 all_gather.192
  713.3 13.9 all_gather.197
  751.8 9.7 all_gather.193
  805.2 10.1 all_gather.199
  837.3 10.5 all_gather.194
  869.8 10.5 all_gather.181
  891.4 12.4 all_gather.200
  915.8 14.7 all_gather.209
  930.5 19.1 all_gather.201
  979.7 28.5 %fusion.34 = (bf16[448,2048]{1,0:T(8,128)(2,1)}, bf16[448,2048]{1,0:T(8,128)(2,1)}, bf16[448,2048]{1,0:T(8,128)(2,1)S(1)}, f32[448,2048]{1,0:T(8,128)S(1)}) fusion(f32[2048]{0:T(1024)S(1)} %copy-done.372, f32[448,2048]{1,0:T(8,128)} %copy-done.383, f32[448,2048]{1,0:T(8,128)} %copy-done.382, bf16[448,1024]{1,0:T(8,128)(2,1)S(1)} %all_gather.183, ...), kind=kOutput, calls=%fused_computation.99 | convolution fusion | flops 2060713984 | bytes 21635072 | tf_op jit(solution)/shard_map/dot_general | solution.py:198
  1029.9 11.2 convert_reduce_fusion.6
  1080.5 24.7 %reduce-scatter.27.cloned.1.call-done = f32[448,512]{1,0:T(8,128)} async-done(((f32[448,1024]{1,0:T(8,128)}), f32[448,512]{1,0:T(8,128)}) %reduce-scatter.27.cloned.1.call-update) | async-done | bytes 917520 | tf_op jit(solution)/shard_map/reduce_scatter | solution.py:48
  1122.3 22.7 %all_gather.214 = bf16[448,1024]{1,0:T(8,128)(2,1)S(1)} all-gather(bf16[448,512]{1,0:T(8,128)(2,1)S(1)} %get-tuple-element.246), channel_id=1, replica_groups=mesh['dp'=16,'tp'=2] {'tp'}, dimensions={1}, use_global_device_ids=true | all-gather | bytes 1376256 | tf_op jit(solution)/shard_map/all_gather | solution.py:52
  1149.6 11.0 all_gather.210
  1166.2 14.9 multiply_reduce_fusion
  1181.1 14.7 multiply_convert_fusion
  1201.1 14.7 multiply_reduce_fusion.1
  1215.8 14.9 multiply_convert_fusion.1
  1253.2 11.0 convert_reduce_fusion.5
  1264.2 11.1 convert_reduce_fusion.4
  1278.8 11.5 all_gather.202
  1293.0 13.0 convert_reduce_fusion.7
  1305.9 14.8 multiply_reduce_fusion.3
  1320.7 14.8 multiply_convert_fusion.3
  1351.6 12.2 all_gather.215
  1368.3 12.9 all_gather.211
  1407.1 10.2 all_gather.203
  1449.6 14.0 all_gather.212
  1463.6 13.4 all_gather.216
  1493.9 11.0 add_convert_fusion
  1521.6 11.4 add_convert_fusion.1
  1691.8 68.5 %reduce-scatter.65.cloned.1.call-done = bf16[2048,64]{0,1:T(8,128)(2,1)} async-done(((bf16[2048,1024]{0,1:T(8,128)(2,1)}), bf16[2048,64]{0,1:T(8,128)(2,1)}) %reduce-scatter.65.cloned.1.call-update) | async-done | bytes 262160 | tf_op jit(solution)/shard_map/reduce_scatter | solution.py:339
  1762.0 73.4 %reduce-scatter.63.cloned.1.call-done = bf16[64,2048]{1,0:T(8,128)(2,1)} async-done(((bf16[1024,2048]{1,0:T(8,128)(2,1)}), bf16[64,2048]{1,0:T(8,128)(2,1)}) %reduce-scatter.63.cloned.1.call-update) | async-done | bytes 262160 | tf_op jit(solution)/shard_map/reduce_scatter | solution.py:336
  1837.2 28.7 %reduce-scatter.33.cloned.1.call-done = f32[448,512]{1,0:T(8,128)} async-done(((f32[448,1024]{1,0:T(8,128)}), f32[448,512]{1,0:T(8,128)}) %reduce-scatter.33.cloned.1.call-update) | async-done | bytes 917520 | tf_op jit(solution)/shard_map/reduce_scatter | solution.py:60
  1865.9 31.1 %reduce-scatter.45.cloned.1.call-done = f32[448,512]{1,0:T(8,128)} async-done(((f32[448,1024]{1,0:T(8,128)}), f32[448,512]{1,0:T(8,128)}) %reduce-scatter.45.cloned.1.call-update) | async-done | bytes 917520 | tf_op jit(solution)/shard_map/reduce_scatter | solution.py:60
  1896.9 31.9 %reduce-scatter.41.cloned.1.call-done = f32[448,512]{1,0:T(8,128)} async-done(((f32[448,1024]{1,0:T(8,128)}), f32[448,512]{1,0:T(8,128)}) %reduce-scatter.41.cloned.1.call-update) | async-done | bytes 917520 | tf_op jit(solution)/shard_map/reduce_scatter | solution.py:60
  1939.5 61.3 %all-reduce.1 = (f32[3,512]{1,0:T(4,128)}, f32[10,512]{1,0:T(8,128)}, f32[2048]{0:T(1024)}) all-reduce(f32[3,512]{1,0:T(4,128)S(1)} %fusion.257, f32[10,512]{1,0:T(8,128)S(1)} %add_add_fusion, f32[2048]{0:T(1024)S(1)} %add_add_fusion.1), channel_id=1, replica_groups=mesh['dp'=16,'tp'=2] {'dp'}, use_global_device_ids=true, to_apply=%region_155.156 | all-reduce | flops 8704 | bytes 69632 | tf_op jit(solution)/shard_map/psum | solution.py:343
  2008.4 34.7 %reduce-scatter.49.cloned.1.call-done = bf16[1,1500,512]{2,1,0:T(8,128)(2,1)} async-done(((bf16[1,1500,1024]{2,1,0:T(8,128)(2,1)}), bf16[1,1500,512]{2,1,0:T(8,128)(2,1)}) %reduce-scatter.49.cloned.1.call-update) | async-done | bytes 1536016 | tf_op jit(solution)/shard_map/reduce_scatter | solution.py:266
  2043.1 45.0 %reduce-scatter.53.cloned.1.call-done = bf16[1,1500,512]{2,1,0:T(8,128)(2,1)} async-done(((bf16[1,1500,1024]{2,1,0:T(8,128)(2,1)}), bf16[1,1500,512]{2,1,0:T(8,128)(2,1)}) %reduce-scatter.53.cloned.1.call-update) | async-done | bytes 1536016 | tf_op jit(solution)/shard_map/reduce_scatter | solution.py:266
  2088.1 44.9 %reduce-scatter.51.cloned.1.call-done = bf16[1,1500,512]{2,1,0:T(8,128)(2,1)} async-done(((bf16[1,1500,1024]{2,1,0:T(8,128)(2,1)}), bf16[1,1500,512]{2,1,0:T(8,128)(2,1)}) %reduce-scatter.51.cloned.1.call-update) | async-done | bytes 1536016 | tf_op jit(solution)/shard_map/reduce_scatter | solution.py:266
  2133.1 44.9 %reduce-scatter.47.cloned.1.call-done = bf16[1,1500,512]{2,1,0:T(8,128)(2,1)} async-done(((bf16[1,1500,1024]{2,1,0:T(8,128)(2,1)}), bf16[1,1500,512]{2,1,0:T(8,128)(2,1)}) %reduce-scatter.47.cloned.1.call-update) | async-done | bytes 1536016 | tf_op jit(solution)/shard_map/reduce_scatter | solution.py:266
  2182.5 19.3 copy.352
  (1215 shorter events, 885.5 us)
Async XLA Ops:
  7.2 53.0 %all-gather.16.cloned.1.call-start = ((), (), s32[]{:S(2)}) async-start(), calls=%async_computation.29 | async-start | bytes 1114112 | tf_op jit(solution)/shard_map/all_gather | solution.py:154
  7.9 82.0 %all-gather.10.cloned.1.call-start = ((), (), s32[]{:S(2)}) async-start(), calls=%async_computation.26 | async-start | bytes 1114112 | tf_op jit(solution)/shard_map/all_gather | solution.py:151
  8.7 124.2 %all-gather.12.cloned.1.call-start = ((), (), s32[]{:S(2)}) async-start(), calls=%async_computation.27 | async-start | bytes 2228224 | tf_op jit(solution)/shard_map/all_gather | solution.py:153
  10.3 168.6 %all-gather.8.cloned.1.call-start = ((), (), s32[]{:S(2)}) async-start(), calls=%async_computation.25 | async-start | bytes 3342336 | tf_op jit(solution)/shard_map/all_gather | solution.py:150
  10.9 222.8 %all-gather.14.cloned.1.call-start = ((), (), s32[]{:S(2)}) async-start(), calls=%async_computation.28 | async-start | bytes 1114112 | tf_op jit(solution)/shard_map/all_gather | solution.py:152
  11.5 274.6 %all-gather.18.cloned.1.call-start = ((), (), s32[]{:S(2)}) async-start(), calls=%async_computation.30 | async-start | bytes 4456448 | tf_op jit(solution)/shard_map/all_gather | solution.py:155
  12.1 308.6 %all-gather.20.cloned.1.call-start = ((), (), s32[]{:S(2)}) async-start(), calls=%async_computation.31 | async-start | bytes 4456448 | tf_op jit(solution)/shard_map/all_gather | solution.py:156
  14.9 395.1 %copy-start.229 = (f32[1,512]{1,0:T(1,128)}, f32[1,512]{1,0:T(1,128)S(1)}, u32[]{:S(2)}) copy-start(f32[1,512]{1,0:T(1,128)S(1)} %get-tuple-element.276) | copy-start | bytes 6148
  14.9 720.9 %copy-start.240 = (f32[1,512]{1,0:T(1,128)}, f32[1,512]{1,0:T(1,128)S(1)}, u32[]{:S(2)}) copy-start(f32[1,512]{1,0:T(1,128)S(1)} %get-tuple-element.278) | copy-start | bytes 6148
  16.0 254.5 %copy-start.350 = (f32[1,512]{1,0:T(1,128)}, f32[1,512]{1,0:T(1,128)S(1)}, u32[]{:S(2)}) copy-start(f32[1,512]{1,0:T(1,128)S(1)} %get-tuple-element.265) | copy-start | bytes 6148
  16.0 260.3 %copy-start.286 = (f32[1,512]{1,0:T(1,128)}, f32[1,512]{1,0:T(1,128)S(1)}, u32[]{:S(2)}) copy-start(f32[1,512]{1,0:T(1,128)S(1)} %get-tuple-element.268) | copy-start | bytes 6148
  16.0 385.9 %copy-start.254 = (f32[1,512]{1,0:T(1,128)}, f32[1,512]{1,0:T(1,128)S(1)}, u32[]{:S(2)}) copy-start(f32[1,512]{1,0:T(1,128)S(1)} %get-tuple-element.259) | copy-start | bytes 6148
  60.2 29.7 %all-to-all-start.1 = ((bf16[512,2,512]{0,2,1:T(8,128)(2,1)}), bf16[512,2,512]{0,2,1:T(8,128)(2,1)S(1)}, u32[]{:S(2)}, u32[]{:S(2)}) async-start(bf16[512,2,512]{0,2,1:T(8,128)(2,1)} %bitcast.687), calls=%async_computation.1 | async-start | bytes 2097152 | tf_op jit(solution)/shard_map/all_to_all | solution.py:161
  89.9 30.9 %all-to-all-start = ((bf16[512,2,512]{0,2,1:T(8,128)(2,1)}), bf16[512,2,512]{0,2,1:T(8,128)(2,1)}, u32[]{:S(2)}, u32[]{:S(2)}) async-start(bf16[512,2,512]{0,2,1:T(8,128)(2,1)} %bitcast.686), calls=%async_computation | async-start | bytes 2097152 | tf_op jit(solution)/shard_map/all_to_all | solution.py:160
  94.3 276.3 %reduce-scatter.35.cloned.1.call-start = ((), (), s32[]{:S(2)}) async-start(), calls=%async_computation.38 | async-start | bytes 2752512 | tf_op jit(solution)/shard_map/reduce_scatter | solution.py:60
  95.1 614.9 %copy-start.232 = (f32[8,64]{1,0:T(8,128)}, f32[8,64]{1,0:T(8,128)S(1)}, u32[]{:S(2)}) copy-start(f32[8,64]{1,0:T(8,128)S(1)} %add.791) | copy-start | bytes 6148
  95.2 333.7 %copy-start.234 = (f32[8,64]{1,0:T(8,128)}, f32[8,64]{1,0:T(8,128)S(1)}, u32[]{:S(2)}) copy-start(f32[8,64]{1,0:T(8,128)S(1)} %add.801) | copy-start | bytes 6148
  331.7 70.2 %reduce-scatter.25.cloned.1.call-start = ((), (), s32[]{:S(2)}) async-start(), calls=%async_computation.33 | async-start | bytes 2752512 | tf_op jit(solution)/shard_map/reduce_scatter | solution.py:48
  337.9 243.1 %reduce-scatter.37.cloned.1.call-start = ((), (), s32[]{:S(2)}) async-start(), calls=%async_computation.39 | async-start | bytes 2752512 | tf_op jit(solution)/shard_map/reduce_scatter | solution.py:60
  525.4 555.0 %reduce-scatter.43.cloned.1.call-start = ((), (), s32[]{:S(2)}) async-start(), calls=%async_computation.42 | async-start | bytes 2752512 | tf_op jit(solution)/shard_map/reduce_scatter | solution.py:60
  915.8 164.7 %reduce-scatter.39.cloned.1.call-start = ((), (), s32[]{:S(2)}) async-start(), calls=%async_computation.40 | async-start | bytes 2752512 | tf_op jit(solution)/shard_map/reduce_scatter | solution.py:60
  979.5 101.0 %reduce-scatter.31.cloned.1.call-start = ((), (), s32[]{:S(2)}) async-start(), calls=%async_computation.36 | async-start | bytes 2752512 | tf_op jit(solution)/shard_map/reduce_scatter | solution.py:60
  1016.9 63.7 %reduce-scatter.29.cloned.1.call-start = ((), (), s32[]{:S(2)}) async-start(), calls=%async_computation.35 | async-start | bytes 2752512 | tf_op jit(solution)/shard_map/reduce_scatter | solution.py:48
  1022.6 82.7 %reduce-scatter.27.cloned.1.call-start = ((), (), s32[]{:S(2)}) async-start(), calls=%async_computation.34 | async-start | bytes 2752512 | tf_op jit(solution)/shard_map/reduce_scatter | solution.py:48
  1044.5 230.9 %reduce-scatter.23.cloned.1.call-start = ((), (), s32[]{:S(2)}) async-start(), calls=%async_computation.32 | async-start | bytes 2752512 | tf_op jit(solution)/shard_map/reduce_scatter | solution.py:48
  1080.4 605.1 %all-reduce.15.cloned.1.call-start = ((), (), s32[]{:S(2)}) async-start(), calls=%async_computation.54 | async-start | bytes 4194304
  1407.0 280.2 %reduce-scatter.61.cloned.1.call-start = ((), (), s32[]{:S(2)}) async-start(), calls=%async_computation.51 | async-start | bytes 1114112 | tf_op jit(solution)/shard_map/reduce_scatter | solution.py:333
  1435.9 252.8 %reduce-scatter.59.cloned.1.call-start = ((), (), s32[]{:S(2)}) async-start(), calls=%async_computation.50 | async-start | bytes 1114112 | tf_op jit(solution)/shard_map/reduce_scatter | solution.py:327
  1442.3 247.9 %reduce-scatter.57.cloned.1.call-start = ((), (), s32[]{:S(2)}) async-start(), calls=%async_computation.49 | async-start | bytes 1114112 | tf_op jit(solution)/shard_map/reduce_scatter | solution.py:324
  1489.7 270.5 %reduce-scatter.65.cloned.1.call-start = ((), (), s32[]{:S(2)}) async-start(), calls=%async_computation.53 | async-start | bytes 4456448 | tf_op jit(solution)/shard_map/reduce_scatter | solution.py:339
  1504.9 330.5 %reduce-scatter.63.cloned.1.call-start = ((), (), s32[]{:S(2)}) async-start(), calls=%async_computation.52 | async-start | bytes 4456448 | tf_op jit(solution)/shard_map/reduce_scatter | solution.py:336
  1533.1 332.8 %reduce-scatter.33.cloned.1.call-start = ((), (), s32[]{:S(2)}) async-start(), calls=%async_computation.37 | async-start | bytes 2752512 | tf_op jit(solution)/shard_map/reduce_scatter | solution.py:60
  1568.2 328.7 %reduce-scatter.45.cloned.1.call-start = ((), (), s32[]{:S(2)}) async-start(), calls=%async_computation.43 | async-start | bytes 2752512 | tf_op jit(solution)/shard_map/reduce_scatter | solution.py:60
  1602.6 326.2 %reduce-scatter.41.cloned.1.call-start = ((), (), s32[]{:S(2)}) async-start(), calls=%async_computation.41 | async-start | bytes 2752512 | tf_op jit(solution)/shard_map/reduce_scatter | solution.py:60
  1639.5 367.1 %reduce-scatter.55.cloned.1.call-start = ((), (), s32[]{:S(2)}) async-start(), calls=%async_computation.48 | async-start | bytes 3342336 | tf_op jit(solution)/shard_map/reduce_scatter | solution.py:321
  1650.3 392.9 %reduce-scatter.49.cloned.1.call-start = ((), (), s32[]{:S(2)}) async-start(), calls=%async_computation.45 | async-start | bytes 4620288 | tf_op jit(solution)/shard_map/reduce_scatter | solution.py:266
  1657.5 430.7 %reduce-scatter.53.cloned.1.call-start = ((), (), s32[]{:S(2)}) async-start(), calls=%async_computation.47 | async-start | bytes 4620288 | tf_op jit(solution)/shard_map/reduce_scatter | solution.py:266
  1665.3 467.7 %reduce-scatter.51.cloned.1.call-start = ((), (), s32[]{:S(2)}) async-start(), calls=%async_computation.46 | async-start | bytes 4620288 | tf_op jit(solution)/shard_map/reduce_scatter | solution.py:266
  1673.4 504.6 %reduce-scatter.47.cloned.1.call-start = ((), (), s32[]{:S(2)}) async-start(), calls=%async_computation.44 | async-start | bytes 4620288 | tf_op jit(solution)/shard_map/reduce_scatter | solution.py:266
  1679.8 249.0 %copy-start.17 = (bf16[1792,512]{1,0:T(8,128)(2,1)S(1)}, bf16[1792,512]{1,0:T(8,128)(2,1)}, u32[]{:S(2)}) copy-start(bf16[1792,512]{1,0:T(8,128)(2,1)} %param.14) | copy-start | bytes 5505028
  1679.8 249.0 %copy-start.239 = (f32[1,512]{1,0:T(1,128)S(1)}, f32[1,512]{1,0:T(1,128)}, u32[]{:S(2)}) copy-start(f32[1,512]{1,0:T(1,128)} %copy-done.237) | copy-start | bytes 6148
  1679.8 249.0 %copy-start.275 = (f32[448]{0:T(512)S(1)}, f32[448]{0:T(512)}, u32[]{:S(2)}) copy-start(f32[448]{0:T(512)} %copy-done.274) | copy-start | bytes 5380
  1679.8 249.0 %copy-start.277 = (f32[448]{0:T(512)S(1)}, f32[448]{0:T(512)}, u32[]{:S(2)}) copy-start(f32[448]{0:T(512)} %copy-done.276) | copy-start | bytes 5380
  1679.9 249.0 %copy-start.279 = (f32[448]{0:T(512)S(1)}, f32[448]{0:T(512)}, u32[]{:S(2)}) copy-start(f32[448]{0:T(512)} %copy-done.278) | copy-start | bytes 5380
  1679.9 249.0 %copy-start.281 = (f32[448]{0:T(512)S(1)}, f32[448]{0:T(512)}, u32[]{:S(2)}) copy-start(f32[448]{0:T(512)} %copy-done.280) | copy-start | bytes 5380
  1679.9 249.0 %copy-start.283 = (f32[448]{0:T(512)S(1)}, f32[448]{0:T(512)}, u32[]{:S(2)}) copy-start(f32[448]{0:T(512)} %copy-done.282) | copy-start | bytes 5380
  1679.9 249.0 %copy-start.285 = (f32[448]{0:T(512)S(1)}, f32[448]{0:T(512)}, u32[]{:S(2)}) copy-start(f32[448]{0:T(512)} %copy-done.284) | copy-start | bytes 5380
  1685.3 246.9 %copy-start.328 = (f32[512]{0:T(512)S(1)}, f32[512]{0:T(512)}, u32[]{:S(2)}) copy-start(f32[512]{0:T(512)} %get-tuple-element.122) | copy-start | bytes 6148
  1685.3 246.9 %copy-start.331 = (f32[512]{0:T(512)S(1)}, f32[512]{0:T(512)}, u32[]{:S(2)}) copy-start(f32[512]{0:T(512)} %get-tuple-element.94) | copy-start | bytes 6148
  1685.3 246.9 %copy-start.336 = (f32[512]{0:T(512)S(1)}, f32[512]{0:T(512)}, u32[]{:S(2)}) copy-start(f32[512]{0:T(512)} %get-tuple-element.205) | copy-start | bytes 6148
  1685.3 246.9 %copy-start.338 = (f32[512]{0:T(512)S(1)}, f32[512]{0:T(512)}, u32[]{:S(2)}) copy-start(f32[512]{0:T(512)} %get-tuple-element.208) | copy-start | bytes 6148
  1685.4 247.0 %copy-start.322 = (f32[448]{0:T(512)S(1)}, f32[448]{0:T(512)}, u32[]{:S(2)}) copy-start(f32[448]{0:T(512)} %get-tuple-element.70) | copy-start | bytes 5380
  1685.4 247.0 %copy-start.323 = (f32[448]{0:T(512)S(1)}, f32[448]{0:T(512)}, u32[]{:S(2)}) copy-start(f32[448]{0:T(512)} %get-tuple-element.105) | copy-start | bytes 5380
  1685.4 253.9 %copy-start.317 = (f32[512]{0:T(512)S(1)}, f32[512]{0:T(512)}, u32[]{:S(2)}) copy-start(f32[512]{0:T(512)} %get-tuple-element.83) | copy-start | bytes 6148
  1685.4 253.9 %copy-start.318 = (f32[512]{0:T(512)S(1)}, f32[512]{0:T(512)}, u32[]{:S(2)}) copy-start(f32[512]{0:T(512)} %get-tuple-element.69) | copy-start | bytes 6148
  1685.4 253.9 %copy-start.319 = (f32[512]{0:T(512)S(1)}, f32[512]{0:T(512)}, u32[]{:S(2)}) copy-start(f32[512]{0:T(512)} %get-tuple-element.87) | copy-start | bytes 6148
  1685.4 253.9 %copy-start.320 = (f32[512]{0:T(512)S(1)}, f32[512]{0:T(512)}, u32[]{:S(2)}) copy-start(f32[512]{0:T(512)} %get-tuple-element.301) | copy-start | bytes 6148
  1685.4 253.9 %copy-start.321 = (f32[512]{0:T(512)S(1)}, f32[512]{0:T(512)}, u32[]{:S(2)}) copy-start(f32[512]{0:T(512)} %get-tuple-element.310) | copy-start | bytes 6148
  1685.4 253.9 %copy-start.346 = (f32[512]{0:T(512)S(1)}, f32[512]{0:T(512)}, u32[]{:S(2)}) copy-start(f32[512]{0:T(512)} %get-tuple-element.81) | copy-start | bytes 6148
  1685.5 253.9 %copy-start.347 = (f32[512]{0:T(512)S(1)}, f32[512]{0:T(512)}, u32[]{:S(2)}) copy-start(f32[512]{0:T(512)} %get-tuple-element.77) | copy-start | bytes 6148
  1685.5 253.9 %copy-start.348 = (f32[512]{0:T(512)S(1)}, f32[512]{0:T(512)}, u32[]{:S(2)}) copy-start(f32[512]{0:T(512)} %get-tuple-element.296) | copy-start | bytes 6148
  1685.5 253.9 %copy-start.349 = (f32[512]{0:T(512)S(1)}, f32[512]{0:T(512)}, u32[]{:S(2)}) copy-start(f32[512]{0:T(512)} %get-tuple-element.300) | copy-start | bytes 6148
  1685.5 315.4 %copy-start.258 = (f32[448]{0:T(512)S(1)}, f32[448]{0:T(512)}, u32[]{:S(2)}) copy-start(f32[448]{0:T(512)} %copy-done.256) | copy-start | bytes 5380
  1685.5 315.4 %copy-start.261 = (f32[448]{0:T(512)S(1)}, f32[448]{0:T(512)}, u32[]{:S(2)}) copy-start(f32[448]{0:T(512)} %copy-done.259) | copy-start | bytes 5380
  (368 other events, 7241.9 us)
Sparse Core Ops, SparseCore 0:
  10.2 40.6 all-gather.15
  53.0 36.8 all-gather.9
  92.7 40.1 all-gather.11
  134.9 43.9 all-gather.7
  181.0 36.7 all-gather.13
  219.8 49.6 all-gather.17
  271.6 49.0 all-gather.19
  331.8 38.6 reduce-scatter.34
  372.9 28.9 reduce-scatter.24
  525.5 30.0 reduce-scatter.36
  915.9 35.0 reduce-scatter.42
  979.6 25.3 reduce-scatter.38
  1017.0 25.3 reduce-scatter.30
  1044.5 28.9 reduce-scatter.28
  1076.2 28.9 reduce-scatter.26
  1107.3 39.0 reduce-scatter.22
  1407.1 96.4 all-reduce.14
  1507.0 56.6 reduce-scatter.60
  1567.8 56.3 reduce-scatter.58
  1627.7 56.3 reduce-scatter.56
  1688.5 71.7 reduce-scatter.64
  1764.1 71.2 reduce-scatter.62
  1837.7 28.0 reduce-scatter.32
  1867.9 28.9 reduce-scatter.44
  1899.8 28.9 reduce-scatter.40
  1933.0 66.4 reduce-scatter.54
  2001.6 41.4 reduce-scatter.48
  2045.5 42.6 reduce-scatter.52
  2090.4 42.6 reduce-scatter.50
  2135.3 42.6 reduce-scatter.46
where the time goes:
time: 2220 us; the launch traced here: 2210 us
  blocking collectives  621 us (28%)
  matrix products  607 us (27%)
  waiting for transfers between devices  526 us (24%)
  local copies, waits for them, and re-layouts  244 us (11%)
  other arithmetic  178 us (8%)
    all_gather x12, blocking collectives, spread_grad(): lax.all_gather(incoming.astype(jnp.bfloat16), 'tp', axis=1, tiled=True)  172 us
    reduce_scatter x4, waiting for transfers between devices, per_device(): lax.psum_scatter(frame_partial.astype(jnp.bfloat16), 'tp', scatter_dimens...  170 us
    all_gather x12, blocking collectives, spread_heads(): return lax.all_gather(columns, 'tp', axis=1, tiled=True)  148 us
    all_gather x12, blocking collectives, norm_forward(): return (lax.all_gather(normed, 'tp', axis=1, tiled=True), unit, inverse)  139 us
    reduce_scatter x8, waiting for transfers between devices, input_total(): lax.psum_scatter(partial_value, 'tp', scatter_dimension=1, tiled=True)  91.7 us
    dot_general x8, matrix products, attend_backward(): jnp.einsum('sqhe,skhe->shqk', grad_mixed, value_rows, preferred_element_t...  89 us
    convert_element_type x8, other arithmetic, attend_backward(): grad_scores = (weights * (grad_weights - inner)).astype(jnp.bfloat16)  80.1 us
    unnamed x801, local copies, waits for them, and re-layouts  77.2 us
  transfers between devices with their start and end apart: 32, of which 15 were waited for; matrix products, arithmetic and copies ran while one was open for 29% of the time, Pallas kernels for 0%

commit v1 on v0

--- a/solution.py
+++ b/solution.py
@@ -1,8 +1,11 @@
+import functools
 import math
 
 import jax
 import jax.numpy as jnp
 from jax import lax
+from jax.experimental import pallas as pl
+from jax.experimental.pallas import tpu as pltpu
 from jax.sharding import PartitionSpec as P
 
 D = 1024
@@ -10,10 +13,1163 @@
 SEQ_MB = 1
 MICRO = 4
 HEAD_DIM = 64
+BF = jnp.bfloat16
+F32 = jnp.float32
+LANES = 128
 
 
 EPSILON = 1e-05
 NEGATIVE = -1e30
+
+QKV, CKV, OUT, CQ, CO = 0, 3, 5, 6, 7
+VMEM_BYTES = 58 << 20
+
+
+def nn(a, b):
+    return jnp.dot(a, b, preferred_element_type=F32)
+
+
+def nt(a, b):
+    return lax.dot_general(a, b, (((1,), (1,)), ((), ())), preferred_element_type=F32)
+
+
+def tn(a, b):
+    return lax.dot_general(a, b, (((0,), (0,)), ((), ())), preferred_element_type=F32)
+
+
+def compiler_params(axes):
+    return pltpu.CompilerParams(
+        dimension_semantics=("arbitrary",) * axes, vmem_limit_bytes=VMEM_BYTES
+    )
+
+
+def cost(flops, *arrays):
+    return pl.CostEstimate(flops=1, bytes_accessed=1, transcendentals=0)
+
+
+def struct(shape, dtype):
+    return jax.ShapeDtypeStruct(shape, dtype)
+
+
+def weight(ref):
+    block = ref[0, :, 0]
+    return block.reshape(block.shape[0] * block.shape[1], block.shape[2])
+
+
+def weight_spec(gathered, index):
+    _, shards, _, rows, width = gathered.shape
+
+    def index_map(*grid):
+        column, block = index(*grid)
+        return (column, 0, block, 0, 0)
+
+    return pl.BlockSpec((1, shards, 1, rows, width), index_map)
+
+
+def whole(array):
+    return pl.BlockSpec(array.shape, lambda *grid: (0,) * len(array.shape))
+
+
+def row_loop(rows, body):
+    step = 128 if rows % 128 == 0 else 64
+
+    def run(at, carried):
+        body(pl.ds(pl.multiple_of(at * step, step), step))
+        return carried
+
+    lax.fori_loop(0, rows // step, run, 0)
+
+
+def norm_stats(values):
+    row_mean = jnp.mean(values, axis=1, keepdims=True)
+    square = jnp.mean(values * values, axis=1, keepdims=True)
+    return row_mean, lax.rsqrt(square - row_mean * row_mean + EPSILON)
+
+
+def write_norm(source_ref, normed_ref, gain, shift):
+    def body(rows):
+        values = source_ref[rows, :].astype(F32)
+        row_mean, inverse = norm_stats(values)
+        normed_ref[rows, :] = ((values - row_mean) * inverse * gain + shift).astype(BF)
+
+    row_loop(source_ref.shape[0], body)
+
+
+def write_norm_back(grad_ref, source_ref, gain, sums_ref, finish):
+    sums_ref[...] = jnp.zeros_like(sums_ref)
+
+    def body(rows):
+        incoming = grad_ref[rows, :]
+        values = source_ref[rows, :].astype(F32)
+        row_mean, inverse = norm_stats(values)
+        unit = (values - row_mean) * inverse
+        scaled = incoming * gain
+        back = inverse * (
+            scaled
+            - jnp.mean(scaled, axis=1, keepdims=True)
+            - unit * jnp.mean(scaled * unit, axis=1, keepdims=True)
+        )
+        low = finish(rows, back)
+        sums_ref[0:1, :] += jnp.sum(incoming * unit, axis=0, keepdims=True)
+        sums_ref[1:2, :] += jnp.sum(incoming, axis=0, keepdims=True)
+        sums_ref[2:3, :] += jnp.sum(low.astype(F32), axis=0, keepdims=True)
+
+    row_loop(grad_ref.shape[0], body)
+
+
+def qkv_kernel(hidden_ref, vec_ref, w_ref, bias_ref, out_ref, normed_ref):
+    @pl.when((pl.program_id(0) == 0) & (pl.program_id(1) == 0))
+    def _():
+        write_norm(hidden_ref, normed_ref, vec_ref[0:1, :], vec_ref[3:4, :])
+
+    out_ref[0, 0] = (nn(normed_ref[...], weight(w_ref)) + bias_ref[0, 0]).astype(BF)
+
+
+def project_qkv(hidden, vec, gathered, bias):
+    columns, width = gathered.shape[0], gathered.shape[-1]
+    tokens = hidden.shape[0]
+    return pl.pallas_call(
+        qkv_kernel,
+        grid=(columns, 3),
+        in_specs=[
+            whole(hidden),
+            whole(vec),
+            weight_spec(gathered, lambda y, c: (y, QKV + c)),
+            pl.BlockSpec((1, 1, 1, width), lambda y, c: (y, c, 0, 0)),
+        ],
+        out_specs=[
+            pl.BlockSpec((1, 1, tokens, width), lambda y, c: (y, c, 0, 0)),
+            whole(hidden),
+        ],
+        out_shape=[struct((columns, 3, tokens, width), BF), struct(hidden.shape, BF)],
+        compiler_params=compiler_params(2),
+        cost_estimate=cost(2 * tokens * D * 3 * columns * width, hidden, hidden),
+        name="project_qkv",
+    )(hidden, vec, gathered, bias)
+
+
+def head_row(head, value):
+    lane = lax.broadcasted_iota(jnp.int32, (1, LANES), 1)
+    inside = (lane >= head * HEAD_DIM) & (lane < (head + 1) * HEAD_DIM)
+    return jnp.where(inside, value, 0.0).astype(BF)
+
+
+def attend(query, key_rows, value_rows, visible, mixed_ref, probs_ref):
+    parts = []
+    for head in range(LANES // HEAD_DIM):
+        scores = nt(key_rows, query * head_row(head, HEAD_DIM**-0.5))
+        if visible is not None:
+            scores = jnp.where(visible, scores, NEGATIVE)
+        weights = jnp.exp(scores - jnp.max(scores, axis=0, keepdims=True))
+        inverse = 1.0 / jnp.sum(weights, axis=0, keepdims=True)
+        probs = (weights * inverse).astype(BF)
+        probs_ref[0, 0, 0, head] = probs
+        part = tn(value_rows, probs)
+        parts.append(part[head * HEAD_DIM : (head + 1) * HEAD_DIM])
+    mixed_ref[0] = jnp.concatenate(parts, axis=0).T.astype(BF)
+
+
+def attend_back(query, key_rows, value_rows, mixed, grad_mixed, probs_ref):
+    grad_f = grad_mixed.astype(F32)
+    product = (grad_f * mixed.astype(F32)).T
+    parts, grad_key, grad_value = [], 0.0, 0.0
+    for head in range(LANES // HEAD_DIM):
+        span = slice(head * HEAD_DIM, (head + 1) * HEAD_DIM)
+        inner = jnp.sum(product[span], axis=0, keepdims=True)
+        own_grad = grad_mixed * head_row(head, 1.0)
+        probs = probs_ref[0, 0, 0, head]
+        grad_weights = nt(value_rows, own_grad)
+        grad_scores = (probs.astype(F32) * (grad_weights - inner)).astype(BF)
+        grad_key = grad_key + nn(grad_scores, query * head_row(head, HEAD_DIM**-0.5))
+        grad_value = grad_value + nn(probs, own_grad)
+        parts.append(tn(key_rows, grad_scores)[span])
+    grad_query = jnp.concatenate(parts, axis=0).T * HEAD_DIM**-0.5
+    return grad_query.astype(BF), grad_key.astype(BF), grad_value.astype(BF)
+
+
+def self_kernel(q_ref, k_ref, v_ref, row_ref, column_ref, mixed_ref, probs_ref):
+    visible = column_ref[0] <= row_ref[0]
+    attend(q_ref[0, 0], k_ref[0, 0], v_ref[0, 0], visible, mixed_ref, probs_ref)
+
+
+def attend_self(qkv, order_row, order_column):
+    columns, _, tokens, width = qkv.shape
+    seqs, pairs = order_row.shape[0], width // LANES
+
+    def part(c):
+        return pl.BlockSpec((1, 1, LEN, LANES), lambda y, p, s: (y, c, s, p))
+
+    return pl.pallas_call(
+        self_kernel,
+        grid=(columns, pairs, seqs),
+        in_specs=[
+            part(0),
+            part(1),
+            part(2),
+            pl.BlockSpec((1, 1, LEN), lambda y, p, s: (s, 0, 0)),
+            pl.BlockSpec((1, LEN, 1), lambda y, p, s: (s, 0, 0)),
+        ],
+        out_specs=[
+            pl.BlockSpec((1, LEN, LANES), lambda y, p, s: (y, s, p)),
+            pl.BlockSpec((1, 1, 1, 2, LEN, LEN), lambda y, p, s: (y, p, s, 0, 0, 0)),
+        ],
+        out_shape=[
+            struct((columns, tokens, width), BF),
+            struct((columns, pairs, seqs, 2, LEN, LEN), BF),
+        ],
+        compiler_params=compiler_params(3),
+        cost_estimate=cost(16 * columns * pairs * seqs * LEN * LEN * LANES, qkv),
+        name="attend_self",
+    )(qkv, qkv, qkv, order_row, order_column)
+
+
+def out_kernel(mixed_ref, hidden_ref, vec_ref, wo_ref, wq_ref, bias_ref, first_ref, normed_ref, query_ref):
+    step, columns = pl.program_id(0), pl.num_programs(0) // 2
+
+    @pl.when(step == 0)
+    def _():
+        first_ref[...] = hidden_ref[...].astype(F32) + vec_ref[8:9, :]
+
+    @pl.when(step < columns)
+    def _():
+        first_ref[...] += nt(mixed_ref[0], weight(wo_ref))
+
+    @pl.when(step == columns - 1)
+    def _():
+        write_norm(first_ref, normed_ref, vec_ref[1:2, :], vec_ref[4:5, :])
+
+    @pl.when(step >= columns)
+    def _():
+        query_ref[0] = (nn(normed_ref[...], weight(wq_ref)) + bias_ref[0]).astype(BF)
+
+
+def project_out(mixed, hidden, vec, gathered, bias):
+    columns, tokens, width = mixed.shape
+
+    def early(i):
+        return jnp.minimum(i, columns - 1)
+
+    def late(i):
+        return jnp.maximum(i - columns, 0)
+
+    return pl.pallas_call(
+        out_kernel,
+        grid=(2 * columns,),
+        in_specs=[
+            pl.BlockSpec((1, tokens, width), lambda i: (early(i), 0, 0)),
+            whole(hidden),
+            whole(vec),
+            weight_spec(gathered, lambda i: (early(i), OUT)),
+            weight_spec(gathered, lambda i: (late(i), CQ)),
+            pl.BlockSpec((1, 1, width), lambda i: (late(i), 0, 0)),
+        ],
+        out_specs=[
+            whole(hidden),
+            whole(hidden),
+            pl.BlockSpec((1, tokens, width), lambda i: (late(i), 0, 0)),
+        ],
+        out_shape=[
+            struct(hidden.shape, F32),
+            struct(hidden.shape, BF),
+            struct((columns, tokens, width), BF),
+        ],
+        compiler_params=compiler_params(1),
+        cost_estimate=cost(4 * tokens * D * columns * width, hidden, hidden, mixed),
+        name="project_out",
+    )(mixed, hidden, vec, gathered, gathered, bias)
+
+
+def pair_kernel(own_ref, frames_ref, w_ref, bias_ref, out_ref):
+    out_ref[0, 0, 0] = (nn(frames_ref[0], weight(w_ref)) + bias_ref[0, 0]).astype(BF)
+
+
+def project_pair(own, frames, gathered, bias, seqs):
+    columns, width = gathered.shape[0], gathered.shape[-1]
+    length = frames.shape[1]
+    out = struct((columns, 2, seqs, length, width), BF)
+    return pl.pallas_call(
+        pair_kernel,
+        grid_spec=pltpu.PrefetchScalarGridSpec(
+            num_scalar_prefetch=1,
+            grid=(seqs, columns, 2),
+            in_specs=[
+                pl.BlockSpec((1, length, D), lambda s, y, c, own: (s, 0, 0)),
+                weight_spec(gathered, lambda s, y, c, own: (y, CKV + c)),
+                pl.BlockSpec((1, 1, 1, width), lambda s, y, c, own: (y, c, 0, 0)),
+            ],
+            out_specs=pl.BlockSpec((1, 1, 1, length, width), lambda s, y, c, own: (y, c, s, 0, 0)),
+        ),
+        out_shape=out,
+        compiler_params=compiler_params(3),
+        cost_estimate=cost(4 * seqs * length * D * columns * width, out, out),
+        name="project_pair",
+    )(own, frames, gathered, bias)
+
+
+def cross_kernel(q_ref, kv_ref, mixed_ref, probs_ref):
+    attend(q_ref[0], kv_ref[0, 0, 0], kv_ref[0, 1, 0], None, mixed_ref, probs_ref)
+
+
+def attend_cross(query, pair):
+    columns, tokens, width = query.shape
+    seqs, length, pairs = pair.shape[2], pair.shape[3], width // LANES
+    return pl.pallas_call(
+        cross_kernel,
+        grid=(columns, pairs, seqs),
+        in_specs=[
+            pl.BlockSpec((1, LEN, LANES), lambda y, p, s: (y, s, p)),
+            pl.BlockSpec((1, 2, 1, length, LANES), lambda y, p, s: (y, 0, s, 0, p)),
+        ],
+        out_specs=[
+            pl.BlockSpec((1, LEN, LANES), lambda y, p, s: (y, s, p)),
+            pl.BlockSpec((1, 1, 1, 2, length, LEN), lambda y, p, s: (y, p, s, 0, 0, 0)),
+        ],
+        out_shape=[
+            struct((columns, tokens, width), BF),
+            struct((columns, pairs, seqs, 2, length, LEN), BF),
+        ],
+        compiler_params=compiler_params(3),
+        cost_estimate=cost(16 * columns * pairs * seqs * LEN * length * LANES, pair),
+        name="attend_cross",
+    )(query, pair)
+
+
+def erf(value):
+    x = jnp.clip(value, -3.832506856900711, 3.832506856900711)
+    square = x * x
+    top = jnp.full_like(x, 0.00022905065861350646)
+    for coefficient in (0.0034082910107109506, 0.050955695062380861, 0.18520832239976145, 1.128379143519084):
+        top = top * square + coefficient
+    bottom = jnp.full_like(x, -1.1791602954361697e-7)
+    for coefficient in (
+        0.000023547966471313185,
+        0.0010179625278914885,
+        0.014070470171167667,
+        0.11098505178285362,
+        0.49746925110067538,
+        1.0,
+    ):
+        bottom = bottom * square + coefficient
+    return x * top / bottom
+
+
+def halves_of(value, own):
+    width = value.shape[1] // 2
+    low, high = value[:, :width], value[:, width:]
+    return jnp.where(own == 0, high, low), jnp.where(own == 0, low, high)
+
+
+def mlp_kernel(
+    own_ref, mixed_ref, first_ref, vec_ref, wo_ref, wu_ref, wd_ref, bias_ref,
+    second_ref, normed_ref, act_ref, slope_ref, send_ref, keep_ref, total_ref,
+):
+    step, columns = pl.program_id(0), 2
+
+    @pl.when(step == 0)
+    def _():
+        second_ref[...] = first_ref[...] + vec_ref[11:12, :]
+
+    @pl.when(step < columns)
+    def _():
+        second_ref[...] += nt(mixed_ref[0], weight(wo_ref))
+
+    @pl.when(step == columns - 1)
+    def _():
+        write_norm(second_ref, normed_ref, vec_ref[2:3, :], vec_ref[5:6, :])
+        total_ref[...] = second_ref[...] + vec_ref[12:13, :]
+
+    @pl.when(step >= columns)
+    def _():
+        before = nn(normed_ref[...], weight(wu_ref)) + bias_ref[0, 0]
+        cdf = 0.5 + 0.5 * erf(before * (0.5**0.5))
+        density = jnp.exp(-0.5 * before * before) * (1.0 / math.sqrt(2.0 * math.pi))
+        act = (before * cdf).astype(BF)
+        act_ref[0, 0] = act
+        slope_ref[0, 0] = (cdf + before * density).astype(BF)
+        total_ref[...] += nt(act, weight(wd_ref))
+
+    @pl.when(step == pl.num_programs(0) - 1)
+    def _():
+        send, keep = halves_of(total_ref[...], own_ref[0])
+        send_ref[...] = send.astype(BF)
+        keep_ref[...] = keep.astype(BF)
+
+
+def mlp_forward(own, mixed, first, vec, gathered, gathered_mlp, bias):
+    columns, tokens, width = mixed.shape
+    blocks = gathered_mlp.shape[2] // 2
+
+    def early(i):
+        return jnp.minimum(i, columns - 1)
+
+    def late(i):
+        rest = jnp.maximum(i - columns, 0)
+        return rest // blocks, rest % blocks
+
+    units = struct((columns, blocks, tokens, width), BF)
+    half = struct((tokens, width), BF)
+    unit_spec = pl.BlockSpec((1, 1, tokens, width), lambda i, own: (*late(i), 0, 0))
+    return pl.pallas_call(
+        mlp_kernel,
+        grid_spec=pltpu.PrefetchScalarGridSpec(
+            num_scalar_prefetch=1,
+            grid=(columns + columns * blocks,),
+            in_specs=[
+                pl.BlockSpec((1, tokens, width), lambda i, own: (early(i), 0, 0)),
+                whole(first),
+                whole(vec),
+                weight_spec(gathered, lambda i, own: (early(i), CO)),
+                weight_spec(gathered_mlp, lambda i, own: late(i)),
+                weight_spec(gathered_mlp, lambda i, own: (late(i)[0], blocks + late(i)[1])),
+                pl.BlockSpec((1, 1, 1, width), lambda i, own: (*late(i), 0, 0)),
+            ],
+            out_specs=[whole(first), whole(first), unit_spec, unit_spec, whole(half), whole(half)],
+            scratch_shapes=[pltpu.VMEM(first.shape, F32)],
+        ),
+        out_shape=[struct(first.shape, F32), struct(first.shape, BF), units, units, half, half],
+        compiler_params=compiler_params(1),
+        cost_estimate=cost(tokens * D * columns * width * (2 + 4 * blocks), first, units, units, gathered_mlp),
+        name="mlp_forward",
+    )(own, mixed, first, vec, gathered, gathered_mlp, gathered_mlp, bias)
+
+
+def mlp_back_kernel(
+    grad_ref, second_ref, vec_ref, wd_ref, wu_ref, wo_ref, slope_ref,
+    before_ref, unit_sum_ref, grad_second_ref, low_ref, sums_ref, mixed_ref, total_ref,
+):
+    step, columns = pl.program_id(0), mixed_ref.shape[1] * 0 + vec_ref.shape[1] // mixed_ref.shape[2]
+    last = pl.num_programs(0) - columns
+
+    @pl.when(step == 0)
+    def _():
+        total_ref[...] = jnp.zeros_like(total_ref)
+
+    @pl.when(step < last)
+    def _():
+        grad_act = nn(grad_ref[...], weight(wd_ref))
+        before = (grad_act * slope_ref[0, 0].astype(F32)).astype(BF)
+        before_ref[0, 0] = before
+        unit_sum_ref[0, 0] = jnp.sum(before.astype(F32), axis=0, keepdims=True)
+        total_ref[...] += nt(before, weight(wu_ref))
+
+    @pl.when(step == last - 1)
+    def _():
+        def finish(rows, back):
+            incoming = grad_ref[rows, :].astype(F32)
+            value = incoming + back
+            grad_second_ref[rows, :] = value
+            low_ref[rows, :] = value.astype(BF)
+            return value.astype(BF)
+
+        write_norm_back(total_ref, second_ref, vec_ref[2:3, :], sums_ref, finish)
+        sums_ref[3:4, :] = jnp.sum(grad_ref[...].astype(F32), axis=0, keepdims=True)
+
+    @pl.when(step >= last)
+    def _():
+        mixed_ref[0] = nn(low_ref[...], weight(wo_ref)).astype(BF)
+
+
+def mlp_backward(grad, second, vec, gathered, gathered_mlp, slope):
+    columns, blocks, tokens, width = slope.shape
+
+    def early(i):
+        rest = jnp.minimum(i, columns * blocks - 1)
+        return rest // blocks, rest % blocks
+
+    def late(i):
+        return jnp.maximum(i - columns * blocks, 0)
+
+    unit_spec = pl.BlockSpec((1, 1, tokens, width), lambda i: (*early(i), 0, 0))
+    sums = struct((8, D), F32)
+    return pl.pallas_call(
+        mlp_back_kernel,
+        grid=(columns * blocks + columns,),
+        in_specs=[
+            whole(grad),
+            whole(second),
+            whole(vec),
+            weight_spec(gathered_mlp, lambda i: (early(i)[0], blocks + early(i)[1])),
+            weight_spec(gathered_mlp, lambda i: early(i)),
+            weight_spec(gathered, lambda i: (late(i), CO)),
+            unit_spec,
+        ],
+        out_specs=[
+            unit_spec,
+            pl.BlockSpec((1, 1, 1, width), lambda i: (*early(i), 0, 0)),
+            whole(second),
+            whole(grad),
+            whole(sums),
+            pl.BlockSpec((1, tokens, width), lambda i: (late(i), 0, 0)),
+        ],
+        out_shape=[
+            struct(slope.shape, BF),
+            struct((columns, blocks, 1, width), F32),
+            struct(second.shape, F32),
+            struct(grad.shape, BF),
+            sums,
+            struct((columns, tokens, width), BF),
+        ],
+        scratch_shapes=[pltpu.VMEM(second.shape, F32)],
+        compiler_params=compiler_params(1),
+        cost_estimate=cost(tokens * D * columns * width * (2 + 4 * blocks), second, slope, slope, gathered_mlp),
+        name="mlp_backward",
+    )(grad, second, vec, gathered_mlp, gathered_mlp, gathered, slope)
+
+
+def cross_back_kernel(q_ref, kv_ref, mixed_ref, grad_ref, probs_ref, query_ref, pair_ref, sums_ref):
+    grad_query, grad_key, grad_value = attend_back(
+        q_ref[0], kv_ref[0, 0, 0], kv_ref[0, 1, 0], mixed_ref[0], grad_ref[0], probs_ref
+    )
+    query_ref[0] = grad_query
+    pair_ref[0, 0, 0] = grad_key
+    pair_ref[0, 1, 0] = grad_value
+
+    @pl.when(pl.program_id(2) == 0)
+    def _():
+        sums_ref[...] = jnp.zeros_like(sums_ref)
+
+    sums_ref[0, 0:1, :] += jnp.sum(grad_query.astype(F32), axis=0, keepdims=True)
+    sums_ref[0, 1:2, :] += jnp.sum(grad_value.astype(F32), axis=0, keepdims=True)
+
+
+def attend_cross_back(query, pair, mixed, grad, probs):
+    columns, tokens, width = query.shape
+    seqs, length, pairs = pair.shape[2], pair.shape[3], width // LANES
+    row_spec = pl.BlockSpec((1, LEN, LANES), lambda y, p, s: (y, s, p))
+    pair_spec = pl.BlockSpec((1, 2, 1, length, LANES), lambda y, p, s: (y, 0, s, 0, p))
+    return pl.pallas_call(
+        cross_back_kernel,
+        grid=(columns, pairs, seqs),
+        in_specs=[
+            row_spec,
+            pair_spec,
+            row_spec,
+            row_spec,
+            pl.BlockSpec((1, 1, 1, 2, length, LEN), lambda y, p, s: (y, p, s, 0, 0, 0)),
+        ],
+        out_specs=[row_spec, pair_spec, pl.BlockSpec((1, 8, LANES), lambda y, p, s: (y, 0, p))],
+        out_shape=[
+            struct(query.shape, BF),
+            struct(pair.shape, BF),
+            struct((columns, 8, width), F32),
+        ],
+        compiler_params=compiler_params(3),
+        cost_estimate=cost(32 * columns * pairs * seqs * LEN * length * LANES, pair, pair, probs),
+        name="attend_cross_back",
+    )(query, pair, mixed, grad, probs)
+
+
+def self_back_kernel(
+    q_ref, k_ref, v_ref, mixed_ref, grad_ref, probs_ref, out_ref, sums_ref
+):
+    grad_query, grad_key, grad_value = attend_back(
+        q_ref[0, 0], k_ref[0, 0], v_ref[0, 0], mixed_ref[0], grad_ref[0], probs_ref
+    )
+    out_ref[0, 0] = grad_query
+    out_ref[0, 1] = grad_key
+    out_ref[0, 2] = grad_value
+
+    @pl.when(pl.program_id(2) == 0)
+    def _():
+        sums_ref[...] = jnp.zeros_like(sums_ref)
+
+    sums_ref[0, 0:1, :] += jnp.sum(grad_query.astype(F32), axis=0, keepdims=True)
+    sums_ref[0, 1:2, :] += jnp.sum(grad_value.astype(F32), axis=0, keepdims=True)
+
+
+def attend_self_back(qkv, mixed, grad, probs):
+    columns, _, tokens, width = qkv.shape
+    seqs, pairs = probs.shape[2], width // LANES
+    row_spec = pl.BlockSpec((1, LEN, LANES), lambda y, p, s: (y, s, p))
+
+    def part(c):
+        return pl.BlockSpec((1, 1, LEN, LANES), lambda y, p, s: (y, c, s, p))
+
+    return pl.pallas_call(
+        self_back_kernel,
+        grid=(columns, pairs, seqs),
+        in_specs=[
+            part(0),
+            part(1),
+            part(2),
+            row_spec,
+            row_spec,
+            pl.BlockSpec((1, 1, 1, 2, LEN, LEN), lambda y, p, s: (y, p, s, 0, 0, 0)),
+        ],
+        out_specs=[
+            pl.BlockSpec((1, 3, LEN, LANES), lambda y, p, s: (y, 0, s, p)),
+            pl.BlockSpec((1, 8, LANES), lambda y, p, s: (y, 0, p)),
+        ],
+        out_shape=[struct(qkv.shape, BF), struct((columns, 8, width), F32)],
+        compiler_params=compiler_params(3),
+        cost_estimate=cost(32 * columns * pairs * seqs * LEN * LEN * LANES, qkv, qkv, probs),
+        name="attend_self_back",
+    )(qkv, qkv, qkv, mixed, grad, probs)
+
+
+def query_back_kernel(
+    grad_ref, first_ref, second_ref, vec_ref, wq_ref, wo_ref,
+    grad_first_ref, low_ref, sums_ref, mixed_ref, total_ref,
+):
+    step, columns = pl.program_id(0), pl.num_programs(0) // 2
+
+    @pl.when(step == 0)
+    def _():
+        total_ref[...] = jnp.zeros_like(total_ref)
+
+    @pl.when(step < columns)
+    def _():
+        total_ref[...] += nt(grad_ref[0], weight(wq_ref))
+
+    @pl.when(step == columns - 1)
+    def _():
+        def finish(rows, back):
+            value = second_ref[rows, :] + back
+            grad_first_ref[rows, :] = value
+            low_ref[rows, :] = value.astype(BF)
+            return value.astype(BF)
+
+        write_norm_back(total_ref, first_ref, vec_ref[1:2, :], sums_ref, finish)
+
+    @pl.when(step >= columns)
+    def _():
+        mixed_ref[0] = nn(low_ref[...], weight(wo_ref)).astype(BF)
+
+
+def query_backward(grad, first, grad_second, vec, gathered):
+    columns, tokens, width = grad.shape
+
+    def early(i):
+        return jnp.minimum(i, columns - 1)
+
+    def late(i):
+        return jnp.maximum(i - columns, 0)
+
+    sums = struct((8, D), F32)
+    return pl.pallas_call(
+        query_back_kernel,
+        grid=(2 * columns,),
+        in_specs=[
+            pl.BlockSpec((1, tokens, width), lambda i: (early(i), 0, 0)),
+            whole(first),
+            whole(first),
+            whole(vec),
+            weight_spec(gathered, lambda i: (early(i), CQ)),
+            weight_spec(gathered, lambda i: (late(i), OUT)),
+        ],
+        out_specs=[
+            whole(first),
+            whole(first),
+            whole(sums),
+            pl.BlockSpec((1, tokens, width), lambda i: (late(i), 0, 0)),
+        ],
+        out_shape=[struct(first.shape, F32), struct(first.shape, BF), sums, struct(grad.shape, BF)],
+        scratch_shapes=[pltpu.VMEM(first.shape, F32)],
+        compiler_params=compiler_params(1),
+        cost_estimate=cost(4 * tokens * D * columns * width, first, first, first, grad),
+        name="query_backward",
+    )(grad, first, grad_second, vec, gathered, gathered)
+
+
+def hidden_back_kernel(
+    own_ref, grad_ref, hidden_ref, first_ref, vec_ref, w_ref, send_ref, keep_ref, sums_ref, total_ref
+):
+    step = pl.program_id(0)
+
+    @pl.when(step == 0)
+    def _():
+        total_ref[...] = jnp.zeros_like(total_ref)
+
+    total_ref[...] += nt(grad_ref[0, 0], weight(w_ref))
+
+    @pl.when(step == pl.num_programs(0) - 1)
+    def _():
+        def finish(rows, back):
+            value = first_ref[rows, :] + back
+            send, keep = halves_of(value, own_ref[0])
+            send_ref[rows, :] = send.astype(BF)
+            keep_ref[rows, :] = keep
+            return value
+
+        write_norm_back(total_ref, hidden_ref, vec_ref[0:1, :], sums_ref, finish)
+
+
+def hidden_backward(own, grad, hidden, grad_first, vec, gathered):
+    columns, _, tokens, width = grad.shape
+    sums, half = struct((8, D), F32), struct((tokens, width), F32)
+    return pl.pallas_call(
+        hidden_back_kernel,
+        grid_spec=pltpu.PrefetchScalarGridSpec(
+            num_scalar_prefetch=1,
+            grid=(3 * columns,),
+            in_specs=[
+                pl.BlockSpec((1, 1, tokens, width), lambda i, own: (i // 3, i % 3, 0, 0)),
+                whole(hidden),
+                whole(grad_first),
+                whole(vec),
+                weight_spec(gathered, lambda i, own: (i // 3, QKV + i % 3)),
+            ],
+            out_specs=[whole(half), whole(half), whole(sums)],
+            scratch_shapes=[pltpu.VMEM(hidden.shape, F32)],
+        ),
+        out_shape=[struct((tokens, width), BF), half, sums],
+        compiler_params=compiler_params(1),
+        cost_estimate=cost(6 * tokens * D * columns * width, grad, grad_first, hidden, grad_first),
+        name="hidden_backward",
+    )(own, grad, hidden, grad_first, vec, gathered)
+
+
+def frames_back_kernel(own_ref, grad_ref, w_ref, send_ref, keep_ref, total_ref):
+    step = pl.program_id(1)
+    part = nt(grad_ref[0, 0, 0], weight(w_ref))
+
+    @pl.when(step == 0)
+    def _():
+        total_ref[...] = part
+
+    @pl.when(step > 0)
+    def _():
+        total_ref[...] += part
+
+    @pl.when(step == pl.num_programs(1) - 1)
+    def _():
+        send, keep = halves_of(total_ref[...], own_ref[0])
+        length, width = keep.shape
+        for ref, value in ((send_ref, send), (keep_ref, keep)):
+            ref[0, :length] = value.astype(BF)
+            ref[0, length:] = jnp.zeros((ref.shape[1] - length, width), BF)
+
+
+def frames_backward(own, grad, gathered):
+    columns, _, seqs, length, width = grad.shape
+    padded = -(-length // 16) * 16
+    half = struct((seqs, padded, width), BF)
+    half_spec = pl.BlockSpec((1, padded, width), lambda s, i, own: (s, 0, 0))
+    return pl.pallas_call(
+        frames_back_kernel,
+        grid_spec=pltpu.PrefetchScalarGridSpec(
+            num_scalar_prefetch=1,
+            grid=(seqs, 2 * columns),
+            in_specs=[
+                pl.BlockSpec((1, 1, 1, length, width), lambda s, i, own: (i // 2, i % 2, s, 0, 0)),
+                weight_spec(gathered, lambda s, i, own: (i // 2, CKV + i % 2)),
+            ],
+            out_specs=[half_spec, half_spec],
+            scratch_shapes=[pltpu.VMEM((length, columns * width), F32)],
+        ),
+        out_shape=[half, half],
+        compiler_params=compiler_params(2),
+        cost_estimate=cost(4 * seqs * length * D * columns * width, grad, grad),
+        name="frames_backward",
+    )(own, grad, gathered)
+
+
+class Plan:
+    def __init__(self, order, bits):
+        self.order, self.rest, self.bits = order, 1 << (bits - 2), bits
+        self.sizes = {"x": 2, "y": 2, "z": self.rest}
+        self.cuts = tuple(self.sizes[c] for c in order)
+
+    def block(self, step_index):
+        return tuple(1 if c == "y" else self.sizes[c] for c in self.order)
+
+    def place(self, column):
+        return tuple(column if c == "y" else 0 for c in self.order)
+
+    def store(self, ref, value):
+        rows = value.shape[0] // (2 * self.rest)
+        value = value.reshape(2, self.rest, rows, value.shape[1])
+        if self.order.index("x") > self.order.index("z"):
+            value = value.swapaxes(0, 1)
+        at = tuple(0 if c == "y" else slice(None) for c in self.order)
+        ref[at + (0,)] = value
+
+
+def cut_rows(place_ref, source, turned_ref, shards):
+    rows = source.shape[0] // shards
+    for shard in range(shards):
+        at = pl.multiple_of(place_ref[1 + shard] * rows, rows)
+        turned_ref[pl.ds(at, rows), :] = source[shard * rows : (shard + 1) * rows]
+
+
+def weight_kernel(plan, frames, place_ref, left_ref, right_ref, send_ref, keep_ref, turned_ref):
+    shards = 1 << plan.bits
+
+    @pl.when((pl.program_id(0) == 0) & (pl.program_id(1) == 0))
+    def _():
+        if frames:
+            for s in range(left_ref.shape[0]):
+                cut_rows(place_ref, left_ref[s].T, turned_ref.at[s], shards)
+        else:
+            cut_rows(place_ref, left_ref[...].T, turned_ref, shards)
+
+    if frames:
+        total = 0.0
+        for s in range(left_ref.shape[0]):
+            total = total + nn(turned_ref[s], right_ref[0, 0, s])
+    else:
+        total = nn(turned_ref[...], right_ref[0, 0])
+    half = total.shape[0] // 2
+    plan.store(send_ref, total[:half].astype(BF))
+    plan.store(keep_ref, total[half:].astype(BF))
+
+
+def weight_grad(plan, place, left, right, frames=False, first=0, count=None):
+    columns, blocks = right.shape[:2]
+    blocks = count or blocks
+    width = right.shape[-1]
+    tokens = right.shape[-2]
+    seqs = right.shape[2] if frames else 1
+    rows = D >> plan.bits
+    part = struct(plan.cuts + (blocks, rows, width), BF)
+    out_spec = pl.BlockSpec(
+        plan.block(0) + (1, rows, width),
+        lambda y, i, place: plan.place(y) + (i, 0, 0),
+    )
+
+    def column(y, place):
+        return jnp.where(y == 1, place[0], 1 - place[0])
+
+    if frames:
+        left_spec = whole(left)
+        right_spec = pl.BlockSpec(
+            (1, 1, seqs, tokens, width), lambda y, i, place: (column(y, place), first + i, 0, 0, 0)
+        )
+        turned = pltpu.VMEM((seqs, D, tokens), BF)
+    else:
+        left_spec = whole(left)
+        right_spec = pl.BlockSpec((1, 1, tokens, width), lambda y, i, place: (column(y, place), first + i, 0, 0))
+        turned = pltpu.VMEM((D, tokens), BF)
+    return pl.pallas_call(
+        functools.partial(weight_kernel, plan, frames),
+        grid_spec=pltpu.PrefetchScalarGridSpec(
+            num_scalar_prefetch=1,
+            grid=(columns, blocks),
+            in_specs=[left_spec, right_spec],
+            out_specs=[out_spec, out_spec],
+            scratch_shapes=[turned],
+        ),
+        out_shape=[part, part],
+        compiler_params=compiler_params(2),
+        cost_estimate=cost(2 * columns * blocks * seqs * tokens * width * D, right, part, part),
+        name="weight_grad",
+    )(place, left, right)
+
+
+def cut_kernel(keep_ref, got_ref, send_ref, out_ref):
+    for part, ref in ((0, send_ref), (1, out_ref)):
+        ref[...] = (keep_ref[part].astype(F32) + got_ref[part].astype(F32)).astype(BF)
+
+
+def add_and_cut(keep, got):
+    shape = keep.shape[1:]
+    width = shape[-1]
+    rows = math.prod(shape[:-1])
+    step = math.gcd(rows, 1024)
+    flat = (2, rows, width)
+    out = struct((rows, width), BF)
+    in_spec = pl.BlockSpec((2, step, width), lambda i: (0, i, 0))
+    out_spec = pl.BlockSpec((step, width), lambda i: (i, 0))
+    send, own = pl.pallas_call(
+        cut_kernel,
+        grid=(rows // step,),
+        in_specs=[in_spec, in_spec],
+        out_specs=[out_spec, out_spec],
+        out_shape=[out, out],
+        compiler_params=compiler_params(1),
+        cost_estimate=cost(0, keep, got, out, out),
+        name="add_and_cut",
+    )(keep.reshape(flat), got.reshape(flat))
+    return send.reshape(shape), own.reshape(shape)
+
+
+def frames_join_kernel(own_ref, keep_ref, *refs):
+    *got_refs, out_ref = refs
+    length, seqs = out_ref.shape[0], len(got_refs)
+    for s in range(seqs):
+        keep = keep_ref[s, :length].astype(F32)
+        got = got_refs[s][0, :length].astype(F32)
+        out_ref[:, s, :] = jnp.where(own_ref[0] == 0, keep, got)
+        out_ref[:, seqs + s, :] = jnp.where(own_ref[0] == 0, got, keep)
+
+
+def join_frames(own, keep, *arguments):
+    *got, length = arguments
+    seqs, padded, width = keep.shape
+    return pl.pallas_call(
+        frames_join_kernel,
+        grid_spec=pltpu.PrefetchScalarGridSpec(
+            num_scalar_prefetch=1,
+            grid=(width // LANES,),
+            in_specs=[pl.BlockSpec((seqs, padded, LANES), lambda i, own: (0, 0, i))]
+            + [pl.BlockSpec((1, padded, LANES), lambda i, own: (0, 0, i))] * seqs,
+            out_specs=pl.BlockSpec((length, 2 * seqs, LANES), lambda i, own: (0, 0, i)),
+        ),
+        out_shape=struct((length, 2 * seqs, width), F32),
+        compiler_params=compiler_params(1),
+        cost_estimate=cost(0, keep),
+        name="join_frames",
+    )(own, keep, *got)
+
+
+def swap(axis, bit, value):
+    size = lax.axis_size(axis)
+    return lax.ppermute(value, axis, [(d, d ^ (1 << bit)) for d in range(size)])
+
+
+def pick(array, index, axis):
+    return lax.dynamic_index_in_dim(array, index, axis, keepdims=False)
+
+
+def exchange(keep, send):
+    if lax.axis_size("tp") != 2:
+        got = lax.all_to_all(send, "tp", split_axis=0, concat_axis=0, tiled=True)
+        return got.astype(keep.dtype)
+    own = lax.axis_index("tp")
+    got = swap("tp", 0, pick(send, 1 - own, 0)).astype(keep.dtype)
+    mine = pick(keep, own, 0)
+    return jnp.where(own == 0, jnp.stack([mine, got]), jnp.stack([got, mine]))
+
+
+def bits_of(axis):
+    return lax.axis_size(axis).bit_length() - 1
+
+
+class Chain:
+    def __init__(self):
+        self.token = None
+
+    def tie(self, *values):
+        if self.token is None:
+            return values
+        return lax.optimization_barrier((*values, self.token))[:-1]
+
+    def hold(self, value):
+        (self.token,) = self.tie(value)
+        return self.token
+
+
+class Reduction:
+    def __init__(self, chain, plan, place, left, right, **options):
+        self.chain, self.result = chain, None
+        stages = {"x": [("dp", 1)], "y": [("tp", 0)], "z": [("dp", b) for b in range(2, plan.bits)]}
+        self.order = [stage for c in plan.order for stage in stages[c]]
+        (right,) = chain.tie(right)
+        send, keep = weight_grad(plan, place, left, right, **options)
+        chain.token = send
+        self.cuts = []
+        for c in plan.order:
+            self.cuts += [2] * len(stages[c])
+        shape = tuple(self.cuts) + send.shape[len(plan.cuts) :]
+        self.keep, self.first, self.got = keep.reshape(shape), send.reshape(shape), None
+
+    def step(self):
+        if self.got is None:
+            self.got = swap("dp", 0, self.chain.tie(self.first)[0])
+        elif self.order:
+            keep, got = self.chain.tie(self.keep, self.got)
+            send, self.keep = add_and_cut(keep, got)
+            self.chain.token = send
+            self.got = swap(*self.order.pop(0), send)
+        elif self.result is None:
+            keep, got = self.chain.tie(self.keep, self.got)
+            self.result = keep.astype(F32) + got.astype(F32)
+
+    def finish(self):
+        while self.result is None:
+            self.step()
+        return self.result
+
+
+def per_device_whole_sequences(
+    hidden_in, encoder_states, positions, self_qkv, self_out, cross_query, cross_kv, cross_out,
+    up_weight, down_weight, norm_gains, bias_rows, up_bias, out_grad,
+):
+    columns, shards = lax.axis_size("tp"), lax.axis_size("dp")
+    own = lax.axis_index("tp")
+    width = hidden_in.shape[1]
+    tokens = hidden_in.shape[0] // columns
+    seqs = positions.shape[0] // columns
+    own_index = own.astype(jnp.int32).reshape(1)
+
+    attention_part = jnp.concatenate(
+        [
+            self_qkv.transpose(1, 0, 2),
+            cross_kv.transpose(1, 0, 2),
+            self_out.T[None],
+            cross_query[None],
+            cross_out.T[None],
+        ]
+    )
+    rows = up_weight.shape[0]
+    blocks = up_weight.shape[1] // width
+    mlp_part = jnp.concatenate(
+        [
+            up_weight.reshape(rows, blocks, width).transpose(1, 0, 2),
+            down_weight.reshape(blocks, width, rows).transpose(0, 2, 1),
+        ]
+    )
+
+    def gather(part):
+        full = lax.all_gather(part, ("tp", "dp"), axis=0)
+        return full.reshape((columns, shards) + part.shape)
+
+    weights, weights_mlp = gather(attention_part), gather(mlp_part)
+
+    def to_tokens(array):
+        mine = lax.dynamic_slice_in_dim(array, own * tokens, tokens, 0)
+        got = swap("tp", 0, lax.dynamic_slice_in_dim(array, (1 - own) * tokens, tokens, 0))
+        return jnp.where(
+            own == 0, jnp.concatenate([mine, got], axis=1), jnp.concatenate([got, mine], axis=1)
+        )
+
+    hidden, grad_final = to_tokens(hidden_in), to_tokens(out_grad)
+    small = jnp.concatenate([norm_gains, bias_rows, up_bias.reshape(blocks, width)])
+    every = jnp.broadcast_to(small, (columns,) + small.shape)
+    every = exchange(every, every)
+    vec = every[:, :13].transpose(1, 0, 2).reshape(13, columns * width)
+    vec = jnp.concatenate([vec, jnp.zeros((3, columns * width), F32)])
+    none = jnp.zeros((columns, width), F32)
+    bias = lambda row: every[:, 3 + row]
+    qkv_bias = jnp.stack([bias(3), none, bias(4)], axis=1)[:, :, None]
+    pair_bias = jnp.stack([none, bias(7)], axis=1)[:, :, None]
+    up_rows = every[:, 13:][:, :, None]
+    order = lax.dynamic_slice_in_dim(positions, own * seqs, seqs, 0)
+
+    frames = lax.optimization_barrier(
+        lax.dynamic_slice_in_dim(encoder_states, own * seqs, seqs, 0)
+    )
+
+    qkv, normed_a = project_qkv(hidden, vec, weights, qkv_bias)
+    pair = project_pair(own_index, frames, weights, pair_bias, seqs)
+    mixed_a, probs_a = attend_self(qkv, order[:, None, :], order[:, :, None])
+    first, normed_c, query = project_out(mixed_a, hidden, vec, weights, bias(6)[:, None])
+    mixed_c, probs_c = attend_cross(query, pair)
+    second, normed_m, activated, slope, send_output, keep_output = mlp_forward(
+        own_index, mixed_c, first, vec, weights, weights_mlp, up_rows
+    )
+
+    got_output = swap("tp", 0, send_output)
+
+    def pair_up(keep, got):
+        got = got.astype(keep.dtype)
+        return jnp.where(own == 0, jnp.stack([keep, got]), jnp.stack([got, keep]))
+
+    chain = Chain()
+    chain.token = send_output
+    bits = bits_of("dp")
+    device = lax.axis_index("dp")
+    shard = jnp.arange(shards)
+    same = ~(shard ^ device)
+    spot = sum(((same >> b) & 1) << (bits - 1 - b) for b in range(bits))
+    place = jnp.concatenate([own_index, spot.astype(jnp.int32)])
+
+    def reduction(left, right, order="xyz", **options):
+        return Reduction(chain, Plan(order, bits), place, left, right, **options)
+
+    def advance(*several):
+        for one in several:
+            one.step()
+
+    def run(kernel, first_array, *arrays):
+        (first_array,) = chain.tie(first_array)
+        results = kernel(first_array, *arrays)
+        chain.token = results[0]
+        return results
+
+    down = reduction(grad_final, activated)
+    advance(down)
+    grad_before, up_sums, grad_second, low_second, sums_m, grad_mixed_c = run(
+        mlp_backward, grad_final, second, vec, weights, weights_mlp, slope
+    )
+    output = pair_up(keep_output, chain.hold(got_output)).reshape(columns * tokens, width)
+    advance(down)
+    up = reduction(normed_m, grad_before, "yxz")
+    advance(up)
+    co = reduction(low_second, mixed_c[:, None], "zyx")
+    advance(up, co)
+    (grad_mixed_c,) = chain.tie(grad_mixed_c)
+    grad_query, grad_pair, sums_cross = run(attend_cross_back, query, pair, mixed_c, grad_mixed_c, probs_c)
+    advance(down, up, co)
+    send_frames, keep_frames = run(
+        lambda grad: frames_backward(own_index, grad, weights), grad_pair
+    )
+    advance(down, up, co)
+    got_frames = [swap("tp", 0, part) for part in jnp.split(chain.tie(send_frames)[0], seqs)]
+    kv = reduction(frames, grad_pair, "xzy", frames=True)
+    got_frames[0] = chain.hold(got_frames[0])
+    grad_first, low_first, sums_c, grad_mixed_a = run(
+        query_backward, grad_query, first, grad_second, vec, weights
+    )
+    advance(down, up, co, kv)
+    (grad_mixed_a,) = chain.tie(grad_mixed_a)
+    grad_triple, sums_self = run(attend_self_back, qkv, mixed_a, grad_mixed_a, probs_a)
+    advance(co, kv)
+    triple = reduction(normed_a, grad_triple, "xyz", first=0, count=2)
+    values = reduction(normed_a, grad_triple, "yxz", first=2, count=1)
+    got_frames[1:] = [chain.hold(part) for part in got_frames[1:]]
+    advance(kv, triple, values)
+    cq = reduction(normed_c, grad_query[:, None], "zxy")
+    advance(triple, values, cq)
+    out = reduction(low_first, mixed_a[:, None], "zyx")
+    advance(kv, cq, out)
+    send_hidden, keep_hidden, sums_a = run(
+        lambda grad: hidden_backward(own_index, grad, hidden, grad_first, vec, weights), grad_triple
+    )
+    got_hidden = swap("tp", 0, chain.tie(send_hidden)[0])
+
+    halves = lambda row: row.reshape(columns, width)
+    gains = [halves(sums[0]) for sums in (sums_a, sums_c, sums_m)]
+    shifts = [halves(sums[1]) for sums in (sums_a, sums_c, sums_m)]
+    sums = jnp.stack(
+        gains
+        + shifts
+        + [
+            sums_self[:, 0],
+            sums_self[:, 1],
+            halves(sums_c[2]),
+            sums_cross[:, 0],
+            sums_cross[:, 1],
+            halves(sums_m[2]),
+            halves(sums_m[3]),
+        ],
+        axis=1,
+    )
+    totals = jnp.concatenate([sums, up_sums[:, :, 0]], axis=1)
+    def spread(totals, bit):
+        return totals + chain.hold(swap("dp", bit, totals))
+
+    totals = spread(totals, 0)
+    advance(triple, values)
+    encoder_grad = join_frames(own_index, keep_frames, *got_frames, frames.shape[1])
+    chain.token = encoder_grad
+    advance(out, cq)
+    hidden_grad = pair_up(keep_hidden, chain.hold(got_hidden)).reshape(columns * tokens, width)
+    chain.hold(hidden_grad)
+    for bit in range(1, bits):
+        totals = spread(totals, bit)
+        advance(triple, values, out, cq)
+    totals = pick(totals, own, 0) + swap("tp", 0, pick(totals, 1 - own, 0))
+    encoder_grad = encoder_grad.transpose(1, 0, 2)
+    own_qkv = jnp.concatenate([triple.finish(), values.finish()])
+    own_ckv, own_cq, own_out = kv.finish(), cq.finish(), out.finish()
+    own_down, own_up, own_co = down.finish(), up.finish(), co.finish()
+
+    return (
+        output,
+        hidden_grad,
+        encoder_grad,
+        own_qkv.transpose(1, 0, 2),
+        own_out[0].T,
+        own_cq[0],
+        own_ckv.transpose(1, 0, 2),
+        own_co[0].T,
+        own_up.transpose(1, 0, 2).reshape(rows, blocks * width),
+        own_down.transpose(0, 2, 1).reshape(blocks * width, rows),
+        totals[:3],
+        totals[3:13],
+        totals[13:].reshape(blocks * width),
+    )
 
 
 def to_heads(matrix, groups):
@@ -390,6 +1546,16 @@
         P(None, "tp"),
         P("tp"),
     )
+    columns, shards = mesh.shape["tp"], mesh.shape["dp"]
+    powers = columns & (columns - 1) == 0 and shards & (shards - 1) == 0
+
+    def device_step(*arrays):
+        seqs = arrays[2].shape[0]
+        wide = arrays[0].shape[1] % LANES == 0
+        if powers and wide and columns == 2 and seqs % columns == 0 and shards >= 8:
+            return per_device_whole_sequences(*arrays)
+        return per_device(*arrays)
+
     return jax.shard_map(
-        per_device, mesh=mesh, in_specs=in_specs, out_specs=out_specs, check_vma=False
-    )
+        device_step, mesh=mesh, in_specs=in_specs, out_specs=out_specs, check_vma=False
+    )

time: 2220 us -> 839 us (0.38)
  blocking collectives: 621 us -> 0 us
  matrix products: 607 us -> 0 us
  Pallas kernels: 0 us -> 512 us
  waiting for transfers between devices: 526 us -> 170 us
  local copies, waits for them, and re-layouts: 244 us -> 64 us
  other arithmetic: 178 us -> 15.6 us
  starting transfers between devices: 11.7 us -> 50.3 us
    dot_general x132 -> x0, matrix products: 607 us -> none  [the longest x8 89 us: attend_backward(): jnp.einsum('sqhe,skhe->shqk', grad_mixed, value_rows, preferred_element_t...]
    pallas_call x0 -> x53, Pallas kernels: none -> 512 us  [the longest x8 87.6 us: weight_grad(): pl.pallas_call(functools.partial(weight_kernel, plan, frames), grid_spec=...]
    all_gather x36 -> x0, blocking collectives: 459 us -> none  [the longest x12 172 us: spread_grad(): lax.all_gather(incoming.astype(jnp.bfloat16), 'tp', axis=1, tiled=True)]
    reduce_scatter x22 -> x0, waiting for transfers between devices: 459 us -> none  [the longest x4 170 us: per_device(): lax.psum_scatter(frame_partial.astype(jnp.bfloat16), 'tp', scatter_dimens...]
    psum x12 -> x0, blocking collectives: 132 us -> none  [the longest x1 61.3 us: per_device(): vector_totals = lax.psum((gain_terms, bias_terms, upbias_terms), 'dp')]
    ppermute x0 -> x52, waiting for transfers between devices: none -> 110 us  [swap(): return lax.ppermute(value, axis, [(d, d ^ 1 << bit) for d in range(size)])]
    slice x42 -> x9, local copies, waits for them, and re-layouts: 113 us -> 5.09 us  [the longest x1 0.88 us: per_device_whole_sequences(): sums_c[2]]
    convert_element_type x21 -> x0, other arithmetic: 98.3 us -> none  [the longest x8 80.1 us: attend_backward(): grad_scores = (weights * (grad_weights - inner)).astype(jnp.bfloat16)]
  transfers between devices with their start and end apart: 32 -> 54, of which waited for: 15 -> 16; matrix products, arithmetic and copies ran while one was open for 29% -> 6% of each run, Pallas kernels for 0% -> 51%
where the time goes in v1:
time: 839 us; the launch traced here: 828 us
  Pallas kernels  512 us (61%)
  waiting for transfers between devices  170 us (20%)
  local copies, waits for them, and re-layouts  64 us (8%)
  starting transfers between devices  50.3 us (6%)
  other arithmetic  15.6 us (2%)
  between operations  15.1 us (2%)
    ppermute x52, waiting for transfers between devices, swap(): return lax.ppermute(value, axis, [(d, d ^ 1 << bit) for d in range(size)])  110 us
    pallas_call x8, Pallas kernels, weight_grad(): pl.pallas_call(functools.partial(weight_kernel, plan, frames), grid_spec=...  87.6 us
    pallas_call x32, Pallas kernels, add_and_cut(): pl.pallas_call(cut_kernel, grid=(rows // step,), in_specs=[in_spec, in_sp...  80.8 us
    all_gather x2, waiting for transfers between devices, gather(): full = lax.all_gather(part, ('tp', 'dp'), axis=0)  60.2 us
    pallas_call x1, Pallas kernels, attend_cross_back(): pl.pallas_call(cross_back_kernel, grid=(columns, pairs, seqs), in_specs=[...  57.4 us
    pallas_call x1, Pallas kernels, attend_cross(): pl.pallas_call(cross_kernel, grid=(columns, pairs, seqs), in_specs=[pl.Bl...  52.4 us
    ppermute x52, starting transfers between devices, swap(): return lax.ppermute(value, axis, [(d, d ^ 1 << bit) for d in range(size)])  50.2 us
    pallas_call x1, Pallas kernels, mlp_forward(): pl.pallas_call(mlp_kernel, grid_spec=pltpu.PrefetchScalarGridSpec(num_sca...  44 us
  transfers between devices with their start and end apart: 54, of which 16 were waited for; matrix products, arithmetic and copies ran while one was open for 6% of the time, Pallas kernels for 51%

profile of v1, /device:TPU:0, one launch (start us, length us, event | category | flops | bytes accessed | tf_op | source)
XLA Modules:
  0.0 827.8 jit_solution(8718512124020508734)
XLA Ops:
  16.2 3.0 collective-permute-start
  19.3 2.5 constant_dynamic-slice_fusion.1
  21.8 2.0 collective-permute-start.3
  23.9 10.0 %constant_dynamic-slice_fusion.2 = bf16[2,1500,1024]{2,0,1:T(2,128)(2,1)} fusion(bf16[4,1500,1024]{2,0,1:T(4,128)(2,1)} %param.15, s32[]{:T(128)S(6)} %select_n.70), kind=kLoop, calls=%fused_computation.31 | loop fusion | bytes 12288004 | tf_op jit(solution)/shard_map/dynamic_slice | solution.py:1040
  36.0 7.3 copy.108.frames_ref.left_ref
  50.5 21.4 %collective-permute-done.3 = bf16[896,512]{1,0:T(8,128)(2,1)} collective-permute-done((bf16[896,512]{1,0:T(8,128)(2,1)}, bf16[896,512]{1,0:T(8,128)(2,1)}, u32[]{:S(2)}, u32[]{:S(2)}) %collective-permute-start.3) | collective-permute-done | bytes 917536 | tf_op jit(solution)/shard_map/ppermute | solution.py:917
  71.8 3.4 maximum_select_fusion.2.left_ref.grad_ref
  75.2 60.2 %all-gather.5.cloned.1.call-done = bf16[256,64,512]{2,1,0:T(8,128)(2,1)} async-done(((bf16[8,64,512]{2,1,0:T(8,128)(2,1)}), bf16[256,64,512]{2,1,0:T(8,128)(2,1)}) %all-gather.5.cloned.1.call-update) | async-done | bytes 16777232 | tf_op jit(solution)/shard_map/all_gather | solution.py:1014
  135.4 12.1 %project_qkv.1 = (bf16[2,3,896,512]{3,2,1,0:T(8,128)(2,1)}, bf16[896,1024]{1,0:T(8,128)(2,1)}) custom-call(bf16[896,1024]{1,0:T(8,128)(2,1)} %maximum_select_fusion.1.hidden_ref, f32[16,1024]{1,0:T(8,128)} %concatenate.37.vec_ref, bf16[2,16,8,64,512]{4,3,2,1,0:T(8,128)(2,1)} %bitcast.233, f32[2,3,1,512]{3,2,1,0:T(1,128)} %copy.89.bias_ref), custom_call_target="tpu_custom_call" | custom-call | flops 1 | bytes 1 | tf_op jit(solution)/shard_map/project_qkv/pallas_call | solution.py:131
  147.5 23.6 %attend_self.1 = (bf16[2,896,512]{2,1,0:T(8,128)(2,1)}, bf16[2,4,2,2,448,448]{5,4,3,2,1,0:T(8,128)(2,1)}) custom-call(bf16[2,3,896,512]{3,2,1,0:T(8,128)(2,1)} %get-tuple-element.324.q_ref.k_ref.v_ref, bf16[2,3,896,512]{3,2,1,0:T(8,128)(2,1)} %get-tuple-element.324.q_ref.k_ref.v_ref, bf16[2,3,896,512]{3,2,1,0:T(8,128)(2,1)} %get-tuple-element.324.q_ref.k_ref.v_ref, ...), custom_call_target="tpu_custom_call" | custom-call | flops 1 | bytes 1 | tf_op jit(solution)/shard_map/attend_self/pallas_call | solution.py:202
  171.2 11.7 %project_out.1 = (f32[896,1024]{1,0:T(8,128)}, bf16[896,1024]{1,0:T(8,128)(2,1)}, bf16[2,896,512]{2,1,0:T(8,128)(2,1)}) custom-call(bf16[2,896,512]{2,1,0:T(8,128)(2,1)} %get-tuple-element.242.mixed_ref, bf16[896,1024]{1,0:T(8,128)(2,1)} %maximum_select_fusion.1.hidden_ref, f32[16,1024]{1,0:T(8,128)} %concatenate.37.vec_ref, ...), custom_call_target="tpu_custom_call" | custom-call | flops 1 | bytes 1 | tf_op jit(solution)/shard_map/project_out/pallas_call | solution.py:255
  182.9 18.7 %project_pair.1.kv_ref = bf16[2,2,2,1500,512]{4,3,2,1,0:T(8,128)(2,1)} custom-call(s32[1]{0:T(128)} %bitcast.own_ref, bf16[2,1500,1024]{2,1,0:T(8,128)(2,1)} %copy.108.frames_ref.left_ref, bf16[2,16,8,64,512]{4,3,2,1,0:T(8,128)(2,1)} %bitcast.236, f32[2,2,1,512]{3,2,1,0:T(1,128)} %copy.92.bias_ref), custom_call_target="tpu_custom_call" | custom-call | flops 1 | bytes 1 | tf_op jit(solution)/shard_map/project_pair/pallas_call | solution.py:290
  201.6 52.4 %attend_cross.1 = (bf16[2,896,512]{2,1,0:T(8,128)(2,1)}, bf16[2,4,2,2,1500,448]{5,4,3,2,1,0:T(8,128)(2,1)}) custom-call(bf16[2,896,512]{2,1,0:T(8,128)(2,1)} %get-tuple-element.276.q_ref, bf16[2,2,2,1500,512]{4,3,2,1,0:T(8,128)(2,1)} %project_pair.1.kv_ref), custom_call_target="tpu_custom_call" | custom-call | flops 1 | bytes 1 | tf_op jit(solution)/shard_map/attend_cross/pallas_call | solution.py:316
  253.9 44.0 %mlp_forward.1 = (f32[896,1024]{1,0:T(8,128)}, bf16[896,1024]{1,0:T(8,128)(2,1)}, bf16[2,4,896,512]{3,2,1,0:T(8,128)(2,1)}, bf16[2,4,896,512]{3,2,1,0:T(8,128)(2...) custom-call(s32[1]{0:T(128)} %bitcast.own_ref, bf16[2,896,512]{2,1,0:T(8,128)(2,1)} %get-tuple-element.244.mixed_ref, ...), custom_call_target="tpu_custom_call" | custom-call | flops 1 | bytes 1 | tf_op jit(solution)/shard_map/mlp_forward/pallas_call | solution.py:412
  297.9 15.4 %weight_grad.8 = (bf16[2,2,4,4,64,512]{5,4,3,2,1,0:T(8,128)(2,1)}, bf16[2,2,4,4,64,512]{5,4,3,2,1,0:T(8,128)(2,1)}) custom-call(s32[17]{0:T(128)} %pad_add_fusion.place_ref, bf16[896,1024]{1,0:T(8,128)(2,1)} %maximum_select_fusion.2.left_ref.grad_ref, bf16[2,4,896,512]{3,2,1,0:T(8,128)(2,1)} %get-tuple-element.249.right_ref), custom_call_target="tpu_custom_call" | custom-call | flops 1 | bytes 1 | tf_op jit(solution)/shard_map/weight_grad/pallas_call | solution.py:843
  315.1 31.4 %mlp_backward.1 = (bf16[2,4,896,512]{3,2,1,0:T(8,128)(2,1)}, f32[2,4,1,512]{3,2,1,0:T(1,128)}, f32[896,1024]{1,0:T(8,128)}, bf16[896,1024]{1,0:T(8,128)(2,1)}, f...) custom-call(bf16[896,1024]{1,0:T(8,128)(2,1)} %maximum_select_fusion.2.left_ref.grad_ref, ...), custom_call_target="tpu_custom_call" | custom-call | flops 1 | bytes 1 | tf_op jit(solution)/shard_map/mlp_backward/pallas_call | solution.py:484
  346.6 2.0 copy-done.2
  348.5 5.2 add_and_cut.32
  353.7 15.2 %weight_grad.9 = (bf16[2,2,4,4,64,512]{5,4,3,2,1,0:T(8,128)(2,1)}, bf16[2,2,4,4,64,512]{5,4,3,2,1,0:T(8,128)(2,1)}) custom-call(s32[17]{0:T(128)} %pad_add_fusion.place_ref, bf16[896,1024]{1,0:T(8,128)(2,1)} %get-tuple-element.257.left_ref, bf16[2,4,896,512]{3,2,1,0:T(8,128)(2,1)} %get-tuple-element.263.right_ref), custom_call_target="tpu_custom_call" | custom-call | flops 1 | bytes 1 | tf_op jit(solution)/shard_map/weight_grad/pallas_call | solution.py:843
  369.8 6.6 weight_grad.10
  376.4 2.0 copy-done.3
  378.4 5.2 add_and_cut.33
  384.7 57.4 %attend_cross_back.1 = (bf16[2,896,512]{2,1,0:T(8,128)(2,1)}, bf16[2,2,2,1500,512]{4,3,2,1,0:T(8,128)(2,1)}, f32[2,8,512]{2,1,0:T(8,128)}) custom-call(bf16[2,896,512]{2,1,0:T(8,128)(2,1)} %get-tuple-element.276.q_ref, bf16[2,2,2,1500,512]{4,3,2,1,0:T(8,128)(2,1)} %project_pair.1.kv_ref, bf16[2,896,512]{2,1,0:T(8,128)(2,1)} %get-tuple-element.244.mixed_ref, ...), custom_call_target="tpu_custom_call" | custom-call | flops 1 | bytes 1 | tf_op jit(solution)/shard_map/attend_cross_back/pallas_call | solution.py:540
  442.2 3.8 add_and_cut.34
  448.1 3.8 add_and_cut.35
  454.2 2.6 add_and_cut.36
  457.4 24.3 %frames_backward.1 = (bf16[2,1504,512]{2,1,0:T(8,128)(2,1)}, bf16[2,1504,512]{2,1,0:T(8,128)(2,1)}) custom-call(s32[1]{0:T(128)} %bitcast.own_ref, bf16[2,2,2,1500,512]{4,3,2,1,0:T(8,128)(2,1)} %get-tuple-element.309.grad_ref.right_ref, bf16[2,16,8,64,512]{4,3,2,1,0:T(8,128)(2,1)} %bitcast.239), custom_call_target="tpu_custom_call" | custom-call | flops 1 | bytes 1 | tf_op jit(solution)/shard_map/frames_backward/pallas_call | solution.py:748
  482.6 2.7 add_and_cut.37
  486.3 3.0 add_and_cut.38
  490.1 2.0 add_and_cut.39
  496.8 21.1 %weight_grad.11 = (bf16[2,4,2,2,64,512]{5,4,3,2,1,0:T(8,128)(2,1)}, bf16[2,4,2,2,64,512]{5,4,3,2,1,0:T(8,128)(2,1)}) custom-call(s32[17]{0:T(128)} %pad_add_fusion.place_ref, bf16[2,1500,1024]{2,1,0:T(8,128)(2,1)} %copy.108.frames_ref.left_ref, bf16[2,2,2,1500,512]{4,3,2,1,0:T(8,128)(2,1)} %get-tuple-element.309.grad_ref.right_ref), custom_call_target="tpu_custom_call" | custom-call | flops 1 | bytes 1 | tf_op jit(solution)/shard_map/weight_grad/pallas_call | solution.py:843
  517.9 9.8 %collective-permute-done.15.refs_0_ = bf16[1,1504,512]{2,1,0:T(8,128)(2,1)S(1)} collective-permute-done((bf16[1,1504,512]{2,1,0:T(8,128)(2,1)S(1)}, bf16[1,1504,512]{2,1,0:T(8,128)(2,1)S(1)}, u32[]{:S(2)}, u32[]{:S(2)}) %collective-permute-start.15) | collective-permute-done | bytes 1540128 | tf_op jit(solution)/shard_map/ppermute | solution.py:917
  527.7 15.6 %query_backward.1 = (f32[896,1024]{1,0:T(8,128)}, bf16[896,1024]{1,0:T(8,128)(2,1)}, f32[8,1024]{1,0:T(8,128)}, bf16[2,896,512]{2,1,0:T(8,128)(2,1)}) custom-call(bf16[2,896,512]{2,1,0:T(8,128)(2,1)} %get-tuple-element.312.grad_ref, f32[896,1024]{1,0:T(8,128)} %get-tuple-element.245.first_ref, f32[896,1024]{1,0:T(8,128)} %get-tuple-element.313.second_ref, ...), custom_call_target="tpu_custom_call" | custom-call | flops 1 | bytes 1 | tf_op jit(solution)/shard_map/query_backward/pallas_call | solution.py:649
  544.1 2.1 add_and_cut.40
  547.0 2.1 add_and_cut.41
  553.6 25.4 %attend_self_back.1 = (bf16[2,3,896,512]{3,2,1,0:T(8,128)(2,1)}, f32[2,8,512]{2,1,0:T(8,128)}) custom-call(bf16[2,3,896,512]{3,2,1,0:T(8,128)(2,1)} %get-tuple-element.324.q_ref.k_ref.v_ref, bf16[2,3,896,512]{3,2,1,0:T(8,128)(2,1)} %get-tuple-element.324.q_ref.k_ref.v_ref, bf16[2,3,896,512]{3,2,1,0:T(8,128)(2,1)} %get-tuple-element.324.q_ref.k_ref.v_ref, ...), custom_call_target="tpu_custom_call" | custom-call | flops 1 | bytes 1 | tf_op jit(solution)/shard_map/attend_self_back/pallas_call | solution.py:588
  579.0 11.5 %collective-permute-done.17 = bf16[2,1,64,512]{3,2,0,1:T(8,128)(2,1)S(1)} collective-permute-done((bf16[2,1,64,512]{3,2,0,1:T(8,128)(2,1)}, bf16[2,1,64,512]{3,2,0,1:T(8,128)(2,1)S(1)}, u32[]{:S(2)}, u32[]{:S(2)}) %collective-permute-start.17) | collective-permute-done | bytes 131104 | tf_op jit(solution)/shard_map/ppermute | solution.py:917
  594.1 3.8 add_and_cut.44
  598.5 9.5 %weight_grad.12 = (bf16[2,2,4,2,64,512]{5,4,3,2,1,0:T(8,128)(2,1)}, bf16[2,2,4,2,64,512]{5,4,3,2,1,0:T(8,128)(2,1)}) custom-call(s32[17]{0:T(128)} %pad_add_fusion.place_ref, bf16[896,1024]{1,0:T(8,128)(2,1)} %get-tuple-element.340.left_ref, bf16[2,3,896,512]{3,2,1,0:T(8,128)(2,1)} %get-tuple-element.373.right_ref.grad_ref), custom_call_target="tpu_custom_call" | custom-call | flops 1 | bytes 1 | tf_op jit(solution)/shard_map/weight_grad/pallas_call | solution.py:843
  608.0 6.5 weight_grad.13
  614.5 8.4 %collective-permute-done.18 = bf16[2,2,2,2,64,512]{5,4,3,2,1,0:T(8,128)(2,1)S(1)} collective-permute-done((bf16[2,2,2,2,64,512]{5,4,3,2,1,0:T(8,128)(2,1)}, bf16[2,2,2,2,64,512]{5,4,3,2,1,0:T(8,128)(2,1)S(1)}, u32[]{:S(2)}, u32[]{:S(2)}) %collective-permute-start.18) | collective-permute-done | bytes 1048608 | tf_op jit(solution)/shard_map/ppermute | solution.py:917
  623.8 2.7 add_and_cut.45
  627.1 6.6 weight_grad.14
  635.0 3.8 add_and_cut.46
  639.9 2.7 add_and_cut.47
  644.8 6.6 weight_grad.15
  651.4 5.7 collective-permute-done.23
  657.9 2.1 add_and_cut.48
  660.9 2.6 add_and_cut.49
  664.9 15.9 %hidden_backward.1 = (bf16[896,512]{1,0:T(8,128)(2,1)}, f32[896,512]{1,0:T(8,128)}, f32[8,1024]{1,0:T(8,128)}) custom-call(s32[1]{0:T(128)} %bitcast.own_ref, bf16[2,3,896,512]{3,2,1,0:T(8,128)(2,1)} %get-tuple-element.373.right_ref.grad_ref, bf16[896,1024]{1,0:T(8,128)(2,1)} %maximum_select_fusion.1.hidden_ref, f32[896,1024]{1,0:T(8,128)} %get-tuple-element.314.first_ref, ...), custom_call_target="tpu_custom_call" | custom-call | flops 1 | bytes 1 | tf_op jit(solution)/shard_map/hidden_backward/pallas_call | solution.py:700
  687.4 2.6 add_and_cut.52
  692.1 11.3 %join_frames.1 = f32[1500,4,512]{2,1,0:T(4,128)} custom-call(s32[1]{0:T(128)} %bitcast.own_ref, bf16[2,1504,512]{2,1,0:T(8,128)(2,1)} %get-tuple-element.380.keep_ref, bf16[1,1504,512]{2,1,0:T(8,128)(2,1)} %copy-done.10, bf16[1,1504,512]{2,1,0:T(8,128)(2,1)} %copy-done.11), custom_call_target="tpu_custom_call" | custom-call | flops 1 | bytes 1 | tf_op jit(solution)/shard_map/join_frames/pallas_call | solution.py:899
  704.4 2.6 add_and_cut.50
  709.0 2.0 add_and_cut.54
  716.7 2.0 add_and_cut.53
  723.4 2.0 add_and_cut.51
  727.8 2.0 add_and_cut.56
  732.6 16.2 %collective-permute-done.33 = bf16[2,2,1,64,512]{4,3,1,0,2:T(8,128)(2,1)S(1)} collective-permute-done((bf16[2,2,1,64,512]{4,3,1,0,2:T(8,128)(2,1)}, bf16[2,2,1,64,512]{4,3,1,0,2:T(8,128)(2,1)S(1)}, u32[]{:S(2)}, u32[]{:S(2)}) %collective-permute-start.33) | collective-permute-done | bytes 262176 | tf_op jit(solution)/shard_map/ppermute | solution.py:917
  755.0 2.3 collective-permute-start.37
  757.4 2.4 maximum_select_fusion
  762.1 2.4 collective-permute-start.49
  769.4 3.6 collective-permute-done.37
  773.0 23.1 %collective-permute-done.42 = bf16[1,64,512]{2,1,0:T(8,128)(2,1)S(1)} collective-permute-done((bf16[1,64,512]{2,1,0:T(8,128)(2,1)}, bf16[1,64,512]{2,1,0:T(8,128)(2,1)S(1)}, u32[]{:S(2)}, u32[]{:S(2)}) %collective-permute-start.42) | collective-permute-done | bytes 65568 | tf_op jit(solution)/shard_map/ppermute | solution.py:917
  802.2 3.8 collective-permute-done.43
  (296 shorter events, 114.8 us)
Async XLA Ops:
  7.2 128.2 %all-gather.5.cloned.1.call-start = ((), (), s32[]{:S(2)}) async-start(), calls=%async_computation | async-start | bytes 17301504 | tf_op jit(solution)/shard_map/all_gather | solution.py:1014
  12.5 241.4 %all-gather.7.cloned.1.call-start = ((), (), s32[]{:S(2)}) async-start(), calls=%async_computation.1 | async-start | bytes 17301504 | tf_op jit(solution)/shard_map/all_gather | solution.py:1014
  16.2 32.5 %collective-permute-start = (bf16[896,512]{1,0:T(8,128)(2,1)}, bf16[896,512]{1,0:T(8,128)(2,1)S(1)}, u32[]{:S(2)}, u32[]{:S(2)}) collective-permute-start(bf16[896,512]{1,0:T(8,128)(2,1)} %get-tuple-element.474), channel_id=1, source_target_pairs={{0,1},{1,0},{2,3},{3,2},{4,5},{5,4},{6,7},{7,6},{8,9},{9,8},{10,11... | collective-permute-start | bytes 2752520 | tf_op jit(solution)/shard_map/ppermute | solution.py:917
  19.2 26.1 %collective-permute-start.1 = (f32[17,512]{1,0:T(8,128)S(1)}, f32[17,512]{1,0:T(8,128)S(1)}, u32[]{:S(2)}, u32[]{:S(2)}) collective-permute-start(f32[17,512]{1,0:T(8,128)S(1)} %get-tuple-element.480), channel_id=1, source_target_pairs={{0,1},{1,0},{2,3},{3,2},{4,5},{5,4},{6,7},{7,6},{8,9},{9,8},{10,11... | collective-permute-start | bytes 104456 | tf_op jit(solution)/shard_map/ppermute | solution.py:917
  21.8 50.0 %collective-permute-start.3 = (bf16[896,512]{1,0:T(8,128)(2,1)}, bf16[896,512]{1,0:T(8,128)(2,1)}, u32[]{:S(2)}, u32[]{:S(2)}) collective-permute-start(bf16[896,512]{1,0:T(8,128)(2,1)} %get-tuple-element.472), channel_id=1, source_target_pairs={{0,1},{1,0},{2,3},{3,2},{4,5},{5,4},{6,7},{7,6},{8,9},{9,8},{10,11... | collective-permute-start | bytes 2752520 | tf_op jit(solution)/shard_map/ppermute | solution.py:917
  313.3 33.3 %collective-permute-start.4 = (bf16[2,2,2,2,4,64,512]{6,5,4,3,2,1,0:T(8,128)(2,1)}, bf16[2,2,2,2,4,64,512]{6,5,4,3,2,1,0:T(8,128)(2,1)S(1)}, u32[]{:S(2)}, u32[]{:S(2)}) collective-permute-start(bf16[2,2,2,2,4,64,512]{6,5,4,3,2,1,0:T(8,128)(2,1)} %bitcast.344), channel_id=1, source_target_pairs={{0,2},{2,0},{4,6},{6,4},{8,10},{10,8},{12,14},{14,12},{16,18},{18,... | collective-permute-start | bytes 12582920 | tf_op jit(solution)/shard_map/ppermute | solution.py:917
  313.6 32.9 %collective-permute-start.2 = (bf16[896,512]{1,0:T(8,128)(2,1)S(1)}, bf16[896,512]{1,0:T(8,128)(2,1)S(1)}, u32[]{:S(2)}, u32[]{:S(2)}) collective-permute-start(bf16[896,512]{1,0:T(8,128)(2,1)S(1)} %copy-done.57), channel_id=1, source_target_pairs={{0,1},{1,0},{2,3},{3,2},{4,5},{5,4},{6,7},{7,6},{8,9},{9,8},{10,11... | collective-permute-start | bytes 2752520 | tf_op jit(solution)/shard_map/ppermute | solution.py:917
  346.5 22.4 %copy-start.22 = (bf16[896,512]{1,0:T(8,128)(2,1)}, bf16[896,512]{1,0:T(8,128)(2,1)S(1)}, u32[]{:S(2)}) copy-start(bf16[896,512]{1,0:T(8,128)(2,1)S(1)} %collective-permute-done.2) | copy-start | bytes 2752516
  369.0 7.4 collective-permute-start.5
  369.0 73.2 %collective-permute-start.8 = (bf16[2,2,2,4,64,512]{5,4,3,2,1,0:T(8,128)(2,1)}, bf16[2,2,2,4,64,512]{5,4,3,2,1,0:T(8,128)(2,1)}, u32[]{:S(2)}, u32[]{:S(2)}) collective-permute-start(bf16[2,2,2,4,64,512]{5,4,3,2,1,0:T(8,128)(2,1)} %bitcast.347), channel_id=1, source_target_pairs={{0,4},{2,6},{4,0},{6,2},{8,12},{10,14},{12,8},{14,10},{16,20},{18,... | collective-permute-start | bytes 6291464 | tf_op jit(solution)/shard_map/ppermute | solution.py:917
  383.6 63.2 %collective-permute-start.7 = (bf16[2,2,2,4,64,512]{5,4,3,2,1,0:T(8,128)(2,1)}, bf16[2,2,2,4,64,512]{5,4,3,2,1,0:T(8,128)(2,1)S(1)}, u32[]{:S(2)}, u32[]{:S(2)}) collective-permute-start(bf16[2,2,2,4,64,512]{5,4,3,2,1,0:T(8,128)(2,1)} %bitcast.348), channel_id=1, source_target_pairs={{0,1},{1,0},{2,3},{3,2},{4,5},{5,4},{6,7},{7,6},{8,9},{9,8},{10,11... | collective-permute-start | bytes 6291464 | tf_op jit(solution)/shard_map/ppermute | solution.py:917
  384.7 68.5 %collective-permute-start.6 = (bf16[2,2,2,2,1,64,512]{6,5,3,2,1,0,4:T(8,128)(2,1)}, bf16[2,2,2,2,1,64,512]{6,5,3,2,1,0,4:T(8,128)(2,1)S(1)}, u32[]{:S(2)}, u32[]{:S(2)}) collective-permute-start(bf16[2,2,2,2,1,64,512]{6,5,3,2,1,0,4:T(8,128)(2,1)} %bitcast.28), channel_id=1, source_target_pairs={{0,2},{2,0},{4,6},{6,4},{8,10},{10,8},{12,14},{14,12},{16,18},{18,... | collective-permute-start | bytes 3145736 | tf_op jit(solution)/shard_map/ppermute | solution.py:917
  445.9 35.7 %collective-permute-start.11 = (bf16[2,2,4,64,512]{4,3,2,1,0:T(8,128)(2,1)}, bf16[2,2,4,64,512]{4,3,2,1,0:T(8,128)(2,1)S(1)}, u32[]{:S(2)}, u32[]{:S(2)}) collective-permute-start(bf16[2,2,4,64,512]{4,3,2,1,0:T(8,128)(2,1)} %bitcast.351), channel_id=1, source_target_pairs={{0,1},{1,0},{2,3},{3,2},{4,5},{5,4},{6,7},{7,6},{8,9},{9,8},{10,11... | collective-permute-start | bytes 3145736 | tf_op jit(solution)/shard_map/ppermute | solution.py:917
  452.0 33.4 %collective-permute-start.10 = (bf16[2,2,4,64,512]{4,3,2,1,0:T(8,128)(2,1)}, bf16[2,2,4,64,512]{4,3,2,1,0:T(8,128)(2,1)S(1)}, u32[]{:S(2)}, u32[]{:S(2)}) collective-permute-start(bf16[2,2,4,64,512]{4,3,2,1,0:T(8,128)(2,1)} %bitcast.352), channel_id=1, source_target_pairs={{0,4},{2,6},{4,0},{6,2},{8,12},{10,14},{12,8},{14,10},{16,20},{18,... | collective-permute-start | bytes 3145736 | tf_op jit(solution)/shard_map/ppermute | solution.py:917
  456.8 32.5 %collective-permute-start.9 = (bf16[2,2,2,1,64,512]{5,4,2,1,0,3:T(8,128)(2,1)}, bf16[2,2,2,1,64,512]{5,4,2,1,0,3:T(8,128)(2,1)S(1)}, u32[]{:S(2)}, u32[]{:S(2)}) collective-permute-start(bf16[2,2,2,1,64,512]{5,4,2,1,0,3:T(8,128)(2,1)} %bitcast.356), channel_id=1, source_target_pairs={{0,8},{2,10},{4,12},{6,14},{8,0},{10,2},{12,4},{14,6},{16,24},{18,... | collective-permute-start | bytes 1572872 | tf_op jit(solution)/shard_map/ppermute | solution.py:917
  492.4 35.3 %collective-permute-start.15 = (bf16[1,1504,512]{2,1,0:T(8,128)(2,1)S(1)}, bf16[1,1504,512]{2,1,0:T(8,128)(2,1)S(1)}, u32[]{:S(2)}, u32[]{:S(2)}) collective-permute-start(bf16[1,1504,512]{2,1,0:T(8,128)(2,1)S(1)} %get-tuple-element.470), channel_id=1, source_target_pairs={{0,1},{1,0},{2,3},{3,2},{4,5},{5,4},{6,7},{7,6},{8,9},{9,8},{10,11... | collective-permute-start | bytes 4620296 | tf_op jit(solution)/shard_map/ppermute | solution.py:917
  493.0 50.3 %collective-permute-start.14 = (bf16[2,4,64,512]{3,2,1,0:T(8,128)(2,1)}, bf16[2,4,64,512]{3,2,1,0:T(8,128)(2,1)S(1)}, u32[]{:S(2)}, u32[]{:S(2)}) collective-permute-start(bf16[2,4,64,512]{3,2,1,0:T(8,128)(2,1)} %bitcast.50), channel_id=1, source_target_pairs={{0,8},{2,10},{4,12},{6,14},{8,0},{10,2},{12,4},{14,6},{16,24},{18,... | collective-permute-start | bytes 1572872 | tf_op jit(solution)/shard_map/ppermute | solution.py:917
  494.5 51.7 %collective-permute-start.13 = (bf16[2,4,64,512]{3,2,1,0:T(8,128)(2,1)}, bf16[2,4,64,512]{3,2,1,0:T(8,128)(2,1)S(1)}, u32[]{:S(2)}, u32[]{:S(2)}) collective-permute-start(bf16[2,4,64,512]{3,2,1,0:T(8,128)(2,1)} %bitcast.53), channel_id=1, source_target_pairs={{0,8},{2,10},{4,12},{6,14},{8,0},{10,2},{12,4},{14,6},{16,24},{18,... | collective-permute-start | bytes 1572872 | tf_op jit(solution)/shard_map/ppermute | solution.py:917
  495.0 54.0 %collective-permute-start.12 = (bf16[2,2,1,64,512]{4,3,1,0,2:T(8,128)(2,1)}, bf16[2,2,1,64,512]{4,3,1,0,2:T(8,128)(2,1)S(1)}, u32[]{:S(2)}, u32[]{:S(2)}) collective-permute-start(bf16[2,2,1,64,512]{4,3,1,0,2:T(8,128)(2,1)} %bitcast.57), channel_id=1, source_target_pairs={{0,16},{2,18},{4,20},{6,22},{8,24},{10,26},{12,28},{14,30},{16,0},... | collective-permute-start | bytes 786440 | tf_op jit(solution)/shard_map/ppermute | solution.py:917
  551.5 41.2 %collective-permute-start.16 = (bf16[2,2,2,2,2,64,512]{6,5,4,3,2,1,0:T(8,128)(2,1)}, bf16[2,2,2,2,2,64,512]{6,5,4,3,2,1,0:T(8,128)(2,1)S(1)}, u32[]{:S(2)}, u32[]{:S(2)}) collective-permute-start(bf16[2,2,2,2,2,64,512]{6,5,4,3,2,1,0:T(8,128)(2,1)} %bitcast.346), channel_id=1, source_target_pairs={{0,2},{2,0},{4,6},{6,4},{8,10},{10,8},{12,14},{14,12},{16,18},{18,... | collective-permute-start | bytes 6291464 | tf_op jit(solution)/shard_map/ppermute | solution.py:917
  551.5 62.9 %collective-permute-start.19 = (bf16[1,1504,512]{2,1,0:T(8,128)(2,1)S(1)}, bf16[1,1504,512]{2,1,0:T(8,128)(2,1)S(1)}, u32[]{:S(2)}, u32[]{:S(2)}) collective-permute-start(bf16[1,1504,512]{2,1,0:T(8,128)(2,1)S(1)} %get-tuple-element.469), channel_id=1, source_target_pairs={{0,1},{1,0},{2,3},{3,2},{4,5},{5,4},{6,7},{7,6},{8,9},{9,8},{10,11... | collective-permute-start | bytes 4620296 | tf_op jit(solution)/shard_map/ppermute | solution.py:917
  552.1 38.4 %collective-permute-start.17 = (bf16[2,1,64,512]{3,2,0,1:T(8,128)(2,1)}, bf16[2,1,64,512]{3,2,0,1:T(8,128)(2,1)S(1)}, u32[]{:S(2)}, u32[]{:S(2)}) collective-permute-start(bf16[2,1,64,512]{3,2,0,1:T(8,128)(2,1)} %bitcast.368), channel_id=1, source_target_pairs={{0,1},{1,0},{2,3},{3,2},{4,5},{5,4},{6,7},{7,6},{8,9},{9,8},{10,11... | collective-permute-start | bytes 393224 | tf_op jit(solution)/shard_map/ppermute | solution.py:917
  597.8 25.0 %collective-permute-start.18 = (bf16[2,2,2,2,64,512]{5,4,3,2,1,0:T(8,128)(2,1)}, bf16[2,2,2,2,64,512]{5,4,3,2,1,0:T(8,128)(2,1)S(1)}, u32[]{:S(2)}, u32[]{:S(2)}) collective-permute-start(bf16[2,2,2,2,64,512]{5,4,3,2,1,0:T(8,128)(2,1)} %bitcast.353), channel_id=1, source_target_pairs={{0,4},{2,6},{4,0},{6,2},{8,12},{10,14},{12,8},{14,10},{16,20},{18,... | collective-permute-start | bytes 3145736 | tf_op jit(solution)/shard_map/ppermute | solution.py:917
  614.5 19.2 %copy-start.11 = (bf16[1,1504,512]{2,1,0:T(8,128)(2,1)}, bf16[1,1504,512]{2,1,0:T(8,128)(2,1)S(1)}, u32[]{:S(2)}) copy-start(bf16[1,1504,512]{2,1,0:T(8,128)(2,1)S(1)} %collective-permute-done.19.refs_1_) | copy-start | bytes 4620292
  626.6 7.1 collective-permute-start.21
  626.6 12.3 %collective-permute-start.20 = (bf16[2,2,2,2,1,64,512]{6,5,3,2,1,0,4:T(8,128)(2,1)}, bf16[2,2,2,2,1,64,512]{6,5,3,2,1,0,4:T(8,128)(2,1)S(1)}, u32[]{:S(2)}, u32[]{:S(2)}) collective-permute-start(bf16[2,2,2,2,1,64,512]{6,5,3,2,1,0,4:T(8,128)(2,1)} %bitcast.86), channel_id=1, source_target_pairs={{0,2},{2,0},{4,6},{6,4},{8,10},{10,8},{12,14},{14,12},{16,18},{18,... | collective-permute-start | bytes 3145736 | tf_op jit(solution)/shard_map/ppermute | solution.py:917
  642.5 17.4 %collective-permute-start.22 = (bf16[2,2,2,2,1,64,512]{6,5,3,2,1,0,4:T(8,128)(2,1)S(1)}, bf16[2,2,2,2,1,64,512]{6,5,3,2,1,0,4:T(8,128)(2,1)S(1)}, u32[]{:S(2)}, u32[]{:S(2)}) collective-permute-start(bf16[2,2,2,2,1,64,512]{6,5,3,2,1,0,4:T(8,128)(2,1)S(1)} %bitcast.350), channel_id=1, source_target_pairs={{0,2},{2,0},{4,6},{6,4},{8,10},{10,8},{12,14},{14,12},{16,18},{18,... | collective-permute-start | bytes 3145736 | tf_op jit(solution)/shard_map/ppermute | solution.py:917
  642.5 14.5 %collective-permute-start.23 = (bf16[2,2,2,64,512]{4,3,2,1,0:T(8,128)(2,1)}, bf16[2,2,2,64,512]{4,3,2,1,0:T(8,128)(2,1)S(1)}, u32[]{:S(2)}, u32[]{:S(2)}) collective-permute-start(bf16[2,2,2,64,512]{4,3,2,1,0:T(8,128)(2,1)} %bitcast.82), channel_id=1, source_target_pairs={{0,8},{2,10},{4,12},{6,14},{8,0},{10,2},{12,4},{14,6},{16,24},{18,... | collective-permute-start | bytes 1572872 | tf_op jit(solution)/shard_map/ppermute | solution.py:917
  644.1 42.3 %collective-permute-start.27 = (bf16[2,2,2,2,64,512]{5,4,3,2,1,0:T(8,128)(2,1)S(1)}, bf16[2,2,2,2,64,512]{5,4,3,2,1,0:T(8,128)(2,1)S(1)}, u32[]{:S(2)}, u32[]{:S(2)}) collective-permute-start(bf16[2,2,2,2,64,512]{5,4,3,2,1,0:T(8,128)(2,1)S(1)} %bitcast.349), channel_id=1, source_target_pairs={{0,4},{2,6},{4,0},{6,2},{8,12},{10,14},{12,8},{14,10},{16,20},{18,... | collective-permute-start | bytes 3145736 | tf_op jit(solution)/shard_map/ppermute | solution.py:917
  663.6 39.9 %collective-permute-start.26 = (bf16[2,2,2,2,1,64,512]{6,5,3,2,1,0,4:T(8,128)(2,1)}, bf16[2,2,2,2,1,64,512]{6,5,3,2,1,0,4:T(8,128)(2,1)S(1)}, u32[]{:S(2)}, u32[]{:S(2)}) collective-permute-start(bf16[2,2,2,2,1,64,512]{6,5,3,2,1,0,4:T(8,128)(2,1)} %bitcast.106), channel_id=1, source_target_pairs={{0,2},{2,0},{4,6},{6,4},{8,10},{10,8},{12,14},{14,12},{16,18},{18,... | collective-permute-start | bytes 3145736 | tf_op jit(solution)/shard_map/ppermute | solution.py:917
  664.4 43.2 %collective-permute-start.35 = (bf16[2,2,2,1,64,512]{5,4,2,1,0,3:T(8,128)(2,1)}, bf16[2,2,2,1,64,512]{5,4,2,1,0,3:T(8,128)(2,1)}, u32[]{:S(2)}, u32[]{:S(2)}) collective-permute-start(bf16[2,2,2,1,64,512]{5,4,2,1,0,3:T(8,128)(2,1)} %bitcast.94), channel_id=1, source_target_pairs={{0,1},{1,0},{2,3},{3,2},{4,5},{5,4},{6,7},{7,6},{8,9},{9,8},{10,11... | collective-permute-start | bytes 1572872 | tf_op jit(solution)/shard_map/ppermute | solution.py:917
  680.8 44.6 %collective-permute-start.24 = (bf16[896,512]{1,0:T(8,128)(2,1)}, bf16[896,512]{1,0:T(8,128)(2,1)}, u32[]{:S(2)}, u32[]{:S(2)}) collective-permute-start(bf16[896,512]{1,0:T(8,128)(2,1)} %get-tuple-element.376), channel_id=1, source_target_pairs={{0,1},{1,0},{2,3},{3,2},{4,5},{5,4},{6,7},{7,6},{8,9},{9,8},{10,11... | collective-permute-start | bytes 2752520 | tf_op jit(solution)/shard_map/ppermute | solution.py:917
  685.0 1.4 collective-permute-start.28
  690.0 25.2 %collective-permute-start.29 = (bf16[2,2,2,64,512]{4,3,2,1,0:T(8,128)(2,1)}, bf16[2,2,2,64,512]{4,3,2,1,0:T(8,128)(2,1)}, u32[]{:S(2)}, u32[]{:S(2)}) collective-permute-start(bf16[2,2,2,64,512]{4,3,2,1,0:T(8,128)(2,1)} %bitcast.355), channel_id=1, source_target_pairs={{0,1},{1,0},{2,3},{3,2},{4,5},{5,4},{6,7},{7,6},{8,9},{9,8},{10,11... | collective-permute-start | bytes 1572872 | tf_op jit(solution)/shard_map/ppermute | solution.py:917
  690.6 32.0 %collective-permute-start.25 = (bf16[2,2,2,1,64,512]{5,4,2,1,0,3:T(8,128)(2,1)}, bf16[2,2,2,1,64,512]{5,4,2,1,0,3:T(8,128)(2,1)S(1)}, u32[]{:S(2)}, u32[]{:S(2)}) collective-permute-start(bf16[2,2,2,1,64,512]{5,4,2,1,0,3:T(8,128)(2,1)} %bitcast.102), channel_id=1, source_target_pairs={{0,8},{2,10},{4,12},{6,14},{8,0},{10,2},{12,4},{14,6},{16,24},{18,... | collective-permute-start | bytes 1572872 | tf_op jit(solution)/shard_map/ppermute | solution.py:917
  707.1 19.9 %collective-permute-start.34 = (bf16[2,2,2,1,64,512]{5,4,2,1,0,3:T(8,128)(2,1)}, bf16[2,2,2,1,64,512]{5,4,2,1,0,3:T(8,128)(2,1)S(1)}, u32[]{:S(2)}, u32[]{:S(2)}) collective-permute-start(bf16[2,2,2,1,64,512]{5,4,2,1,0,3:T(8,128)(2,1)} %bitcast.354), channel_id=1, source_target_pairs={{0,8},{2,10},{4,12},{6,14},{8,0},{10,2},{12,4},{14,6},{16,24},{18,... | collective-permute-start | bytes 1572872 | tf_op jit(solution)/shard_map/ppermute | solution.py:917
  707.6 4.7 collective-permute-start.30
  712.3 7.0 collective-permute-start.36
  715.2 37.4 %collective-permute-start.32 = (f32[2,17,512]{2,1,0:T(8,128)S(1)}, f32[2,17,512]{2,1,0:T(8,128)S(1)}, u32[]{:S(2)}, u32[]{:S(2)}) collective-permute-start(f32[2,17,512]{2,1,0:T(8,128)S(1)} %add.81), channel_id=1, source_target_pairs={{0,8},{2,10},{4,12},{6,14},{8,0},{10,2},{12,4},{14,6},{16,24},{18,... | collective-permute-start | bytes 208904 | tf_op jit(solution)/shard_map/ppermute | solution.py:917
  719.3 33.3 %collective-permute-start.31 = (bf16[2,2,64,512]{3,2,1,0:T(8,128)(2,1)}, bf16[2,2,64,512]{3,2,1,0:T(8,128)(2,1)S(1)}, u32[]{:S(2)}, u32[]{:S(2)}) collective-permute-start(bf16[2,2,64,512]{3,2,1,0:T(8,128)(2,1)} %bitcast.360), channel_id=1, source_target_pairs={{0,8},{2,10},{4,12},{6,14},{8,0},{10,2},{12,4},{14,6},{16,24},{18,... | collective-permute-start | bytes 786440 | tf_op jit(solution)/shard_map/ppermute | solution.py:917
  722.6 37.2 %collective-permute-start.41 = (bf16[2,1,64,512]{3,2,0,1:T(8,128)(2,1)}, bf16[2,1,64,512]{3,2,0,1:T(8,128)(2,1)S(1)}, u32[]{:S(2)}, u32[]{:S(2)}) collective-permute-start(bf16[2,1,64,512]{3,2,0,1:T(8,128)(2,1)} %bitcast.364), channel_id=1, source_target_pairs={{0,8},{2,10},{4,12},{6,14},{8,0},{10,2},{12,4},{14,6},{16,24},{18,... | collective-permute-start | bytes 393224 | tf_op jit(solution)/shard_map/ppermute | solution.py:917
  725.4 23.4 %collective-permute-start.33 = (bf16[2,2,1,64,512]{4,3,1,0,2:T(8,128)(2,1)}, bf16[2,2,1,64,512]{4,3,1,0,2:T(8,128)(2,1)S(1)}, u32[]{:S(2)}, u32[]{:S(2)}) collective-permute-start(bf16[2,2,1,64,512]{4,3,1,0,2:T(8,128)(2,1)} %bitcast.363), channel_id=1, source_target_pairs={{0,16},{2,18},{4,20},{6,22},{8,24},{10,26},{12,28},{14,30},{16,0},... | collective-permute-start | bytes 786440 | tf_op jit(solution)/shard_map/ppermute | solution.py:917
  729.8 27.5 %copy-start.9 = (f32[896,512]{1,0:T(8,128)S(1)}, f32[896,512]{1,0:T(8,128)}, u32[]{:S(2)}) copy-start(f32[896,512]{1,0:T(8,128)} %get-tuple-element.374) | copy-start | bytes 5505028
  729.8 32.3 %collective-permute-start.40 = (bf16[2,2,1,64,512]{4,3,1,0,2:T(8,128)(2,1)}, bf16[2,2,1,64,512]{4,3,1,0,2:T(8,128)(2,1)S(1)}, u32[]{:S(2)}, u32[]{:S(2)}) collective-permute-start(bf16[2,2,1,64,512]{4,3,1,0,2:T(8,128)(2,1)} %bitcast.361), channel_id=1, source_target_pairs={{0,16},{2,18},{4,20},{6,22},{8,24},{10,26},{12,28},{14,30},{16,0},... | collective-permute-start | bytes 786440 | tf_op jit(solution)/shard_map/ppermute | solution.py:917
  751.2 15.0 %collective-permute-start.39 = (bf16[2,1,64,512]{3,2,0,1:T(8,128)(2,1)}, bf16[2,1,64,512]{3,2,0,1:T(8,128)(2,1)S(1)}, u32[]{:S(2)}, u32[]{:S(2)}) collective-permute-start(bf16[2,1,64,512]{3,2,0,1:T(8,128)(2,1)} %bitcast.366), channel_id=1, source_target_pairs={{0,4},{2,6},{4,0},{6,2},{8,12},{10,14},{12,8},{14,10},{16,20},{18,... | collective-permute-start | bytes 393224 | tf_op jit(solution)/shard_map/ppermute | solution.py:917
  752.6 16.1 %collective-permute-start.38 = (f32[2,17,512]{2,1,0:T(8,128)S(1)}, f32[2,17,512]{2,1,0:T(8,128)S(1)}, u32[]{:S(2)}, u32[]{:S(2)}) collective-permute-start(f32[2,17,512]{2,1,0:T(8,128)S(1)} %add.82), channel_id=1, source_target_pairs={{0,16},{2,18},{4,20},{6,22},{8,24},{10,26},{12,28},{14,30},{16,0},... | collective-permute-start | bytes 208904 | tf_op jit(solution)/shard_map/ppermute | solution.py:917
  755.0 18.0 %collective-permute-start.37 = (bf16[2,64,512]{2,1,0:T(8,128)(2,1)}, bf16[2,64,512]{2,1,0:T(8,128)(2,1)S(1)}, u32[]{:S(2)}, u32[]{:S(2)}) collective-permute-start(bf16[2,64,512]{2,1,0:T(8,128)(2,1)} %bitcast.367), channel_id=1, source_target_pairs={{0,16},{2,18},{4,20},{6,22},{8,24},{10,26},{12,28},{14,30},{16,0},... | collective-permute-start | bytes 393224 | tf_op jit(solution)/shard_map/ppermute | solution.py:917
  757.4 40.2 %copy-start.45 = (bf16[128,512]{1,0:T(8,128)(2,1)S(1)}, bf16[128,512]{1,0:T(8,128)(2,1)}, u32[]{:S(2)}) copy-start(bf16[128,512]{1,0:T(8,128)(2,1)} %get-tuple-element.423) | copy-start | bytes 393220
  759.8 54.8 %collective-permute-start.50 = (bf16[4,64,512]{2,1,0:T(8,128)(2,1)S(1)}, bf16[4,64,512]{2,1,0:T(8,128)(2,1)S(1)}, u32[]{:S(2)}, u32[]{:S(2)}) collective-permute-start(bf16[4,64,512]{2,1,0:T(8,128)(2,1)S(1)} %bitcast.357), channel_id=1, source_target_pairs={{0,16},{2,18},{4,20},{6,22},{8,24},{10,26},{12,28},{14,30},{16,0},... | collective-permute-start | bytes 786440 | tf_op jit(solution)/shard_map/ppermute | solution.py:917
  762.1 53.7 %copy-start.39 = (bf16[256,512]{1,0:T(8,128)(2,1)S(1)}, bf16[256,512]{1,0:T(8,128)(2,1)}, u32[]{:S(2)}) copy-start(bf16[256,512]{1,0:T(8,128)(2,1)} %get-tuple-element.466) | copy-start | bytes 786436
  762.1 52.4 %collective-permute-start.49 = (bf16[4,64,512]{2,1,0:T(8,128)(2,1)S(1)}, bf16[4,64,512]{2,1,0:T(8,128)(2,1)S(1)}, u32[]{:S(2)}, u32[]{:S(2)}) collective-permute-start(bf16[4,64,512]{2,1,0:T(8,128)(2,1)S(1)} %bitcast.358), channel_id=1, source_target_pairs={{0,16},{2,18},{4,20},{6,22},{8,24},{10,26},{12,28},{14,30},{16,0},... | collective-permute-start | bytes 786440 | tf_op jit(solution)/shard_map/ppermute | solution.py:917
  766.2 34.5 %copy-start.61 = (bf16[128,512]{1,0:T(8,128)(2,1)S(1)}, bf16[128,512]{1,0:T(8,128)(2,1)}, u32[]{:S(2)}) copy-start(bf16[128,512]{1,0:T(8,128)(2,1)} %get-tuple-element.433) | copy-start | bytes 393220
  766.2 49.5 %collective-permute-start.48 = (bf16[1,64,512]{2,1,0:T(8,128)(2,1)S(1)}, bf16[1,64,512]{2,1,0:T(8,128)(2,1)S(1)}, u32[]{:S(2)}, u32[]{:S(2)}) collective-permute-start(bf16[1,64,512]{2,1,0:T(8,128)(2,1)S(1)} %bitcast.369), channel_id=1, source_target_pairs={{0,4},{2,6},{4,0},{6,2},{8,12},{10,14},{12,8},{14,10},{16,20},{18,... | collective-permute-start | bytes 196616 | tf_op jit(solution)/shard_map/ppermute | solution.py:917
  768.7 37.3 %copy-start.63 = (bf16[64,512]{1,0:T(8,128)(2,1)S(1)}, bf16[64,512]{1,0:T(8,128)(2,1)}, u32[]{:S(2)}) copy-start(bf16[64,512]{1,0:T(8,128)(2,1)} %get-tuple-element.436) | copy-start | bytes 196612
  768.7 42.2 %collective-permute-start.45 = (bf16[2,2,64,512]{3,2,1,0:T(8,128)(2,1)S(1)}, bf16[2,2,64,512]{3,2,1,0:T(8,128)(2,1)S(1)}, u32[]{:S(2)}, u32[]{:S(2)}) collective-permute-start(bf16[2,2,64,512]{3,2,1,0:T(8,128)(2,1)S(1)} %bitcast.359), channel_id=1, source_target_pairs={{0,16},{2,18},{4,20},{6,22},{8,24},{10,26},{12,28},{14,30},{16,0},... | collective-permute-start | bytes 786440 | tf_op jit(solution)/shard_map/ppermute | solution.py:917
  769.4 46.5 %copy-start.40 = (bf16[256,512]{1,0:T(8,128)(2,1)S(1)}, bf16[256,512]{1,0:T(8,128)(2,1)}, u32[]{:S(2)}) copy-start(bf16[256,512]{1,0:T(8,128)(2,1)} %get-tuple-element.463) | copy-start | bytes 786436
  773.0 23.1 %collective-permute-start.42 = (bf16[1,64,512]{2,1,0:T(8,128)(2,1)}, bf16[1,64,512]{2,1,0:T(8,128)(2,1)S(1)}, u32[]{:S(2)}, u32[]{:S(2)}) collective-permute-start(bf16[1,64,512]{2,1,0:T(8,128)(2,1)} %bitcast.372), channel_id=1, source_target_pairs={{0,16},{2,18},{4,20},{6,22},{8,24},{10,26},{12,28},{14,30},{16,0},... | collective-permute-start | bytes 196616 | tf_op jit(solution)/shard_map/ppermute | solution.py:917
  796.1 4.6 collective-permute-start.51
  798.5 17.5 %copy-start.48 = (bf16[64,512]{1,0:T(8,128)(2,1)S(1)}, bf16[64,512]{1,0:T(8,128)(2,1)}, u32[]{:S(2)}) copy-start(bf16[64,512]{1,0:T(8,128)(2,1)} %get-tuple-element.460) | copy-start | bytes 196612
  798.5 17.5 %copy-start.49 = (bf16[64,512]{1,0:T(8,128)(2,1)S(1)}, bf16[64,512]{1,0:T(8,128)(2,1)}, u32[]{:S(2)}) copy-start(bf16[64,512]{1,0:T(8,128)(2,1)} %get-tuple-element.454) | copy-start | bytes 196612
  800.7 5.3 collective-permute-start.43
  806.0 9.8 %collective-permute-start.46 = (bf16[1,64,512]{2,1,0:T(8,128)(2,1)S(1)}, bf16[1,64,512]{2,1,0:T(8,128)(2,1)S(1)}, u32[]{:S(2)}, u32[]{:S(2)}) collective-permute-start(bf16[1,64,512]{2,1,0:T(8,128)(2,1)S(1)} %bitcast.370), channel_id=1, source_target_pairs={{0,1},{1,0},{2,3},{3,2},{4,5},{5,4},{6,7},{7,6},{8,9},{9,8},{10,11... | collective-permute-start | bytes 196616 | tf_op jit(solution)/shard_map/ppermute | solution.py:917
  810.9 7.5 collective-permute-start.44
  814.5 5.0 collective-permute-start.47
  (54 other events, 213.7 us)
Sparse Core Ops, SparseCore 0:
  12.6 122.7 all-gather.4
  138.8 113.0 all-gather.6

commit v2 on v1

--- a/solution.py
+++ b/solution.py
@@ -21,8 +21,9 @@
 EPSILON = 1e-05
 NEGATIVE = -1e30
 
-QKV, CKV, OUT, CQ, CO = 0, 3, 5, 6, 7
+QKV, OUT, CKV, CQ, CO = 0, 3, 4, 6, 7
 VMEM_BYTES = 58 << 20
+SELF_LANES = 256
 
 
 def nn(a, b):
@@ -44,7 +45,10 @@
 
 
 def cost(flops, *arrays):
-    return pl.CostEstimate(flops=1, bytes_accessed=1, transcendentals=0)
+    time = (3e-6 + flops / 700e12) / 7
+    return pl.CostEstimate(
+        flops=int(time * 1153e12), bytes_accessed=int(time * 3690e9), transcendentals=0
+    )
 
 
 def struct(shape, dtype):
@@ -117,91 +121,118 @@
     row_loop(grad_ref.shape[0], body)
 
 
-def qkv_kernel(hidden_ref, vec_ref, w_ref, bias_ref, out_ref, normed_ref):
-    @pl.when((pl.program_id(0) == 0) & (pl.program_id(1) == 0))
-    def _():
-        write_norm(hidden_ref, normed_ref, vec_ref[0:1, :], vec_ref[3:4, :])
-
+def first_norm_kernel(hidden_ref, vec_ref, normed_ref):
+    write_norm(hidden_ref, normed_ref, vec_ref[0:1, :], vec_ref[3:4, :])
+
+
+def first_norm(hidden, vec):
+    return pl.pallas_call(
+        first_norm_kernel,
+        out_shape=struct(hidden.shape, BF),
+        compiler_params=pltpu.CompilerParams(vmem_limit_bytes=VMEM_BYTES),
+        cost_estimate=cost(0, hidden),
+        name="first_norm",
+    )(hidden, vec)
+
+
+def qkv_kernel(normed_ref, w_ref, bias_ref, out_ref):
     out_ref[0, 0] = (nn(normed_ref[...], weight(w_ref)) + bias_ref[0, 0]).astype(BF)
 
 
-def project_qkv(hidden, vec, gathered, bias):
+def project_qkv(normed, gathered, bias):
     columns, width = gathered.shape[0], gathered.shape[-1]
-    tokens = hidden.shape[0]
+    tokens = normed.shape[0]
     return pl.pallas_call(
         qkv_kernel,
         grid=(columns, 3),
         in_specs=[
-            whole(hidden),
-            whole(vec),
+            whole(normed),
             weight_spec(gathered, lambda y, c: (y, QKV + c)),
             pl.BlockSpec((1, 1, 1, width), lambda y, c: (y, c, 0, 0)),
         ],
-        out_specs=[
-            pl.BlockSpec((1, 1, tokens, width), lambda y, c: (y, c, 0, 0)),
-            whole(hidden),
-        ],
-        out_shape=[struct((columns, 3, tokens, width), BF), struct(hidden.shape, BF)],
+        out_specs=pl.BlockSpec((1, 1, tokens, width), lambda y, c: (y, c, 0, 0)),
+        out_shape=struct((columns, 3, tokens, width), BF),
         compiler_params=compiler_params(2),
-        cost_estimate=cost(2 * tokens * D * 3 * columns * width, hidden, hidden),
+        cost_estimate=cost(2 * tokens * D * 3 * columns * width, normed),
         name="project_qkv",
-    )(hidden, vec, gathered, bias)
-
-
-def head_row(head, value):
-    lane = lax.broadcasted_iota(jnp.int32, (1, LANES), 1)
+    )(normed, gathered, bias)
+
+
+def head_row(head, value, lanes):
+    lane = lax.broadcasted_iota(jnp.int32, (1, lanes), 1)
     inside = (lane >= head * HEAD_DIM) & (lane < (head + 1) * HEAD_DIM)
     return jnp.where(inside, value, 0.0).astype(BF)
 
 
-def attend(query, key_rows, value_rows, visible, mixed_ref, probs_ref):
-    parts = []
-    for head in range(LANES // HEAD_DIM):
-        scores = nt(key_rows, query * head_row(head, HEAD_DIM**-0.5))
-        if visible is not None:
-            scores = jnp.where(visible, scores, NEGATIVE)
-        weights = jnp.exp(scores - jnp.max(scores, axis=0, keepdims=True))
-        inverse = 1.0 / jnp.sum(weights, axis=0, keepdims=True)
-        probs = (weights * inverse).astype(BF)
-        probs_ref[0, 0, 0, head] = probs
-        part = tn(value_rows, probs)
-        parts.append(part[head * HEAD_DIM : (head + 1) * HEAD_DIM])
-    mixed_ref[0] = jnp.concatenate(parts, axis=0).T.astype(BF)
-
-
-def attend_back(query, key_rows, value_rows, mixed, grad_mixed, probs_ref):
-    grad_f = grad_mixed.astype(F32)
-    product = (grad_f * mixed.astype(F32)).T
-    parts, grad_key, grad_value = [], 0.0, 0.0
-    for head in range(LANES // HEAD_DIM):
+def by_head(parts):
+    lane = lax.broadcasted_iota(jnp.int32, (1, parts[0].shape[1]), 1)
+    value = parts[0]
+    for head in range(1, len(parts)):
+        value = jnp.where(lane >= head * HEAD_DIM, parts[head], value)
+    return value
+
+
+def attend(query, key_rows, value_rows, bias, mixed_ref, weights_ref, inverse_ref):
+    lanes = query.shape[1]
+    heads = lanes // HEAD_DIM
+    scores = []
+    for head in range(heads):
+        one = nt(query * head_row(head, HEAD_DIM**-0.5, lanes), key_rows)
+        scores.append(one if bias is None else one + bias)
+    mixed = []
+    for head in range(heads):
+        maximum = jnp.max(scores[head], axis=1, keepdims=True)
+        weights = jnp.exp(scores[head] - maximum).astype(BF)
+        weights_ref[0, 0, 0, head] = weights
+        own = head_row(head, 1.0, lanes)
+        mixed.append(nn(weights, value_rows * own + (1.0 - own.astype(F32)).astype(BF)))
+    sums = by_head([mixed[(head - 1) % heads] for head in range(heads)])
+    inverse = 1.0 / pltpu.roll(sums, lanes - HEAD_DIM, 1)
+    inverse_ref[0] = inverse
+    mixed_ref[0] = (by_head(mixed) * inverse).astype(BF)
+
+
+def attend_back(query, key_rows, value_rows, mixed, grad_mixed, weights_ref, inverse):
+    lanes = query.shape[1]
+    heads = lanes // HEAD_DIM
+    grad = (grad_mixed.astype(F32) * inverse).astype(BF)
+    product = grad.astype(F32) * mixed.astype(F32)
+    scaled = query * jnp.full((1, 1), HEAD_DIM**-0.5, BF)
+    grad_weights = [nt(grad * head_row(head, 1.0, lanes), value_rows) for head in range(heads)]
+    grad_query, grad_key, grad_value = [], [], []
+    for head in range(heads):
         span = slice(head * HEAD_DIM, (head + 1) * HEAD_DIM)
-        inner = jnp.sum(product[span], axis=0, keepdims=True)
-        own_grad = grad_mixed * head_row(head, 1.0)
-        probs = probs_ref[0, 0, 0, head]
-        grad_weights = nt(value_rows, own_grad)
-        grad_scores = (probs.astype(F32) * (grad_weights - inner)).astype(BF)
-        grad_key = grad_key + nn(grad_scores, query * head_row(head, HEAD_DIM**-0.5))
-        grad_value = grad_value + nn(probs, own_grad)
-        parts.append(tn(key_rows, grad_scores)[span])
-    grad_query = jnp.concatenate(parts, axis=0).T * HEAD_DIM**-0.5
-    return grad_query.astype(BF), grad_key.astype(BF), grad_value.astype(BF)
-
-
-def self_kernel(q_ref, k_ref, v_ref, row_ref, column_ref, mixed_ref, probs_ref):
-    visible = column_ref[0] <= row_ref[0]
-    attend(q_ref[0, 0], k_ref[0, 0], v_ref[0, 0], visible, mixed_ref, probs_ref)
+        own = product * head_row(head, 1.0, lanes).astype(F32)
+        inner = jnp.sum(own, axis=1, keepdims=True)
+        weights = weights_ref[0, 0, 0, head]
+        grad_value.append(tn(grad, weights)[span])
+        grad_scores = (weights.astype(F32) * (grad_weights[head] - inner)).astype(BF)
+        grad_query.append(nn(grad_scores, key_rows))
+        grad_key.append(tn(scaled, grad_scores)[span])
+    return (
+        (by_head(grad_query) * HEAD_DIM**-0.5).astype(BF),
+        jnp.concatenate(grad_key, axis=0).T.astype(BF),
+        jnp.concatenate(grad_value, axis=0).T.astype(BF),
+    )
+
+
+def self_kernel(q_ref, k_ref, v_ref, row_ref, column_ref, mixed_ref, weights_ref, inverse_ref):
+    bias = jnp.where(row_ref[0] <= column_ref[0], 0.0, NEGATIVE)
+    attend(q_ref[0, 0], k_ref[0, 0], v_ref[0, 0], bias, mixed_ref, weights_ref, inverse_ref)
 
 
 def attend_self(qkv, order_row, order_column):
     columns, _, tokens, width = qkv.shape
-    seqs, pairs = order_row.shape[0], width // LANES
+    seqs = order_row.shape[0]
+    lanes = SELF_LANES if width % SELF_LANES == 0 else LANES
+    groups, heads = width // lanes, lanes // HEAD_DIM
 
     def part(c):
-        return pl.BlockSpec((1, 1, LEN, LANES), lambda y, p, s: (y, c, s, p))
+        return pl.BlockSpec((1, 1, LEN, lanes), lambda y, p, s: (y, c, s, p))
 
     return pl.pallas_call(
         self_kernel,
-        grid=(columns, pairs, seqs),
+        grid=(columns, groups, seqs),
         in_specs=[
             part(0),
             part(1),
@@ -210,15 +241,17 @@
             pl.BlockSpec((1, LEN, 1), lambda y, p, s: (s, 0, 0)),
         ],
         out_specs=[
-            pl.BlockSpec((1, LEN, LANES), lambda y, p, s: (y, s, p)),
-            pl.BlockSpec((1, 1, 1, 2, LEN, LEN), lambda y, p, s: (y, p, s, 0, 0, 0)),
+            pl.BlockSpec((1, LEN, lanes), lambda y, p, s: (y, s, p)),
+            pl.BlockSpec((1, 1, 1, heads, LEN, LEN), lambda y, p, s: (y, p, s, 0, 0, 0)),
+            pl.BlockSpec((1, LEN, lanes), lambda y, p, s: (y, s, p)),
         ],
         out_shape=[
             struct((columns, tokens, width), BF),
-            struct((columns, pairs, seqs, 2, LEN, LEN), BF),
+            struct((columns, groups, seqs, heads, LEN, LEN), BF),
+            struct((columns, tokens, width), F32),
         ],
         compiler_params=compiler_params(3),
-        cost_estimate=cost(16 * columns * pairs * seqs * LEN * LEN * LANES, qkv),
+        cost_estimate=cost(16 * columns * width * seqs * LEN * LEN, qkv),
         name="attend_self",
     )(qkv, qkv, qkv, order_row, order_column)
 
@@ -306,8 +339,8 @@
     )(own, frames, gathered, bias)
 
 
-def cross_kernel(q_ref, kv_ref, mixed_ref, probs_ref):
-    attend(q_ref[0], kv_ref[0, 0, 0], kv_ref[0, 1, 0], None, mixed_ref, probs_ref)
+def cross_kernel(q_ref, kv_ref, mixed_ref, weights_ref, inverse_ref):
+    attend(q_ref[0], kv_ref[0, 0, 0], kv_ref[0, 1, 0], None, mixed_ref, weights_ref, inverse_ref)
 
 
 def attend_cross(query, pair):
@@ -322,35 +355,18 @@
         ],
         out_specs=[
             pl.BlockSpec((1, LEN, LANES), lambda y, p, s: (y, s, p)),
-            pl.BlockSpec((1, 1, 1, 2, length, LEN), lambda y, p, s: (y, p, s, 0, 0, 0)),
+            pl.BlockSpec((1, 1, 1, 2, LEN, length), lambda y, p, s: (y, p, s, 0, 0, 0)),
+            pl.BlockSpec((1, LEN, LANES), lambda y, p, s: (y, s, p)),
         ],
         out_shape=[
             struct((columns, tokens, width), BF),
-            struct((columns, pairs, seqs, 2, length, LEN), BF),
+            struct((columns, pairs, seqs, 2, LEN, length), BF),
+            struct((columns, tokens, width), F32),
         ],
         compiler_params=compiler_params(3),
         cost_estimate=cost(16 * columns * pairs * seqs * LEN * length * LANES, pair),
         name="attend_cross",
     )(query, pair)
-
-
-def erf(value):
-    x = jnp.clip(value, -3.832506856900711, 3.832506856900711)
-    square = x * x
-    top = jnp.full_like(x, 0.00022905065861350646)
-    for coefficient in (0.0034082910107109506, 0.050955695062380861, 0.18520832239976145, 1.128379143519084):
-        top = top * square + coefficient
-    bottom = jnp.full_like(x, -1.1791602954361697e-7)
-    for coefficient in (
-        0.000023547966471313185,
-        0.0010179625278914885,
-        0.014070470171167667,
-        0.11098505178285362,
-        0.49746925110067538,
-        1.0,
-    ):
-        bottom = bottom * square + coefficient
-    return x * top / bottom
 
 
 def halves_of(value, own):
@@ -380,13 +396,17 @@
 
     @pl.when(step >= columns)
     def _():
-        before = nn(normed_ref[...], weight(wu_ref)) + bias_ref[0, 0]
-        cdf = 0.5 + 0.5 * erf(before * (0.5**0.5))
-        density = jnp.exp(-0.5 * before * before) * (1.0 / math.sqrt(2.0 * math.pi))
-        act = (before * cdf).astype(BF)
-        act_ref[0, 0] = act
-        slope_ref[0, 0] = (cdf + before * density).astype(BF)
-        total_ref[...] += nt(act, weight(wd_ref))
+        up, down = weight(wu_ref), weight(wd_ref)
+        part = up.shape[1] // 2
+        spans = [slice(p * part, (p + 1) * part) for p in range(2)]
+        befores = [nn(normed_ref[...], up[:, span]) + bias_ref[0, 0, :, span] for span in spans]
+        for span, before in zip(spans, befores):
+            cdf = 0.5 + 0.5 * lax.erf(before * (0.5**0.5))
+            density = jnp.exp(-0.5 * before * before) * (1.0 / math.sqrt(2.0 * math.pi))
+            act = (before * cdf).astype(BF)
+            act_ref[0, 0, :, span] = act
+            slope_ref[0, 0, :, span] = (cdf + before * density).astype(BF)
+            total_ref[...] += nt(act, down[:, span])
 
     @pl.when(step == pl.num_programs(0) - 1)
     def _():
@@ -516,9 +536,11 @@
     )(grad, second, vec, gathered_mlp, gathered_mlp, gathered, slope)
 
 
-def cross_back_kernel(q_ref, kv_ref, mixed_ref, grad_ref, probs_ref, query_ref, pair_ref, sums_ref):
+def cross_back_kernel(
+    q_ref, kv_ref, mixed_ref, grad_ref, weights_ref, inverse_ref, query_ref, pair_ref, sums_ref
+):
     grad_query, grad_key, grad_value = attend_back(
-        q_ref[0], kv_ref[0, 0, 0], kv_ref[0, 1, 0], mixed_ref[0], grad_ref[0], probs_ref
+        q_ref[0], kv_ref[0, 0, 0], kv_ref[0, 1, 0], mixed_ref[0], grad_ref[0], weights_ref, inverse_ref[0]
     )
     query_ref[0] = grad_query
     pair_ref[0, 0, 0] = grad_key
@@ -532,7 +554,7 @@
     sums_ref[0, 1:2, :] += jnp.sum(grad_value.astype(F32), axis=0, keepdims=True)
 
 
-def attend_cross_back(query, pair, mixed, grad, probs):
+def attend_cross_back(query, pair, mixed, grad, weights, inverse):
     columns, tokens, width = query.shape
     seqs, length, pairs = pair.shape[2], pair.shape[3], width // LANES
     row_spec = pl.BlockSpec((1, LEN, LANES), lambda y, p, s: (y, s, p))
@@ -545,7 +567,8 @@
             pair_spec,
             row_spec,
             row_spec,
-            pl.BlockSpec((1, 1, 1, 2, length, LEN), lambda y, p, s: (y, p, s, 0, 0, 0)),
+            pl.BlockSpec((1, 1, 1, 2, LEN, length), lambda y, p, s: (y, p, s, 0, 0, 0)),
+            row_spec,
         ],
         out_specs=[row_spec, pair_spec, pl.BlockSpec((1, 8, LANES), lambda y, p, s: (y, 0, p))],
         out_shape=[
@@ -554,16 +577,16 @@
             struct((columns, 8, width), F32),
         ],
         compiler_params=compiler_params(3),
-        cost_estimate=cost(32 * columns * pairs * seqs * LEN * length * LANES, pair, pair, probs),
+        cost_estimate=cost(32 * columns * pairs * seqs * LEN * length * LANES, pair, pair),
         name="attend_cross_back",
-    )(query, pair, mixed, grad, probs)
+    )(query, pair, mixed, grad, weights, inverse)
 
 
 def self_back_kernel(
-    q_ref, k_ref, v_ref, mixed_ref, grad_ref, probs_ref, out_ref, sums_ref
+    q_ref, k_ref, v_ref, mixed_ref, grad_ref, weights_ref, inverse_ref, out_ref, sums_ref
 ):
     grad_query, grad_key, grad_value = attend_back(
-        q_ref[0, 0], k_ref[0, 0], v_ref[0, 0], mixed_ref[0], grad_ref[0], probs_ref
+        q_ref[0, 0], k_ref[0, 0], v_ref[0, 0], mixed_ref[0], grad_ref[0], weights_ref, inverse_ref[0]
     )
     out_ref[0, 0] = grad_query
     out_ref[0, 1] = grad_key
@@ -577,34 +600,36 @@
     sums_ref[0, 1:2, :] += jnp.sum(grad_value.astype(F32), axis=0, keepdims=True)
 
 
-def attend_self_back(qkv, mixed, grad, probs):
+def attend_self_back(qkv, mixed, grad, weights, inverse):
     columns, _, tokens, width = qkv.shape
-    seqs, pairs = probs.shape[2], width // LANES
-    row_spec = pl.BlockSpec((1, LEN, LANES), lambda y, p, s: (y, s, p))
+    groups, seqs, heads = weights.shape[1:4]
+    lanes = heads * HEAD_DIM
+    row_spec = pl.BlockSpec((1, LEN, lanes), lambda y, p, s: (y, s, p))
 
     def part(c):
-        return pl.BlockSpec((1, 1, LEN, LANES), lambda y, p, s: (y, c, s, p))
+        return pl.BlockSpec((1, 1, LEN, lanes), lambda y, p, s: (y, c, s, p))
 
     return pl.pallas_call(
         self_back_kernel,
-        grid=(columns, pairs, seqs),
+        grid=(columns, groups, seqs),
         in_specs=[
             part(0),
             part(1),
             part(2),
             row_spec,
             row_spec,
-            pl.BlockSpec((1, 1, 1, 2, LEN, LEN), lambda y, p, s: (y, p, s, 0, 0, 0)),
+            pl.BlockSpec((1, 1, 1, heads, LEN, LEN), lambda y, p, s: (y, p, s, 0, 0, 0)),
+            row_spec,
         ],
         out_specs=[
-            pl.BlockSpec((1, 3, LEN, LANES), lambda y, p, s: (y, 0, s, p)),
-            pl.BlockSpec((1, 8, LANES), lambda y, p, s: (y, 0, p)),
+            pl.BlockSpec((1, 3, LEN, lanes), lambda y, p, s: (y, 0, s, p)),
+            pl.BlockSpec((1, 8, lanes), lambda y, p, s: (y, 0, p)),
         ],
         out_shape=[struct(qkv.shape, BF), struct((columns, 8, width), F32)],
         compiler_params=compiler_params(3),
-        cost_estimate=cost(32 * columns * pairs * seqs * LEN * LEN * LANES, qkv, qkv, probs),
+        cost_estimate=cost(32 * columns * width * seqs * LEN * LEN, qkv, qkv),
         name="attend_self_back",
-    )(qkv, qkv, qkv, mixed, grad, probs)
+    )(qkv, qkv, qkv, mixed, grad, weights, inverse)
 
 
 def query_back_kernel(
@@ -674,15 +699,15 @@
 def hidden_back_kernel(
     own_ref, grad_ref, hidden_ref, first_ref, vec_ref, w_ref, send_ref, keep_ref, sums_ref, total_ref
 ):
-    step = pl.program_id(0)
-
-    @pl.when(step == 0)
-    def _():
-        total_ref[...] = jnp.zeros_like(total_ref)
-
-    total_ref[...] += nt(grad_ref[0, 0], weight(w_ref))
-
-    @pl.when(step == pl.num_programs(0) - 1)
+    part = total_ref.shape[1] // 2
+    product = nt(joined(grad_ref), weight_rows(w_ref))
+    for half in range(2):
+
+        @pl.when(pl.program_id(0) == half)
+        def _():
+            total_ref[:, half * part : (half + 1) * part] = product
+
+    @pl.when(pl.program_id(0) == 1)
     def _():
         def finish(rows, back):
             value = first_ref[rows, :] + back
@@ -696,18 +721,19 @@
 
 def hidden_backward(own, grad, hidden, grad_first, vec, gathered):
     columns, _, tokens, width = grad.shape
+    _, shards, _, rows, _ = gathered.shape
     sums, half = struct((8, D), F32), struct((tokens, width), F32)
     return pl.pallas_call(
         hidden_back_kernel,
         grid_spec=pltpu.PrefetchScalarGridSpec(
             num_scalar_prefetch=1,
-            grid=(3 * columns,),
+            grid=(2,),
             in_specs=[
-                pl.BlockSpec((1, 1, tokens, width), lambda i, own: (i // 3, i % 3, 0, 0)),
+                whole(grad),
                 whole(hidden),
                 whole(grad_first),
                 whole(vec),
-                weight_spec(gathered, lambda i, own: (i // 3, QKV + i % 3)),
+                pl.BlockSpec((columns, shards // 2, 3, rows, width), lambda i, own: (0, i, QKV, 0, 0)),
             ],
             out_specs=[whole(half), whole(half), whole(sums)],
             scratch_shapes=[pltpu.VMEM(hidden.shape, F32)],
@@ -719,43 +745,47 @@
     )(own, grad, hidden, grad_first, vec, gathered)
 
 
-def frames_back_kernel(own_ref, grad_ref, w_ref, send_ref, keep_ref, total_ref):
-    step = pl.program_id(1)
-    part = nt(grad_ref[0, 0, 0], weight(w_ref))
-
-    @pl.when(step == 0)
-    def _():
-        total_ref[...] = part
-
-    @pl.when(step > 0)
-    def _():
-        total_ref[...] += part
-
-    @pl.when(step == pl.num_programs(1) - 1)
-    def _():
-        send, keep = halves_of(total_ref[...], own_ref[0])
-        length, width = keep.shape
-        for ref, value in ((send_ref, send), (keep_ref, keep)):
-            ref[0, :length] = value.astype(BF)
+def joined(ref):
+    return jnp.concatenate([ref[y, c] for y in range(ref.shape[0]) for c in range(ref.shape[1])], axis=1)
+
+
+def weight_rows(ref):
+    columns, shards, blocks, rows, width = ref.shape
+    parts = [ref[y, :, c].reshape(shards * rows, width) for y in range(columns) for c in range(blocks)]
+    return jnp.concatenate(parts, axis=1)
+
+
+def frames_back_kernel(own_ref, grad_ref, w_ref, send_ref, keep_ref):
+    grad = jnp.concatenate([grad_ref[y, c, 0] for y in range(grad_ref.shape[0]) for c in range(2)], axis=1)
+    value = nt(grad, weight_rows(w_ref)).astype(BF)
+    length, width = value.shape
+    for part, ref in ((0, send_ref), (1, keep_ref)):
+
+        @pl.when(pl.program_id(1) == part)
+        def _():
+            ref[0, :length] = value
             ref[0, length:] = jnp.zeros((ref.shape[1] - length, width), BF)
 
 
 def frames_backward(own, grad, gathered):
     columns, _, seqs, length, width = grad.shape
-    padded = -(-length // 16) * 16
+    _, shards, _, rows, _ = gathered.shape
+    padded = -(-length // 32) * 32
     half = struct((seqs, padded, width), BF)
     half_spec = pl.BlockSpec((1, padded, width), lambda s, i, own: (s, 0, 0))
     return pl.pallas_call(
         frames_back_kernel,
         grid_spec=pltpu.PrefetchScalarGridSpec(
             num_scalar_prefetch=1,
-            grid=(seqs, 2 * columns),
+            grid=(seqs, 2),
             in_specs=[
-                pl.BlockSpec((1, 1, 1, length, width), lambda s, i, own: (i // 2, i % 2, s, 0, 0)),
-                weight_spec(gathered, lambda s, i, own: (i // 2, CKV + i % 2)),
+                pl.BlockSpec((columns, 2, 1, length, width), lambda s, i, own: (0, 0, s, 0, 0)),
+                pl.BlockSpec(
+                    (columns, shards // 2, 2, rows, width),
+                    lambda s, i, own: (0, jnp.where(i == 1, own[0], 1 - own[0]), CKV // 2, 0, 0),
+                ),
             ],
             out_specs=[half_spec, half_spec],
-            scratch_shapes=[pltpu.VMEM((length, columns * width), F32)],
         ),
         out_shape=[half, half],
         compiler_params=compiler_params(2),
@@ -792,103 +822,129 @@
         turned_ref[pl.ds(at, rows), :] = source[shard * rows : (shard + 1) * rows]
 
 
-def weight_kernel(plan, frames, place_ref, left_ref, right_ref, send_ref, keep_ref, turned_ref):
-    shards = 1 << plan.bits
-
-    @pl.when((pl.program_id(0) == 0) & (pl.program_id(1) == 0))
-    def _():
-        if frames:
-            for s in range(left_ref.shape[0]):
-                cut_rows(place_ref, left_ref[s].T, turned_ref.at[s], shards)
-        else:
-            cut_rows(place_ref, left_ref[...].T, turned_ref, shards)
-
-    if frames:
-        total = 0.0
-        for s in range(left_ref.shape[0]):
-            total = total + nn(turned_ref[s], right_ref[0, 0, s])
+def turn_kernel(bits, place_ref, source_ref, turned_ref):
+    cut_rows(place_ref, source_ref[0].T, turned_ref.at[0], 1 << bits)
+
+
+def turn(bits, place, source):
+    seqs, tokens, depth = source.shape
+    return pl.pallas_call(
+        functools.partial(turn_kernel, bits),
+        grid_spec=pltpu.PrefetchScalarGridSpec(
+            num_scalar_prefetch=1,
+            grid=(seqs,),
+            in_specs=[pl.BlockSpec((1, tokens, depth), lambda s, place: (s, 0, 0))],
+            out_specs=pl.BlockSpec((1, depth, tokens), lambda s, place: (s, 0, 0)),
+        ),
+        out_shape=struct((seqs, depth, tokens), BF),
+        compiler_params=compiler_params(1),
+        cost_estimate=cost(0, source),
+        name="turn",
+    )(place, source)
+
+
+def weight_kernel(plan, turned, place_ref, left_ref, right_ref, *refs):
+    if turned:
+        send_ref, keep_ref = refs[-2:]
+        lefts = [left_ref[s] for s in range(left_ref.shape[0])]
     else:
-        total = nn(turned_ref[...], right_ref[0, 0])
+        send_ref, keep_ref, turned_ref = refs[-3:]
+
+        @pl.when((pl.program_id(0) == 0) & (pl.program_id(1) == 0))
+        def _():
+            cut_rows(place_ref, left_ref[...].T, turned_ref, 1 << plan.bits)
+
+        lefts = [turned_ref[...]]
+    total = 0.0
+    for s, left in enumerate(lefts):
+        total = total + nn(left, right_ref[0, 0, s])
     half = total.shape[0] // 2
     plan.store(send_ref, total[:half].astype(BF))
     plan.store(keep_ref, total[half:].astype(BF))
 
 
-def weight_grad(plan, place, left, right, frames=False, first=0, count=None):
-    columns, blocks = right.shape[:2]
+def weight_grad(plan, place, left, right, first=0, count=None, at=0, room=None, into=()):
+    columns, blocks, seqs, tokens, width = right.shape
     blocks = count or blocks
-    width = right.shape[-1]
-    tokens = right.shape[-2]
-    seqs = right.shape[2] if frames else 1
     rows = D >> plan.bits
-    part = struct(plan.cuts + (blocks, rows, width), BF)
+    turned = len(left.shape) == 3
+    part = struct(plan.cuts + (room or blocks, rows, width), BF)
     out_spec = pl.BlockSpec(
         plan.block(0) + (1, rows, width),
-        lambda y, i, place: plan.place(y) + (i, 0, 0),
-    )
-
-    def column(y, place):
-        return jnp.where(y == 1, place[0], 1 - place[0])
-
-    if frames:
-        left_spec = whole(left)
-        right_spec = pl.BlockSpec(
-            (1, 1, seqs, tokens, width), lambda y, i, place: (column(y, place), first + i, 0, 0, 0)
-        )
-        turned = pltpu.VMEM((seqs, D, tokens), BF)
-    else:
-        left_spec = whole(left)
-        right_spec = pl.BlockSpec((1, 1, tokens, width), lambda y, i, place: (column(y, place), first + i, 0, 0))
-        turned = pltpu.VMEM((D, tokens), BF)
+        lambda y, i, place: plan.place(y) + (at + i, 0, 0),
+    )
+
+    def right_index(y, i, place):
+        return (jnp.where(y == 1, place[0], 1 - place[0]), first + i, 0, 0, 0)
+
     return pl.pallas_call(
-        functools.partial(weight_kernel, plan, frames),
+        functools.partial(weight_kernel, plan, turned),
         grid_spec=pltpu.PrefetchScalarGridSpec(
             num_scalar_prefetch=1,
             grid=(columns, blocks),
-            in_specs=[left_spec, right_spec],
+            in_specs=[whole(left), pl.BlockSpec((1, 1, seqs, tokens, width), right_index)]
+            + [pl.BlockSpec(memory_space=pl.ANY) for _ in into],
             out_specs=[out_spec, out_spec],
-            scratch_shapes=[turned],
+            scratch_shapes=[] if turned else [pltpu.VMEM((D, tokens), BF)],
         ),
         out_shape=[part, part],
+        input_output_aliases={3: 0, 4: 1} if into else {},
         compiler_params=compiler_params(2),
         cost_estimate=cost(2 * columns * blocks * seqs * tokens * width * D, right, part, part),
         name="weight_grad",
-    )(place, left, right)
-
-
-def cut_kernel(keep_ref, got_ref, send_ref, out_ref):
-    for part, ref in ((0, send_ref), (1, out_ref)):
-        ref[...] = (keep_ref[part].astype(F32) + got_ref[part].astype(F32)).astype(BF)
-
-
-def add_and_cut(keep, got):
-    shape = keep.shape[1:]
-    width = shape[-1]
-    rows = math.prod(shape[:-1])
-    step = math.gcd(rows, 1024)
-    flat = (2, rows, width)
-    out = struct((rows, width), BF)
-    in_spec = pl.BlockSpec((2, step, width), lambda i: (0, i, 0))
-    out_spec = pl.BlockSpec((step, width), lambda i: (i, 0))
-    send, own = pl.pallas_call(
-        cut_kernel,
-        grid=(rows // step,),
-        in_specs=[in_spec, in_spec],
-        out_specs=[out_spec, out_spec],
-        out_shape=[out, out],
+    )(place, left, right, *into)
+
+
+def cut_kernel(starts, *refs):
+    step, count = pl.program_id(0), len(starts) - 1
+    for p in range(count):
+        keep_ref, got_ref = refs[2 * p], refs[2 * p + 1]
+        outs = refs[2 * (count + p)], refs[2 * (count + p) + 1]
+
+        @pl.when((step >= starts[p]) & (step < starts[p + 1]))
+        def _():
+            for part in (0, 1):
+                outs[part][...] = keep_ref[part] + got_ref[part]
+
+
+def add_and_cut(pairs):
+    starts, arrays, in_specs, out_specs, outs = [0], [], [], [], []
+    for keep, got in pairs:
+        width = keep.shape[-1]
+        rows = math.prod(keep.shape[1:-1])
+        block = math.gcd(rows, 512)
+        begin, blocks = starts[-1], rows // block
+        starts.append(begin + blocks)
+
+        def index(i, begin=begin, blocks=blocks):
+            return jnp.clip(i - begin, 0, blocks - 1)
+
+        arrays += [keep.reshape(2, rows, width), got.reshape(2, rows, width)]
+        in_specs += [pl.BlockSpec((2, block, width), lambda i, index=index: (0, index(i), 0))] * 2
+        out_specs += [pl.BlockSpec((block, width), lambda i, index=index: (index(i), 0))] * 2
+        outs += [struct((rows, width), BF)] * 2
+    results = pl.pallas_call(
+        functools.partial(cut_kernel, tuple(starts)),
+        grid=(starts[-1],),
+        in_specs=in_specs,
+        out_specs=out_specs,
+        out_shape=outs,
         compiler_params=compiler_params(1),
-        cost_estimate=cost(0, keep, got, out, out),
+        cost_estimate=cost(0, *arrays),
         name="add_and_cut",
-    )(keep.reshape(flat), got.reshape(flat))
-    return send.reshape(shape), own.reshape(shape)
+    )(*arrays)
+    return [
+        tuple(r.reshape(keep.shape[1:]) for r in results[2 * p : 2 * p + 2])
+        for p, (keep, _) in enumerate(pairs)
+    ]
 
 
 def frames_join_kernel(own_ref, keep_ref, *refs):
     *got_refs, out_ref = refs
-    length, seqs = out_ref.shape[0], len(got_refs)
+    length, seqs = out_ref.shape[0], keep_ref.shape[0]
     for s in range(seqs):
         keep = keep_ref[s, :length].astype(F32)
-        got = got_refs[s][0, :length].astype(F32)
+        got = jnp.concatenate([got_refs[2 * s][0], got_refs[2 * s + 1][0]], axis=0)[:length].astype(F32)
         out_ref[:, s, :] = jnp.where(own_ref[0] == 0, keep, got)
         out_ref[:, seqs + s, :] = jnp.where(own_ref[0] == 0, got, keep)
 
@@ -902,7 +958,7 @@
             num_scalar_prefetch=1,
             grid=(width // LANES,),
             in_specs=[pl.BlockSpec((seqs, padded, LANES), lambda i, own: (0, 0, i))]
-            + [pl.BlockSpec((1, padded, LANES), lambda i, own: (0, 0, i))] * seqs,
+            + [pl.BlockSpec((1, padded // 2, LANES), lambda i, own: (0, 0, i))] * (2 * seqs),
             out_specs=pl.BlockSpec((length, 2 * seqs, LANES), lambda i, own: (0, 0, i)),
         ),
         out_shape=struct((length, 2 * seqs, width), F32),
@@ -950,35 +1006,36 @@
 
 
 class Reduction:
-    def __init__(self, chain, plan, place, left, right, **options):
-        self.chain, self.result = chain, None
+    def __init__(self, plan, parts):
+        self.result, self.got = None, None
         stages = {"x": [("dp", 1)], "y": [("tp", 0)], "z": [("dp", b) for b in range(2, plan.bits)]}
-        self.order = [stage for c in plan.order for stage in stages[c]]
-        (right,) = chain.tie(right)
-        send, keep = weight_grad(plan, place, left, right, **options)
-        chain.token = send
-        self.cuts = []
+        self.order = [("dp", 0)] + [stage for c in plan.order for stage in stages[c]]
+        cuts = []
         for c in plan.order:
-            self.cuts += [2] * len(stages[c])
-        shape = tuple(self.cuts) + send.shape[len(plan.cuts) :]
-        self.keep, self.first, self.got = keep.reshape(shape), send.reshape(shape), None
-
-    def step(self):
-        if self.got is None:
-            self.got = swap("dp", 0, self.chain.tie(self.first)[0])
-        elif self.order:
-            keep, got = self.chain.tie(self.keep, self.got)
-            send, self.keep = add_and_cut(keep, got)
-            self.chain.token = send
-            self.got = swap(*self.order.pop(0), send)
-        elif self.result is None:
-            keep, got = self.chain.tie(self.keep, self.got)
-            self.result = keep.astype(F32) + got.astype(F32)
-
-    def finish(self):
-        while self.result is None:
-            self.step()
-        return self.result
+            cuts += [2] * len(stages[c])
+        self.send, self.keep = (p.reshape(tuple(cuts) + p.shape[len(plan.cuts) :]) for p in parts)
+
+
+def launch(chain, reductions):
+    for one in reductions:
+        one.got = swap(*one.order.pop(0), chain.tie(one.send)[0])
+
+
+def advance(chain, *reductions):
+    open_ones = [one for one in reductions if one.got is not None and one.order]
+    if open_ones:
+        tied = chain.tie(*[a for one in open_ones for a in (one.keep, one.got)])
+        pieces = add_and_cut([tied[2 * i : 2 * i + 2] for i in range(len(open_ones))])
+        for one, (send, keep) in zip(open_ones, pieces):
+            one.send, one.keep = send, keep
+        chain.token = pieces[-1][0]
+    launch(chain, [one for one in reductions if one.order])
+
+
+def finish(chain, *reductions):
+    while any(one.order for one in reductions):
+        advance(chain, *[one for one in reductions if one.order])
+    return [one.keep.astype(F32) + one.got.astype(F32) for one in reductions]
 
 
 def per_device_whole_sequences(
@@ -995,8 +1052,8 @@
     attention_part = jnp.concatenate(
         [
             self_qkv.transpose(1, 0, 2),
+            self_out.T[None],
             cross_kv.transpose(1, 0, 2),
-            self_out.T[None],
             cross_query[None],
             cross_out.T[None],
         ]
@@ -1023,7 +1080,8 @@
             own == 0, jnp.concatenate([mine, got], axis=1), jnp.concatenate([got, mine], axis=1)
         )
 
-    hidden, grad_final = to_tokens(hidden_in), to_tokens(out_grad)
+    hidden = lax.optimization_barrier(to_tokens(hidden_in))
+    grad_final = lax.optimization_barrier(to_tokens(out_grad))
     small = jnp.concatenate([norm_gains, bias_rows, up_bias.reshape(blocks, width)])
     every = jnp.broadcast_to(small, (columns,) + small.shape)
     every = exchange(every, every)
@@ -1040,36 +1098,45 @@
         lax.dynamic_slice_in_dim(encoder_states, own * seqs, seqs, 0)
     )
 
-    qkv, normed_a = project_qkv(hidden, vec, weights, qkv_bias)
-    pair = project_pair(own_index, frames, weights, pair_bias, seqs)
-    mixed_a, probs_a = attend_self(qkv, order[:, None, :], order[:, :, None])
-    first, normed_c, query = project_out(mixed_a, hidden, vec, weights, bias(6)[:, None])
-    mixed_c, probs_c = attend_cross(query, pair)
-    second, normed_m, activated, slope, send_output, keep_output = mlp_forward(
-        own_index, mixed_c, first, vec, weights, weights_mlp, up_rows
-    )
-
-    got_output = swap("tp", 0, send_output)
-
-    def pair_up(keep, got):
-        got = got.astype(keep.dtype)
-        return jnp.where(own == 0, jnp.stack([keep, got]), jnp.stack([got, keep]))
-
-    chain = Chain()
-    chain.token = send_output
     bits = bits_of("dp")
     device = lax.axis_index("dp")
     shard = jnp.arange(shards)
     same = ~(shard ^ device)
     spot = sum(((same >> b) & 1) << (bits - 1 - b) for b in range(bits))
     place = jnp.concatenate([own_index, spot.astype(jnp.int32)])
-
-    def reduction(left, right, order="xyz", **options):
-        return Reduction(chain, Plan(order, bits), place, left, right, **options)
-
-    def advance(*several):
-        for one in several:
-            one.step()
+    turned_frames = turn(bits, place, frames)
+    turned_grad = turn(bits, place, grad_final[None])
+
+    normed_a = first_norm(hidden, vec)
+    turned_a = turn(bits, place, normed_a[None])
+    ready = lax.optimization_barrier((normed_a, turned_a, turned_frames, turned_grad))
+    qkv = project_qkv(ready[0], weights, qkv_bias)
+    pair = project_pair(own_index, frames, weights, pair_bias, seqs)
+    mixed_a, *attention_a = attend_self(qkv, order[:, None, :], order[:, :, None])
+    first, normed_c, query = project_out(mixed_a, hidden, vec, weights, bias(6)[:, None])
+    mixed_c, *attention_c = attend_cross(query, pair)
+    turned_c = turn(bits, place, normed_c[None])
+    mixed_now, _ = lax.optimization_barrier((mixed_c, turned_c))
+    second, normed_m, activated, slope, send_output, keep_output = mlp_forward(
+        own_index, mixed_now, first, vec, weights, weights_mlp, up_rows
+    )
+
+    got_output = swap("tp", 0, send_output)
+
+    def pair_up(keep, got):
+        got = got.astype(keep.dtype)
+        return jnp.where(own == 0, jnp.stack([keep, got]), jnp.stack([got, keep]))
+
+    chain = Chain()
+    chain.token = send_output
+
+    def gradient(order, left, right, **options):
+        parts = weight_grad(Plan(order, bits), place, left, chain.tie(right)[0], **options)
+        chain.token = parts[0]
+        return parts
+
+    def reduction(order, left, right, **options):
+        return Reduction(Plan(order, bits), gradient(order, left, right, **options))
 
     def run(kernel, first_array, *arrays):
         (first_array,) = chain.tie(first_array)
@@ -1077,45 +1144,49 @@
         chain.token = results[0]
         return results
 
-    down = reduction(grad_final, activated)
-    advance(down)
+    down = reduction("xyz", turned_grad, activated[:, :, None])
+    advance(chain, down)
     grad_before, up_sums, grad_second, low_second, sums_m, grad_mixed_c = run(
         mlp_backward, grad_final, second, vec, weights, weights_mlp, slope
     )
     output = pair_up(keep_output, chain.hold(got_output)).reshape(columns * tokens, width)
-    advance(down)
-    up = reduction(normed_m, grad_before, "yxz")
-    advance(up)
-    co = reduction(low_second, mixed_c[:, None], "zyx")
-    advance(up, co)
+    advance(chain, down)
+    up = reduction("yxz", normed_m, grad_before[:, :, None])
+    advance(chain, up)
+    two = gradient("zxy", low_second, mixed_c[:, None, None], room=2)
+    advance(chain, up)
     (grad_mixed_c,) = chain.tie(grad_mixed_c)
-    grad_query, grad_pair, sums_cross = run(attend_cross_back, query, pair, mixed_c, grad_mixed_c, probs_c)
-    advance(down, up, co)
+    grad_query, grad_pair, sums_cross = run(attend_cross_back, query, pair, mixed_c, grad_mixed_c, *attention_c)
+    advance(chain, down, up)
     send_frames, keep_frames = run(
         lambda grad: frames_backward(own_index, grad, weights), grad_pair
     )
-    advance(down, up, co)
-    got_frames = [swap("tp", 0, part) for part in jnp.split(chain.tie(send_frames)[0], seqs)]
-    kv = reduction(frames, grad_pair, "xzy", frames=True)
-    got_frames[0] = chain.hold(got_frames[0])
+    advance(chain, down, up)
+    parts = chain.tie(send_frames)[0].reshape(2 * seqs, -1, width)
+    got_frames = [swap("tp", 0, part) for part in jnp.split(parts, 2 * seqs)]
+    kv = reduction("xyz", turned_frames, grad_pair)
+    two = reduction("zxy", turned_c, grad_query[:, None, None], at=1, room=2, into=two)
+    got_frames[:seqs] = [chain.hold(part) for part in got_frames[:seqs]]
+    advance(chain, down, up, kv, two)
     grad_first, low_first, sums_c, grad_mixed_a = run(
         query_backward, grad_query, first, grad_second, vec, weights
     )
-    advance(down, up, co, kv)
+    last = gradient("xyz", low_first, mixed_a[:, None, None], room=2)
+    got_frames[seqs] = chain.hold(got_frames[seqs])
+    advance(chain, kv, two)
     (grad_mixed_a,) = chain.tie(grad_mixed_a)
-    grad_triple, sums_self = run(attend_self_back, qkv, mixed_a, grad_mixed_a, probs_a)
-    advance(co, kv)
-    triple = reduction(normed_a, grad_triple, "xyz", first=0, count=2)
-    values = reduction(normed_a, grad_triple, "yxz", first=2, count=1)
-    got_frames[1:] = [chain.hold(part) for part in got_frames[1:]]
-    advance(kv, triple, values)
-    cq = reduction(normed_c, grad_query[:, None], "zxy")
-    advance(triple, values, cq)
-    out = reduction(low_first, mixed_a[:, None], "zyx")
-    advance(kv, cq, out)
+    grad_triple, sums_self = run(attend_self_back, qkv, mixed_a, grad_mixed_a, *attention_a)
+    got_frames[seqs + 1 :] = [chain.hold(part) for part in got_frames[seqs + 1 :]]
+    advance(chain, kv, two)
+    pairs = reduction("yxz", turned_a, grad_triple[:, :, None], first=1, count=2)
+    advance(chain, pairs)
+    last = reduction("xyz", turned_a, grad_triple[:, :, None], count=1, at=1, room=2, into=last)
+    advance(chain, last)
+    advance(chain, pairs, last)
     send_hidden, keep_hidden, sums_a = run(
         lambda grad: hidden_backward(own_index, grad, hidden, grad_first, vec, weights), grad_triple
     )
+    advance(chain, kv, two, pairs, last)
     got_hidden = swap("tp", 0, chain.tie(send_hidden)[0])
 
     halves = lambda row: row.reshape(columns, width)
@@ -1140,30 +1211,30 @@
         return totals + chain.hold(swap("dp", bit, totals))
 
     totals = spread(totals, 0)
-    advance(triple, values)
+    (keep_frames,) = chain.tie(keep_frames)
     encoder_grad = join_frames(own_index, keep_frames, *got_frames, frames.shape[1])
     chain.token = encoder_grad
-    advance(out, cq)
+    advance(chain, kv, two, pairs, last)
+    totals = spread(totals, 1)
     hidden_grad = pair_up(keep_hidden, chain.hold(got_hidden)).reshape(columns * tokens, width)
-    chain.hold(hidden_grad)
-    for bit in range(1, bits):
+    hidden_grad = chain.hold(hidden_grad)
+    advance(chain, pairs, last)
+    for bit in range(2, bits):
         totals = spread(totals, bit)
-        advance(triple, values, out, cq)
     totals = pick(totals, own, 0) + swap("tp", 0, pick(totals, 1 - own, 0))
     encoder_grad = encoder_grad.transpose(1, 0, 2)
-    own_qkv = jnp.concatenate([triple.finish(), values.finish()])
-    own_ckv, own_cq, own_out = kv.finish(), cq.finish(), out.finish()
-    own_down, own_up, own_co = down.finish(), up.finish(), co.finish()
+    own_down, own_up, own_kv, own_two, own_pairs, own_last = finish(chain, down, up, kv, two, pairs, last)
+    own_qkv = jnp.concatenate([own_last[1:], own_pairs])
 
     return (
         output,
         hidden_grad,
         encoder_grad,
         own_qkv.transpose(1, 0, 2),
-        own_out[0].T,
-        own_cq[0],
-        own_ckv.transpose(1, 0, 2),
-        own_co[0].T,
+        own_last[0].T,
+        own_two[1],
+        own_kv.transpose(1, 0, 2),
+        own_two[0].T,
         own_up.transpose(1, 0, 2).reshape(rows, blocks * width),
         own_down.transpose(0, 2, 1).reshape(blocks * width, rows),
         totals[:3],

time: 839 us -> 734 us (0.87)
  Pallas kernels: 512 us -> 448 us
  waiting for transfers between devices: 170 us -> 147 us
  local copies, waits for them, and re-layouts: 64 us -> 54.3 us
    ppermute x52 -> x44, waiting for transfers between devices: 110 us -> 78.7 us  [swap(): return lax.ppermute(value, axis, [(d, d ^ 1 << bit) for d in range(size)])]
    pallas_call x43 -> x27, Pallas kernels: 229 us -> 210 us  [the longest x8 83.6 us: weight_grad(): pl.pallas_call(functools.partial(weight_kernel, plan, turned), grid_spec=...]
    pallas_call x1, Pallas kernels: 52.4 us -> 34.2 us  [attend_cross(): pl.pallas_call(cross_kernel, grid=(columns, pairs, seqs), in_specs=[pl.Bl...]
    pallas_call x1, Pallas kernels: 44 us -> 32.2 us  [mlp_forward(): pl.pallas_call(mlp_kernel, grid_spec=pltpu.PrefetchScalarGridSpec(num_sca...]
    unnamed x138 -> x121, local copies, waits for them, and re-layouts: 35 us -> 25.1 us
    pallas_call x1, Pallas kernels: 57.4 us -> 49 us  [attend_cross_back(): pl.pallas_call(cross_back_kernel, grid=(columns, pairs, seqs), in_specs=[...]
    ppermute x52 -> x44, starting transfers between devices: 50.2 us -> 43.7 us  [swap(): return lax.ppermute(value, axis, [(d, d ^ 1 << bit) for d in range(size)])]
  transfers between devices with their start and end apart: 54 -> 46, of which waited for: 16 -> 17; matrix products, arithmetic and copies ran while one was open for 6% -> 6% of each run, Pallas kernels for 51% -> 46%
where the time goes in v2:
time: 734 us; the launch traced here: 722 us
  Pallas kernels  448 us (61%)
  waiting for transfers between devices  147 us (20%)
  local copies, waits for them, and re-layouts  54.3 us (7%)
  starting transfers between devices  43.8 us (6%)
  between operations  15.2 us (2%)
  other arithmetic  12.9 us (2%)
    pallas_call x8, Pallas kernels, weight_grad(): pl.pallas_call(functools.partial(weight_kernel, plan, turned), grid_spec=...  83.6 us
    ppermute x44, waiting for transfers between devices, swap(): return lax.ppermute(value, axis, [(d, d ^ 1 << bit) for d in range(size)])  78.7 us
    all_gather x2, waiting for transfers between devices, gather(): full = lax.all_gather(part, ('tp', 'dp'), axis=0)  68.5 us
    pallas_call x11, Pallas kernels, add_and_cut(): pl.pallas_call(functools.partial(cut_kernel, tuple(starts)), grid=(starts...  52.9 us
    pallas_call x1, Pallas kernels, attend_cross_back(): pl.pallas_call(cross_back_kernel, grid=(columns, pairs, seqs), in_specs=[...  49 us
    ppermute x44, starting transfers between devices, swap(): return lax.ppermute(value, axis, [(d, d ^ 1 << bit) for d in range(size)])  43.7 us
    pallas_call x1, Pallas kernels, attend_cross(): pl.pallas_call(cross_kernel, grid=(columns, pairs, seqs), in_specs=[pl.Bl...  34.2 us
    pallas_call x1, Pallas kernels, mlp_forward(): pl.pallas_call(mlp_kernel, grid_spec=pltpu.PrefetchScalarGridSpec(num_sca...  32.2 us
  transfers between devices with their start and end apart: 46, of which 17 were waited for; matrix products, arithmetic and copies ran while one was open for 6% of the time, Pallas kernels for 46%

profile of v2, /device:TPU:0, one launch (start us, length us, event | category | flops | bytes accessed | tf_op | source)
XLA Modules:
  0.0 722.1 jit_solution(12404726221635342007)
XLA Ops:
  16.2 3.0 collective-permute-start
  19.3 2.5 constant_dynamic-slice_fusion.2
  21.8 2.0 collective-permute-start.2
  23.8 8.5 %constant_dynamic-slice_fusion.3 = bf16[2,1500,1024]{2,0,1:T(2,128)(2,1)S(1)} fusion(bf16[4,1500,1024]{2,0,1:T(4,128)(2,1)} %param.15, s32[]{:T(128)S(6)} %select_n.70), kind=kLoop, calls=%fused_computation.36 | loop fusion | bytes 12288004 | tf_op jit(solution)/shard_map/dynamic_slice | solution.py:1098
  32.3 4.6 copy.131.source_ref.frames_ref
  37.6 6.3 turn.5.left_ref
  48.8 1.8 maximum_select_fusion.1.hidden_ref
  50.6 21.2 %collective-permute-done.2 = bf16[896,512]{1,0:T(8,128)(2,1)} collective-permute-done((bf16[896,512]{1,0:T(8,128)(2,1)}, bf16[896,512]{1,0:T(8,128)(2,1)}, u32[]{:S(2)}, u32[]{:S(2)}) %collective-permute-start.2) | collective-permute-done | bytes 917536 | tf_op jit(solution)/shard_map/ppermute | solution.py:973
  71.8 3.4 maximum_select_fusion.2.grad_ref
  75.3 4.1 first_norm.1.normed_ref
  79.4 4.0 turn.4.left_ref
  83.4 4.1 turn.6.left_ref
  87.5 47.9 %all-gather.5.cloned.1.call-done = bf16[256,64,512]{2,1,0:T(8,128)(2,1)} async-done(((bf16[8,64,512]{2,1,0:T(8,128)(2,1)}), bf16[256,64,512]{2,1,0:T(8,128)(2,1)}) %all-gather.5.cloned.1.call-update) | async-done | bytes 16777232 | tf_op jit(solution)/shard_map/all_gather | solution.py:1071
  135.4 10.6 %project_qkv.1.q_ref.k_ref.v_ref = bf16[2,3,896,512]{3,2,1,0:T(8,128)(2,1)} custom-call(bf16[896,1024]{1,0:T(8,128)(2,1)} %first_norm.1.normed_ref, bf16[2,16,8,64,512]{4,3,2,1,0:T(8,128)(2,1)} %bitcast.210, f32[2,3,1,512]{3,2,1,0:T(1,128)} %copy.114.bias_ref), custom_call_target="tpu_custom_call" | custom-call | flops 1820597504 | bytes 5826543 | tf_op jit(solution)/shard_map/project_qkv/pallas_call | solution.py:145
  146.0 16.5 %attend_self.1 = (bf16[2,896,512]{2,1,0:T(8,128)(2,1)}, bf16[2,2,2,4,448,448]{5,4,3,2,1,0:T(8,128)(2,1)}, f32[2,896,512]{2,1,0:T(8,128)}) custom-call(bf16[2,3,896,512]{3,2,1,0:T(8,128)(2,1)} %project_qkv.1.q_ref.k_ref.v_ref, bf16[2,3,896,512]{3,2,1,0:T(8,128)(2,1)} %project_qkv.1.q_ref.k_ref.v_ref, bf16[2,3,896,512]{3,2,1,0:T(8,128)(2,1)} %project_qkv.1.q_ref.k_ref.v_ref, ...), custom_call_target="tpu_custom_call" | custom-call | flops 2041673216 | bytes 6534062 | tf_op jit(solution)/shard_map/attend_self/pallas_call | solution.py:233
  162.5 11.6 %project_out.1 = (f32[896,1024]{1,0:T(8,128)}, bf16[896,1024]{1,0:T(8,128)(2,1)}, bf16[2,896,512]{2,1,0:T(8,128)(2,1)}) custom-call(bf16[2,896,512]{2,1,0:T(8,128)(2,1)} %get-tuple-element.223.mixed_ref, bf16[896,1024]{1,0:T(8,128)(2,1)} %maximum_select_fusion.1.hidden_ref, f32[16,1024]{1,0:T(8,128)} %concatenate.37.vec_ref, ...), custom_call_target="tpu_custom_call" | custom-call | flops 1378445952 | bytes 4411505 | tf_op jit(solution)/shard_map/project_out/pallas_call | solution.py:288
  174.1 4.0 turn.7.left_ref
  178.2 19.0 %project_pair.1.kv_ref = bf16[2,2,2,1500,512]{4,3,2,1,0:T(8,128)(2,1)} custom-call(s32[1]{0:T(128)} %bitcast.own_ref, bf16[2,1500,1024]{2,1,0:T(8,128)(2,1)} %copy.131.source_ref.frames_ref, bf16[2,16,8,64,512]{4,3,2,1,0:T(8,128)(2,1)} %bitcast.213, f32[2,2,1,512]{3,2,1,0:T(1,128)} %copy.116.bias_ref), custom_call_target="tpu_custom_call" | custom-call | flops 3454979072 | bytes 11057131 | tf_op jit(solution)/shard_map/project_pair/pallas_call | solution.py:323
  197.2 34.2 %attend_cross.1 = (bf16[2,896,512]{2,1,0:T(8,128)(2,1)}, bf16[2,4,2,2,448,1500]{5,4,3,2,1,0:T(8,128)(2,1)}, f32[2,896,512]{2,1,0:T(8,128)}) custom-call(bf16[2,896,512]{2,1,0:T(8,128)(2,1)} %get-tuple-element.255.q_ref, bf16[2,2,2,1500,512]{4,3,2,1,0:T(8,128)(2,1)} %project_pair.1.kv_ref), custom_call_target="tpu_custom_call" | custom-call | flops 5675606016 | bytes 18163908 | tf_op jit(solution)/shard_map/attend_cross/pallas_call | solution.py:349
  231.3 20.6 %all-gather.7.cloned.1.call-done = bf16[256,64,512]{2,1,0:T(8,128)(2,1)} async-done(((bf16[8,64,512]{2,1,0:T(8,128)(2,1)}), bf16[256,64,512]{2,1,0:T(8,128)(2,1)}) %all-gather.7.cloned.1.call-update) | async-done | bytes 16777232 | tf_op jit(solution)/shard_map/all_gather | solution.py:1071
  252.0 32.2 %mlp_forward.1 = (f32[896,1024]{1,0:T(8,128)}, bf16[896,1024]{1,0:T(8,128)(2,1)}, bf16[2,4,896,512]{3,2,1,0:T(8,128)(2,1)}, bf16[2,4,896,512]{3,2,1,0:T(8,128)(2...) custom-call(s32[1]{0:T(128)} %bitcast.own_ref, bf16[2,896,512]{2,1,0:T(8,128)(2,1)} %get-tuple-element.227.mixed_ref, ...), custom_call_target="tpu_custom_call" | custom-call | flops 4473506816 | bytes 14316773 | tf_op jit(solution)/shard_map/mlp_forward/pallas_call | solution.py:432
  284.2 14.7 %weight_grad.8 = (bf16[2,2,4,4,64,512]{5,4,3,2,1,0:T(8,128)(2,1)}, bf16[2,2,4,4,64,512]{5,4,3,2,1,0:T(8,128)(2,1)}) custom-call(s32[17]{0:T(128)} %pad_add_fusion.place_ref, bf16[1,1024,896]{2,1,0:T(8,128)(2,1)} %turn.6.left_ref, bf16[2,4,1,896,512]{4,3,2,1,0:T(8,128)(2,1)} %bitcast.234), custom_call_target="tpu_custom_call" | custom-call | flops 2262748928 | bytes 7241581 | tf_op jit(solution)/shard_map/weight_grad/pallas_call | solution.py:880
  300.6 31.0 %mlp_backward.1 = (bf16[2,4,896,512]{3,2,1,0:T(8,128)(2,1)}, f32[2,4,1,512]{3,2,1,0:T(1,128)}, f32[896,1024]{1,0:T(8,128)}, bf16[896,1024]{1,0:T(8,128)(2,1)}, f...) custom-call(bf16[896,1024]{1,0:T(8,128)(2,1)} %maximum_select_fusion.2.grad_ref, ...), custom_call_target="tpu_custom_call" | custom-call | flops 4473506816 | bytes 14316773 | tf_op jit(solution)/shard_map/mlp_backward/pallas_call | solution.py:504
  331.7 2.0 copy-done.2
  333.8 5.8 add_and_cut.11
  339.5 15.4 %weight_grad.9 = (bf16[2,2,4,4,64,512]{5,4,3,2,1,0:T(8,128)(2,1)}, bf16[2,2,4,4,64,512]{5,4,3,2,1,0:T(8,128)(2,1)}) custom-call(s32[17]{0:T(128)} %pad_add_fusion.place_ref, bf16[896,1024]{1,0:T(8,128)(2,1)} %get-tuple-element.239.left_ref, bf16[2,4,1,896,512]{4,3,2,1,0:T(8,128)(2,1)} %bitcast.233), custom_call_target="tpu_custom_call" | custom-call | flops 2262748928 | bytes 7241581 | tf_op jit(solution)/shard_map/weight_grad/pallas_call | solution.py:880
  355.6 6.6 weight_grad.10
  362.3 2.0 copy-done.3
  364.3 5.8 add_and_cut.12
  371.2 49.0 %attend_cross_back.1 = (bf16[2,896,512]{2,1,0:T(8,128)(2,1)}, bf16[2,2,2,1500,512]{4,3,2,1,0:T(8,128)(2,1)}, f32[2,8,512]{2,1,0:T(8,128)}) custom-call(bf16[2,896,512]{2,1,0:T(8,128)(2,1)} %get-tuple-element.255.q_ref, bf16[2,2,2,1500,512]{4,3,2,1,0:T(8,128)(2,1)} %project_pair.1.kv_ref, bf16[2,896,512]{2,1,0:T(8,128)(2,1)} %get-tuple-element.227.mixed_ref, ...), custom_call_target="tpu_custom_call" | custom-call | flops 10857069568 | bytes 34746388 | tf_op jit(solution)/shard_map/attend_cross_back/pallas_call | solution.py:562
  421.6 6.6 add_and_cut.13
  430.4 19.3 %frames_backward.1 = (bf16[2,1504,512]{2,1,0:T(8,128)(2,1)}, bf16[2,1504,512]{2,1,0:T(8,128)(2,1)}) custom-call(s32[1]{0:T(128)} %bitcast.own_ref, bf16[2,2,2,1500,512]{4,3,2,1,0:T(8,128)(2,1)} %get-tuple-element.283.grad_ref.right_ref, bf16[2,16,8,64,512]{4,3,2,1,0:T(8,128)(2,1)} %bitcast.216), custom_call_target="tpu_custom_call" | custom-call | flops 3454979072 | bytes 11057131 | tf_op jit(solution)/shard_map/frames_backward/pallas_call | solution.py:776
  449.8 3.6 collective-permute-done.8
  454.9 3.9 add_and_cut.14
  462.8 1.6 collective-permute-start.11
  464.4 19.1 %weight_grad.11 = (bf16[2,2,4,2,64,512]{5,4,3,2,1,0:T(8,128)(2,1)}, bf16[2,2,4,2,64,512]{5,4,3,2,1,0:T(8,128)(2,1)}) custom-call(s32[17]{0:T(128)} %pad_add_fusion.place_ref, bf16[2,1024,1500]{2,1,0:T(8,128)(2,1)} %turn.5.left_ref, bf16[2,2,2,1500,512]{4,3,2,1,0:T(8,128)(2,1)} %get-tuple-element.283.grad_ref.right_ref), custom_call_target="tpu_custom_call" | custom-call | flops 3454979072 | bytes 11057131 | tf_op jit(solution)/shard_map/weight_grad/pallas_call | solution.py:880
  483.5 6.1 weight_grad.12
  489.6 5.2 collective-permute-done.12.refs_1_
  495.7 2.9 add_and_cut.15
  500.4 15.1 %query_backward.1 = (f32[896,1024]{1,0:T(8,128)}, bf16[896,1024]{1,0:T(8,128)(2,1)}, f32[8,1024]{1,0:T(8,128)}, bf16[2,896,512]{2,1,0:T(8,128)(2,1)}) custom-call(bf16[2,896,512]{2,1,0:T(8,128)(2,1)} %get-tuple-element.305.grad_ref, f32[896,1024]{1,0:T(8,128)} %get-tuple-element.228.first_ref, f32[896,1024]{1,0:T(8,128)} %get-tuple-element.306.second_ref, ...), custom_call_target="tpu_custom_call" | custom-call | flops 1378445952 | bytes 4411505 | tf_op jit(solution)/shard_map/query_backward/pallas_call | solution.py:674
  515.5 6.6 weight_grad.13
  523.5 6.6 add_and_cut.16
  532.8 23.7 %attend_self_back.1 = (bf16[2,3,896,512]{3,2,1,0:T(8,128)(2,1)}, f32[2,8,512]{2,1,0:T(8,128)}) custom-call(bf16[2,3,896,512]{3,2,1,0:T(8,128)(2,1)} %project_qkv.1.q_ref.k_ref.v_ref, bf16[2,3,896,512]{3,2,1,0:T(8,128)(2,1)} %project_qkv.1.q_ref.k_ref.v_ref, bf16[2,3,896,512]{3,2,1,0:T(8,128)(2,1)} %project_qkv.1.q_ref.k_ref.v_ref, ...), custom_call_target="tpu_custom_call" | custom-call | flops 3589203712 | bytes 11486696 | tf_op jit(solution)/shard_map/attend_self_back/pallas_call | solution.py:612
  557.9 3.7 add_and_cut.17
  561.6 8.9 %weight_grad.14 = (bf16[2,2,4,2,64,512]{5,4,3,2,1,0:T(8,128)(2,1)}, bf16[2,2,4,2,64,512]{5,4,3,2,1,0:T(8,128)(2,1)}) custom-call(s32[17]{0:T(128)} %pad_add_fusion.place_ref, bf16[1,1024,896]{2,1,0:T(8,128)(2,1)} %turn.4.left_ref, bf16[2,3,1,896,512]{4,3,2,1,0:T(8,128)(2,1)} %bitcast.224), custom_call_target="tpu_custom_call" | custom-call | flops 1378445952 | bytes 4411505 | tf_op jit(solution)/shard_map/weight_grad/pallas_call | solution.py:880
  570.5 6.0 weight_grad.15
  577.1 3.9 collective-permute-done.21
  580.9 3.0 collective-permute-done.20
  585.3 6.7 add_and_cut.18
  600.1 16.1 %hidden_backward.1 = (bf16[896,512]{1,0:T(8,128)(2,1)}, f32[896,512]{1,0:T(8,128)}, f32[8,1024]{1,0:T(8,128)}) custom-call(s32[1]{0:T(128)} %bitcast.own_ref, bf16[2,3,896,512]{3,2,1,0:T(8,128)(2,1)} %get-tuple-element.348.grad_ref, bf16[896,1024]{1,0:T(8,128)(2,1)} %maximum_select_fusion.1.hidden_ref, f32[896,1024]{1,0:T(8,128)} %get-tuple-element.308.first_ref, ...), custom_call_target="tpu_custom_call" | custom-call | flops 1820597504 | bytes 5826543 | tf_op jit(solution)/shard_map/hidden_backward/pallas_call | solution.py:726
  616.2 12.4 %collective-permute-done.22 = bf16[2,2,2,64,512]{4,3,2,1,0:T(8,128)(2,1)S(1)} collective-permute-done((bf16[2,2,2,64,512]{4,3,2,1,0:T(8,128)(2,1)}, bf16[2,2,2,64,512]{4,3,2,1,0:T(8,128)(2,1)S(1)}, u32[]{:S(2)}, u32[]{:S(2)}) %collective-permute-start.22) | collective-permute-done | bytes 524320 | tf_op jit(solution)/shard_map/ppermute | solution.py:973
  630.3 5.3 add_and_cut.19
  640.9 3.1 maximum_select_fusion.3
  645.6 9.0 %collective-permute-done.30 = bf16[2,2,64,512]{3,2,1,0:T(8,128)(2,1)S(1)} collective-permute-done((bf16[2,2,64,512]{3,2,1,0:T(8,128)(2,1)}, bf16[2,2,64,512]{3,2,1,0:T(8,128)(2,1)S(1)}, u32[]{:S(2)}, u32[]{:S(2)}) %collective-permute-start.30) | collective-permute-done | bytes 262176 | tf_op jit(solution)/shard_map/ppermute | solution.py:973
  654.6 1.6 collective-permute-start.29
  656.4 11.1 %join_frames.1 = f32[1500,4,512]{2,1,0:T(4,128)} custom-call(s32[1]{0:T(128)} %bitcast.own_ref, bf16[2,1504,512]{2,1,0:T(8,128)(2,1)} %get-tuple-element.390.keep_ref, bf16[1,752,512]{2,1,0:T(8,128)(2,1)} %copy-done.22, bf16[1,752,512]{2,1,0:T(8,128)(2,1)} %copy-done.23, bf16[1,752,512]{2,1,0:T(8,128)(2,1)} %collective-permute-done.16.refs_2_, ...), custom_call_target="tpu_custom_call" | custom-call | flops 494142848 | bytes 1581428 | tf_op jit(solution)/shard_map/join_frames/pallas_call | solution.py:955
  669.3 3.4 add_and_cut.20
  681.6 2.3 maximum_select_fusion
  683.9 3.9 collective-permute-done.33
  687.7 3.9 collective-permute-done.34
  692.4 2.1 add_and_cut.21
  695.4 5.2 collective-permute-done.42
  703.8 2.6 collective-permute-start.36
  708.2 4.4 collective-permute-done.35
  (247 shorter events, 73.1 us)
Async XLA Ops:
  7.2 30.4 %copy-start = (s32[4,448]{1,0:T(4,128)S(1)}, s32[4,448]{1,0:T(4,128)}, u32[]{:S(2)}) copy-start(s32[4,448]{1,0:T(4,128)} %param.16) | copy-start | bytes 21508
  7.2 128.2 %all-gather.5.cloned.1.call-start = ((), (), s32[]{:S(2)}) async-start(), calls=%async_computation | async-start | bytes 17301504 | tf_op jit(solution)/shard_map/all_gather | solution.py:1071
  12.5 239.5 %all-gather.7.cloned.1.call-start = ((), (), s32[]{:S(2)}) async-start(), calls=%async_computation.1 | async-start | bytes 17301504 | tf_op jit(solution)/shard_map/all_gather | solution.py:1071
  16.2 32.6 %collective-permute-start = (bf16[896,512]{1,0:T(8,128)(2,1)}, bf16[896,512]{1,0:T(8,128)(2,1)S(1)}, u32[]{:S(2)}, u32[]{:S(2)}) collective-permute-start(bf16[896,512]{1,0:T(8,128)(2,1)} %get-tuple-element.451), channel_id=1, source_target_pairs={{0,1},{1,0},{2,3},{3,2},{4,5},{5,4},{6,7},{7,6},{8,9},{9,8},{10,11... | collective-permute-start | bytes 2752520 | tf_op jit(solution)/shard_map/ppermute | solution.py:973
  19.2 26.3 %collective-permute-start.1 = (f32[17,512]{1,0:T(8,128)S(1)}, f32[17,512]{1,0:T(8,128)S(1)}, u32[]{:S(2)}, u32[]{:S(2)}) collective-permute-start(f32[17,512]{1,0:T(8,128)S(1)} %get-tuple-element.461), channel_id=1, source_target_pairs={{0,1},{1,0},{2,3},{3,2},{4,5},{5,4},{6,7},{7,6},{8,9},{9,8},{10,11... | collective-permute-start | bytes 104456 | tf_op jit(solution)/shard_map/ppermute | solution.py:973
  21.8 50.0 %collective-permute-start.2 = (bf16[896,512]{1,0:T(8,128)(2,1)}, bf16[896,512]{1,0:T(8,128)(2,1)}, u32[]{:S(2)}, u32[]{:S(2)}) collective-permute-start(bf16[896,512]{1,0:T(8,128)(2,1)} %get-tuple-element.449), channel_id=1, source_target_pairs={{0,1},{1,0},{2,3},{3,2},{4,5},{5,4},{6,7},{7,6},{8,9},{9,8},{10,11... | collective-permute-start | bytes 2752520 | tf_op jit(solution)/shard_map/ppermute | solution.py:973
  284.2 15.0 %copy-start.44 = (bf16[896,512]{1,0:T(8,128)(2,1)S(1)}, bf16[896,512]{1,0:T(8,128)(2,1)}, u32[]{:S(2)}) copy-start(bf16[896,512]{1,0:T(8,128)(2,1)} %get-tuple-element.230) | copy-start | bytes 2752516
  298.9 32.8 %collective-permute-start.4 = (bf16[2,2,2,2,4,64,512]{6,5,4,3,2,1,0:T(8,128)(2,1)}, bf16[2,2,2,2,4,64,512]{6,5,4,3,2,1,0:T(8,128)(2,1)S(1)}, u32[]{:S(2)}, u32[]{:S(2)}) collective-permute-start(bf16[2,2,2,2,4,64,512]{6,5,4,3,2,1,0:T(8,128)(2,1)} %bitcast.308), channel_id=1, source_target_pairs={{0,2},{2,0},{4,6},{6,4},{8,10},{10,8},{12,14},{14,12},{16,18},{18,... | collective-permute-start | bytes 12582920 | tf_op jit(solution)/shard_map/ppermute | solution.py:973
  299.2 32.5 %collective-permute-start.3 = (bf16[896,512]{1,0:T(8,128)(2,1)S(1)}, bf16[896,512]{1,0:T(8,128)(2,1)S(1)}, u32[]{:S(2)}, u32[]{:S(2)}) collective-permute-start(bf16[896,512]{1,0:T(8,128)(2,1)S(1)} %copy-done.44), channel_id=1, source_target_pairs={{0,1},{1,0},{2,3},{3,2},{4,5},{5,4},{6,7},{7,6},{8,9},{9,8},{10,11... | collective-permute-start | bytes 2752520 | tf_op jit(solution)/shard_map/ppermute | solution.py:973
  331.7 23.3 %copy-start.20 = (bf16[896,512]{1,0:T(8,128)(2,1)}, bf16[896,512]{1,0:T(8,128)(2,1)S(1)}, u32[]{:S(2)}) copy-start(bf16[896,512]{1,0:T(8,128)(2,1)S(1)} %collective-permute-done.3) | copy-start | bytes 2752516
  355.0 7.4 %collective-permute-start.5 = (bf16[2,2,2,2,4,64,512]{6,5,4,3,2,1,0:T(8,128)(2,1)}, bf16[2,2,2,2,4,64,512]{6,5,4,3,2,1,0:T(8,128)(2,1)S(1)}, u32[]{:S(2)}, u32[]{:S(2)}) collective-permute-start(bf16[2,2,2,2,4,64,512]{6,5,4,3,2,1,0:T(8,128)(2,1)} %bitcast.309), channel_id=1, source_target_pairs={{0,2},{2,0},{4,6},{6,4},{8,10},{10,8},{12,14},{14,12},{16,18},{18,... | collective-permute-start | bytes 12582920 | tf_op jit(solution)/shard_map/ppermute | solution.py:973
  355.0 65.3 %collective-permute-start.6 = (bf16[2,2,2,4,64,512]{5,4,3,2,1,0:T(8,128)(2,1)}, bf16[2,2,2,4,64,512]{5,4,3,2,1,0:T(8,128)(2,1)}, u32[]{:S(2)}, u32[]{:S(2)}) collective-permute-start(bf16[2,2,2,4,64,512]{5,4,3,2,1,0:T(8,128)(2,1)} %bitcast.311), channel_id=1, source_target_pairs={{0,4},{2,6},{4,0},{6,2},{8,12},{10,14},{12,8},{14,10},{16,20},{18,... | collective-permute-start | bytes 6291464 | tf_op jit(solution)/shard_map/ppermute | solution.py:973
  370.1 50.1 %collective-permute-start.7 = (bf16[2,2,2,4,64,512]{5,4,3,2,1,0:T(8,128)(2,1)}, bf16[2,2,2,4,64,512]{5,4,3,2,1,0:T(8,128)(2,1)S(1)}, u32[]{:S(2)}, u32[]{:S(2)}) collective-permute-start(bf16[2,2,2,4,64,512]{5,4,3,2,1,0:T(8,128)(2,1)} %bitcast.312), channel_id=1, source_target_pairs={{0,1},{1,0},{2,3},{3,2},{4,5},{5,4},{6,7},{7,6},{8,9},{9,8},{10,11... | collective-permute-start | bytes 6291464 | tf_op jit(solution)/shard_map/ppermute | solution.py:973
  428.2 25.2 %collective-permute-start.8 = (bf16[2,2,4,64,512]{4,3,2,1,0:T(8,128)(2,1)}, bf16[2,2,4,64,512]{4,3,2,1,0:T(8,128)(2,1)S(1)}, u32[]{:S(2)}, u32[]{:S(2)}) collective-permute-start(bf16[2,2,4,64,512]{4,3,2,1,0:T(8,128)(2,1)} %bitcast.319), channel_id=1, source_target_pairs={{0,1},{1,0},{2,3},{3,2},{4,5},{5,4},{6,7},{7,6},{8,9},{9,8},{10,11... | collective-permute-start | bytes 3145736 | tf_op jit(solution)/shard_map/ppermute | solution.py:973
  429.1 24.8 %collective-permute-start.9 = (bf16[2,2,4,64,512]{4,3,2,1,0:T(8,128)(2,1)}, bf16[2,2,4,64,512]{4,3,2,1,0:T(8,128)(2,1)S(1)}, u32[]{:S(2)}, u32[]{:S(2)}) collective-permute-start(bf16[2,2,4,64,512]{4,3,2,1,0:T(8,128)(2,1)} %bitcast.318), channel_id=1, source_target_pairs={{0,4},{2,6},{4,0},{6,2},{8,12},{10,14},{12,8},{14,10},{16,20},{18,... | collective-permute-start | bytes 3145736 | tf_op jit(solution)/shard_map/ppermute | solution.py:973
  460.3 29.3 %collective-permute-start.13 = (bf16[1,752,512]{2,1,0:T(8,128)(2,1)}, bf16[1,752,512]{2,1,0:T(8,128)(2,1)S(1)}, u32[]{:S(2)}, u32[]{:S(2)}) collective-permute-start(bf16[1,752,512]{2,1,0:T(8,128)(2,1)} %get-tuple-element.446), channel_id=1, source_target_pairs={{0,1},{1,0},{2,3},{3,2},{4,5},{5,4},{6,7},{7,6},{8,9},{9,8},{10,11... | collective-permute-start | bytes 2310152 | tf_op jit(solution)/shard_map/ppermute | solution.py:973
  461.5 33.4 %collective-permute-start.12 = (bf16[1,752,512]{2,1,0:T(8,128)(2,1)}, bf16[1,752,512]{2,1,0:T(8,128)(2,1)S(1)}, u32[]{:S(2)}, u32[]{:S(2)}) collective-permute-start(bf16[1,752,512]{2,1,0:T(8,128)(2,1)} %get-tuple-element.447), channel_id=1, source_target_pairs={{0,1},{1,0},{2,3},{3,2},{4,5},{5,4},{6,7},{7,6},{8,9},{9,8},{10,11... | collective-permute-start | bytes 2310152 | tf_op jit(solution)/shard_map/ppermute | solution.py:973
  462.4 32.5 %collective-permute-start.10 = (bf16[2,4,64,512]{3,2,1,0:T(8,128)(2,1)}, bf16[2,4,64,512]{3,2,1,0:T(8,128)(2,1)S(1)}, u32[]{:S(2)}, u32[]{:S(2)}) collective-permute-start(bf16[2,4,64,512]{3,2,1,0:T(8,128)(2,1)} %bitcast.55), channel_id=1, source_target_pairs={{0,8},{2,10},{4,12},{6,14},{8,0},{10,2},{12,4},{14,6},{16,24},{18,... | collective-permute-start | bytes 1572872 | tf_op jit(solution)/shard_map/ppermute | solution.py:973
  462.8 32.1 %collective-permute-start.11 = (bf16[2,4,64,512]{3,2,1,0:T(8,128)(2,1)}, bf16[2,4,64,512]{3,2,1,0:T(8,128)(2,1)}, u32[]{:S(2)}, u32[]{:S(2)}) collective-permute-start(bf16[2,4,64,512]{3,2,1,0:T(8,128)(2,1)} %bitcast.51), channel_id=1, source_target_pairs={{0,8},{2,10},{4,12},{6,14},{8,0},{10,2},{12,4},{14,6},{16,24},{18,... | collective-permute-start | bytes 1572872 | tf_op jit(solution)/shard_map/ppermute | solution.py:973
  483.5 15.8 %copy-start.21 = (bf16[1,752,512]{2,1,0:T(8,128)(2,1)S(1)}, bf16[1,752,512]{2,1,0:T(8,128)(2,1)}, u32[]{:S(2)}) copy-start(bf16[1,752,512]{2,1,0:T(8,128)(2,1)} %get-tuple-element.445) | copy-start | bytes 2310148
  489.6 9.1 %copy-start.5 = (bf16[4,2,2,2,64,512]{5,4,3,2,1,0:T(8,128)(2,1)S(1)}, bf16[4,2,2,2,64,512]{5,4,3,2,1,0:T(8,128)(2,1)}, u32[]{:S(2)}) copy-start(bf16[4,2,2,2,64,512]{5,4,3,2,1,0:T(8,128)(2,1)} %get-tuple-element.294) | copy-start | bytes 6291460
  489.6 9.0 %copy-start.22 = (bf16[1,752,512]{2,1,0:T(8,128)(2,1)}, bf16[1,752,512]{2,1,0:T(8,128)(2,1)S(1)}, u32[]{:S(2)}) copy-start(bf16[1,752,512]{2,1,0:T(8,128)(2,1)S(1)} %collective-permute-done.13.refs_0_) | copy-start | bytes 2310148
  498.7 23.4 %collective-permute-start.15 = (bf16[2,2,2,2,2,64,512]{6,5,4,3,2,1,0:T(8,128)(2,1)S(1)}, bf16[2,2,2,2,2,64,512]{6,5,4,3,2,1,0:T(8,128)(2,1)S(1)}, u32[]{:S(2)}, u32[]{:S(2)}) collective-permute-start(bf16[2,2,2,2,2,64,512]{6,5,4,3,2,1,0:T(8,128)(2,1)S(1)} %bitcast.242), channel_id=1, source_target_pairs={{0,2},{2,0},{4,6},{6,4},{8,10},{10,8},{12,14},{14,12},{16,18},{18,... | collective-permute-start | bytes 6291464 | tf_op jit(solution)/shard_map/ppermute | solution.py:973
  498.8 23.4 %collective-permute-start.14 = (bf16[2,2,2,2,2,64,512]{6,5,4,3,2,1,0:T(8,128)(2,1)}, bf16[2,2,2,2,2,64,512]{6,5,4,3,2,1,0:T(8,128)(2,1)}, u32[]{:S(2)}, u32[]{:S(2)}) collective-permute-start(bf16[2,2,2,2,2,64,512]{6,5,4,3,2,1,0:T(8,128)(2,1)} %bitcast.310), channel_id=1, source_target_pairs={{0,2},{2,0},{4,6},{6,4},{8,10},{10,8},{12,14},{14,12},{16,18},{18,... | collective-permute-start | bytes 6291464 | tf_op jit(solution)/shard_map/ppermute | solution.py:973
  499.3 22.8 %collective-permute-start.16 = (bf16[1,752,512]{2,1,0:T(8,128)(2,1)S(1)}, bf16[1,752,512]{2,1,0:T(8,128)(2,1)}, u32[]{:S(2)}, u32[]{:S(2)}) collective-permute-start(bf16[1,752,512]{2,1,0:T(8,128)(2,1)S(1)} %copy-done.21), channel_id=1, source_target_pairs={{0,1},{1,0},{2,3},{3,2},{4,5},{5,4},{6,7},{7,6},{8,9},{9,8},{10,11... | collective-permute-start | bytes 2310152 | tf_op jit(solution)/shard_map/ppermute | solution.py:973
  530.1 26.4 %collective-permute-start.17 = (bf16[2,2,2,2,64,512]{5,4,3,2,1,0:T(8,128)(2,1)}, bf16[2,2,2,2,64,512]{5,4,3,2,1,0:T(8,128)(2,1)S(1)}, u32[]{:S(2)}, u32[]{:S(2)}) collective-permute-start(bf16[2,2,2,2,64,512]{5,4,3,2,1,0:T(8,128)(2,1)} %bitcast.317), channel_id=1, source_target_pairs={{0,4},{2,6},{4,0},{6,2},{8,12},{10,14},{12,8},{14,10},{16,20},{18,... | collective-permute-start | bytes 3145736 | tf_op jit(solution)/shard_map/ppermute | solution.py:973
  531.3 25.3 %collective-permute-start.18 = (bf16[2,2,2,2,64,512]{5,4,3,2,1,0:T(8,128)(2,1)}, bf16[2,2,2,2,64,512]{5,4,3,2,1,0:T(8,128)(2,1)S(1)}, u32[]{:S(2)}, u32[]{:S(2)}) collective-permute-start(bf16[2,2,2,2,64,512]{5,4,3,2,1,0:T(8,128)(2,1)} %bitcast.316), channel_id=1, source_target_pairs={{0,8},{2,10},{4,12},{6,14},{8,0},{10,2},{12,4},{14,6},{16,24},{18,... | collective-permute-start | bytes 3145736 | tf_op jit(solution)/shard_map/ppermute | solution.py:973
  531.7 24.8 %collective-permute-start.19 = (bf16[1,752,512]{2,1,0:T(8,128)(2,1)S(1)}, bf16[1,752,512]{2,1,0:T(8,128)(2,1)S(1)}, u32[]{:S(2)}, u32[]{:S(2)}) collective-permute-start(bf16[1,752,512]{2,1,0:T(8,128)(2,1)S(1)} %get-tuple-element.444), channel_id=1, source_target_pairs={{0,1},{1,0},{2,3},{3,2},{4,5},{5,4},{6,7},{7,6},{8,9},{9,8},{10,11... | collective-permute-start | bytes 2310152 | tf_op jit(solution)/shard_map/ppermute | solution.py:973
  556.5 20.1 %copy-start.24 = (bf16[1,752,512]{2,1,0:T(8,128)(2,1)}, bf16[1,752,512]{2,1,0:T(8,128)(2,1)S(1)}, u32[]{:S(2)}) copy-start(bf16[1,752,512]{2,1,0:T(8,128)(2,1)S(1)} %collective-permute-done.19.refs_3_) | copy-start | bytes 2310148
  576.6 4.4 collective-permute-start.21
  576.6 7.4 %collective-permute-start.20 = (bf16[2,2,2,2,2,64,512]{6,5,4,3,2,1,0:T(8,128)(2,1)}, bf16[2,2,2,2,2,64,512]{6,5,4,3,2,1,0:T(8,128)(2,1)S(1)}, u32[]{:S(2)}, u32[]{:S(2)}) collective-permute-start(bf16[2,2,2,2,2,64,512]{6,5,4,3,2,1,0:T(8,128)(2,1)} %bitcast.313), channel_id=1, source_target_pairs={{0,2},{2,0},{4,6},{6,4},{8,10},{10,8},{12,14},{14,12},{16,18},{18,... | collective-permute-start | bytes 6291464 | tf_op jit(solution)/shard_map/ppermute | solution.py:973
  585.3 9.5 %copy-start.45 = (bf16[512,512]{1,0:T(8,128)(2,1)S(1)}, bf16[512,512]{1,0:T(8,128)(2,1)}, u32[]{:S(2)}) copy-start(bf16[512,512]{1,0:T(8,128)(2,1)} %get-tuple-element.333) | copy-start | bytes 1572868
  585.3 11.1 %copy-start.42 = (f32[8,1024]{1,0:T(8,128)S(1)}, f32[8,1024]{1,0:T(8,128)}, u32[]{:S(2)}) copy-start(f32[8,1024]{1,0:T(8,128)} %get-tuple-element.373) | copy-start | bytes 98308
  592.0 36.7 %collective-permute-start.24 = (bf16[2,2,2,2,64,512]{5,4,3,2,1,0:T(8,128)(2,1)}, bf16[2,2,2,2,64,512]{5,4,3,2,1,0:T(8,128)(2,1)S(1)}, u32[]{:S(2)}, u32[]{:S(2)}) collective-permute-start(bf16[2,2,2,2,64,512]{5,4,3,2,1,0:T(8,128)(2,1)} %bitcast.315), channel_id=1, source_target_pairs={{0,1},{1,0},{2,3},{3,2},{4,5},{5,4},{6,7},{7,6},{8,9},{9,8},{10,11... | collective-permute-start | bytes 3145736 | tf_op jit(solution)/shard_map/ppermute | solution.py:973
  592.9 35.7 %collective-permute-start.25 = (bf16[2,2,2,2,64,512]{5,4,3,2,1,0:T(8,128)(2,1)}, bf16[2,2,2,2,64,512]{5,4,3,2,1,0:T(8,128)(2,1)S(1)}, u32[]{:S(2)}, u32[]{:S(2)}) collective-permute-start(bf16[2,2,2,2,64,512]{5,4,3,2,1,0:T(8,128)(2,1)} %bitcast.314), channel_id=1, source_target_pairs={{0,4},{2,6},{4,0},{6,2},{8,12},{10,14},{12,8},{14,10},{16,20},{18,... | collective-permute-start | bytes 3145736 | tf_op jit(solution)/shard_map/ppermute | solution.py:973
  593.8 34.8 %collective-permute-start.22 = (bf16[2,2,2,64,512]{4,3,2,1,0:T(8,128)(2,1)}, bf16[2,2,2,64,512]{4,3,2,1,0:T(8,128)(2,1)S(1)}, u32[]{:S(2)}, u32[]{:S(2)}) collective-permute-start(bf16[2,2,2,64,512]{4,3,2,1,0:T(8,128)(2,1)} %bitcast.92), channel_id=1, source_target_pairs={{0,1},{1,0},{2,3},{3,2},{4,5},{5,4},{6,7},{7,6},{8,9},{9,8},{10,11... | collective-permute-start | bytes 1572872 | tf_op jit(solution)/shard_map/ppermute | solution.py:973
  594.8 33.8 %collective-permute-start.23 = (bf16[2,2,2,64,512]{4,3,2,1,0:T(8,128)(2,1)S(1)}, bf16[2,2,2,64,512]{4,3,2,1,0:T(8,128)(2,1)S(1)}, u32[]{:S(2)}, u32[]{:S(2)}) collective-permute-start(bf16[2,2,2,64,512]{4,3,2,1,0:T(8,128)(2,1)S(1)} %bitcast.320), channel_id=1, source_target_pairs={{0,16},{2,18},{4,20},{6,22},{8,24},{10,26},{12,28},{14,30},{16,0},... | collective-permute-start | bytes 1572872 | tf_op jit(solution)/shard_map/ppermute | solution.py:973
  597.2 42.6 %collective-permute-start.40 = (bf16[4,64,512]{2,1,0:T(8,128)(2,1)}, bf16[4,64,512]{2,1,0:T(8,128)(2,1)S(1)}, u32[]{:S(2)}, u32[]{:S(2)}) collective-permute-start(bf16[4,64,512]{2,1,0:T(8,128)(2,1)} %bitcast.160), channel_id=1, source_target_pairs={{0,16},{2,18},{4,20},{6,22},{8,24},{10,26},{12,28},{14,30},{16,0},... | collective-permute-start | bytes 786440 | tf_op jit(solution)/shard_map/ppermute | solution.py:973
  630.3 10.7 %copy-start.19 = (bf16[896,512]{1,0:T(8,128)(2,1)S(1)}, bf16[896,512]{1,0:T(8,128)(2,1)}, u32[]{:S(2)}) copy-start(bf16[896,512]{1,0:T(8,128)(2,1)} %get-tuple-element.229) | copy-start | bytes 2752516
  635.6 20.7 %copy-start.34 = (bf16[256,512]{1,0:T(8,128)(2,1)S(1)}, bf16[256,512]{1,0:T(8,128)(2,1)}, u32[]{:S(2)}) copy-start(bf16[256,512]{1,0:T(8,128)(2,1)} %get-tuple-element.426) | copy-start | bytes 786436
  635.6 32.7 %collective-permute-start.31 = (bf16[2,2,2,64,512]{4,3,2,1,0:T(8,128)(2,1)}, bf16[2,2,2,64,512]{4,3,2,1,0:T(8,128)(2,1)S(1)}, u32[]{:S(2)}, u32[]{:S(2)}) collective-permute-start(bf16[2,2,2,64,512]{4,3,2,1,0:T(8,128)(2,1)} %bitcast.322), channel_id=1, source_target_pairs={{0,4},{2,6},{4,0},{6,2},{8,12},{10,14},{12,8},{14,10},{16,20},{18,... | collective-permute-start | bytes 1572872 | tf_op jit(solution)/shard_map/ppermute | solution.py:973
  636.4 18.3 %collective-permute-start.30 = (bf16[2,2,64,512]{3,2,1,0:T(8,128)(2,1)}, bf16[2,2,64,512]{3,2,1,0:T(8,128)(2,1)S(1)}, u32[]{:S(2)}, u32[]{:S(2)}) collective-permute-start(bf16[2,2,64,512]{3,2,1,0:T(8,128)(2,1)} %bitcast.328), channel_id=1, source_target_pairs={{0,4},{2,6},{4,0},{6,2},{8,12},{10,14},{12,8},{14,10},{16,20},{18,... | collective-permute-start | bytes 786440 | tf_op jit(solution)/shard_map/ppermute | solution.py:973
  637.7 30.6 %collective-permute-start.32 = (bf16[2,2,2,64,512]{4,3,2,1,0:T(8,128)(2,1)}, bf16[2,2,2,64,512]{4,3,2,1,0:T(8,128)(2,1)S(1)}, u32[]{:S(2)}, u32[]{:S(2)}) collective-permute-start(bf16[2,2,2,64,512]{4,3,2,1,0:T(8,128)(2,1)} %bitcast.321), channel_id=1, source_target_pairs={{0,1},{1,0},{2,3},{3,2},{4,5},{5,4},{6,7},{7,6},{8,9},{9,8},{10,11... | collective-permute-start | bytes 1572872 | tf_op jit(solution)/shard_map/ppermute | solution.py:973
  639.7 15.0 %copy-start.47 = (bf16[256,512]{1,0:T(8,128)(2,1)S(1)}, bf16[256,512]{1,0:T(8,128)(2,1)}, u32[]{:S(2)}) copy-start(bf16[256,512]{1,0:T(8,128)(2,1)} %get-tuple-element.379) | copy-start | bytes 786436
  639.7 4.3 collective-permute-start.27
  639.8 41.5 %collective-permute-start.26 = (bf16[896,512]{1,0:T(8,128)(2,1)}, bf16[896,512]{1,0:T(8,128)(2,1)S(1)}, u32[]{:S(2)}, u32[]{:S(2)}) collective-permute-start(bf16[896,512]{1,0:T(8,128)(2,1)} %get-tuple-element.370), channel_id=1, source_target_pairs={{0,1},{1,0},{2,3},{3,2},{4,5},{5,4},{6,7},{7,6},{8,9},{9,8},{10,11... | collective-permute-start | bytes 2752520 | tf_op jit(solution)/shard_map/ppermute | solution.py:973
  644.0 30.2 %collective-permute-start.39 = (bf16[4,64,512]{2,1,0:T(8,128)(2,1)S(1)}, bf16[4,64,512]{2,1,0:T(8,128)(2,1)S(1)}, u32[]{:S(2)}, u32[]{:S(2)}) collective-permute-start(bf16[4,64,512]{2,1,0:T(8,128)(2,1)S(1)} %bitcast.323), channel_id=1, source_target_pairs={{0,16},{2,18},{4,20},{6,22},{8,24},{10,26},{12,28},{14,30},{16,0},... | collective-permute-start | bytes 786440 | tf_op jit(solution)/shard_map/ppermute | solution.py:973
  654.6 12.9 %copy-start.30 = (bf16[2,2,64,512]{3,2,1,0:T(8,128)(2,1)}, bf16[2,2,64,512]{3,2,1,0:T(8,128)(2,1)S(1)}, u32[]{:S(2)}) copy-start(bf16[2,2,64,512]{3,2,1,0:T(8,128)(2,1)S(1)} %collective-permute-done.30) | copy-start | bytes 786436
  654.6 12.9 %collective-permute-start.29 = (bf16[2,2,64,512]{3,2,1,0:T(8,128)(2,1)S(1)}, bf16[2,2,64,512]{3,2,1,0:T(8,128)(2,1)S(1)}, u32[]{:S(2)}, u32[]{:S(2)}) collective-permute-start(bf16[2,2,64,512]{3,2,1,0:T(8,128)(2,1)S(1)} %bitcast.324), channel_id=1, source_target_pairs={{0,8},{2,10},{4,12},{6,14},{8,0},{10,2},{12,4},{14,6},{16,24},{18,... | collective-permute-start | bytes 786440 | tf_op jit(solution)/shard_map/ppermute | solution.py:973
  667.5 8.5 %collective-permute-start.28 = (f32[2,17,512]{2,1,0:T(8,128)S(1)}, f32[2,17,512]{2,1,0:T(8,128)S(1)}, u32[]{:S(2)}, u32[]{:S(2)}) collective-permute-start(f32[2,17,512]{2,1,0:T(8,128)S(1)} %add.74), channel_id=1, source_target_pairs={{0,4},{2,6},{4,0},{6,2},{8,12},{10,14},{12,8},{14,10},{16,20},{18,... | collective-permute-start | bytes 208904 | tf_op jit(solution)/shard_map/ppermute | solution.py:973
  672.7 7.5 %collective-permute-start.38 = (bf16[2,64,512]{2,1,0:T(8,128)(2,1)}, bf16[2,64,512]{2,1,0:T(8,128)(2,1)S(1)}, u32[]{:S(2)}, u32[]{:S(2)}) collective-permute-start(bf16[2,64,512]{2,1,0:T(8,128)(2,1)} %bitcast.335), channel_id=1, source_target_pairs={{0,16},{2,18},{4,20},{6,22},{8,24},{10,26},{12,28},{14,30},{16,0},... | collective-permute-start | bytes 393224 | tf_op jit(solution)/shard_map/ppermute | solution.py:973
  676.0 18.5 %collective-permute-start.41 = (f32[2,17,512]{2,1,0:T(8,128)S(1)}, f32[2,17,512]{2,1,0:T(8,128)S(1)}, u32[]{:S(2)}, u32[]{:S(2)}) collective-permute-start(f32[2,17,512]{2,1,0:T(8,128)S(1)} %add.81), channel_id=1, source_target_pairs={{0,8},{2,10},{4,12},{6,14},{8,0},{10,2},{12,4},{14,6},{16,24},{18,... | collective-permute-start | bytes 208904 | tf_op jit(solution)/shard_map/ppermute | solution.py:973
  676.6 11.1 %collective-permute-start.33 = (bf16[2,2,64,512]{3,2,1,0:T(8,128)(2,1)S(1)}, bf16[2,2,64,512]{3,2,1,0:T(8,128)(2,1)S(1)}, u32[]{:S(2)}, u32[]{:S(2)}) collective-permute-start(bf16[2,2,64,512]{3,2,1,0:T(8,128)(2,1)S(1)} %bitcast.329), channel_id=1, source_target_pairs={{0,8},{2,10},{4,12},{6,14},{8,0},{10,2},{12,4},{14,6},{16,24},{18,... | collective-permute-start | bytes 786440 | tf_op jit(solution)/shard_map/ppermute | solution.py:973
  678.1 13.5 %collective-permute-start.34 = (bf16[2,2,64,512]{3,2,1,0:T(8,128)(2,1)S(1)}, bf16[2,2,64,512]{3,2,1,0:T(8,128)(2,1)S(1)}, u32[]{:S(2)}, u32[]{:S(2)}) collective-permute-start(bf16[2,2,64,512]{3,2,1,0:T(8,128)(2,1)S(1)} %bitcast.327), channel_id=1, source_target_pairs={{0,8},{2,10},{4,12},{6,14},{8,0},{10,2},{12,4},{14,6},{16,24},{18,... | collective-permute-start | bytes 786440 | tf_op jit(solution)/shard_map/ppermute | solution.py:973
  680.2 15.2 %collective-permute-start.37 = (bf16[2,64,512]{2,1,0:T(8,128)(2,1)S(1)}, bf16[2,64,512]{2,1,0:T(8,128)(2,1)S(1)}, u32[]{:S(2)}, u32[]{:S(2)}) collective-permute-start(bf16[2,64,512]{2,1,0:T(8,128)(2,1)S(1)} %bitcast.332), channel_id=1, source_target_pairs={{0,1},{1,0},{2,3},{3,2},{4,5},{5,4},{6,7},{7,6},{8,9},{9,8},{10,11... | collective-permute-start | bytes 393224 | tf_op jit(solution)/shard_map/ppermute | solution.py:973
  683.9 11.5 %copy-start.35 = (bf16[128,512]{1,0:T(8,128)(2,1)S(1)}, bf16[128,512]{1,0:T(8,128)(2,1)}, u32[]{:S(2)}) copy-start(bf16[128,512]{1,0:T(8,128)(2,1)} %get-tuple-element.418) | copy-start | bytes 393220
  694.5 9.3 %copy-start.53 = (bf16[128,512]{1,0:T(8,128)(2,1)S(1)}, bf16[128,512]{1,0:T(8,128)(2,1)}, u32[]{:S(2)}) copy-start(bf16[128,512]{1,0:T(8,128)(2,1)} %get-tuple-element.416) | copy-start | bytes 393220
  694.5 18.1 %copy-start.37 = (bf16[128,512]{1,0:T(8,128)(2,1)S(1)}, bf16[128,512]{1,0:T(8,128)(2,1)}, u32[]{:S(2)}) copy-start(bf16[128,512]{1,0:T(8,128)(2,1)} %get-tuple-element.412) | copy-start | bytes 393220
  694.5 19.5 %copy-start.36 = (bf16[128,512]{1,0:T(8,128)(2,1)S(1)}, bf16[128,512]{1,0:T(8,128)(2,1)}, u32[]{:S(2)}) copy-start(bf16[128,512]{1,0:T(8,128)(2,1)} %get-tuple-element.415) | copy-start | bytes 393220
  694.5 6.1 collective-permute-start.42
  695.3 19.5 %copy-start.1 = (s32[4,448]{1,0:T(4,128)S(1)}, s32[4,448]{1,0:T(4,128)}, u32[]{:S(2)}) copy-start(s32[4,448]{1,0:T(4,128)} %param.16) | copy-start | bytes 21508
  700.6 5.7 collective-permute-start.43
  703.4 9.1 %collective-permute-start.35 = (bf16[2,64,512]{2,1,0:T(8,128)(2,1)S(1)}, bf16[2,64,512]{2,1,0:T(8,128)(2,1)S(1)}, u32[]{:S(2)}, u32[]{:S(2)}) collective-permute-start(bf16[2,64,512]{2,1,0:T(8,128)(2,1)S(1)} %bitcast.334), channel_id=1, source_target_pairs={{0,16},{2,18},{4,20},{6,22},{8,24},{10,26},{12,28},{14,30},{16,0},... | collective-permute-start | bytes 393224 | tf_op jit(solution)/shard_map/ppermute | solution.py:973
  703.8 10.2 %collective-permute-start.36 = (bf16[2,64,512]{2,1,0:T(8,128)(2,1)S(1)}, bf16[2,64,512]{2,1,0:T(8,128)(2,1)S(1)}, u32[]{:S(2)}, u32[]{:S(2)}) collective-permute-start(bf16[2,64,512]{2,1,0:T(8,128)(2,1)S(1)} %bitcast.333), channel_id=1, source_target_pairs={{0,16},{2,18},{4,20},{6,22},{8,24},{10,26},{12,28},{14,30},{16,0},... | collective-permute-start | bytes 393224 | tf_op jit(solution)/shard_map/ppermute | solution.py:973
  (37 other events, 123.5 us)
Sparse Core Ops, SparseCore 0:
  12.6 122.7 all-gather.4
  138.8 113.0 all-gather.6
